TPU v7x, 32 devices: a whole 2x2x4 slice. The times are simulated.
32 devices in a mesh: fsdp: 8 (over y, x, core), ulysses: 4 (over z).
Axes of the slice: x: 2, y: 2, z: 4, core: 2. Of those that a mesh axis runs over, the one named last changes fastest.
Arguments:
- layer_input: bfloat16 [24, 1024, 2048], P('fsdp', 'ulysses'), may hold values from -6 to 6
- cotangent: bfloat16 [24, 1024, 2048], P('fsdp', 'ulysses'), may hold values from -6 to 6
- positions: int32 [24, 1024], P('fsdp', 'ulysses'), may hold values from 0 to 4095
- block_ids: int32 [24, 1024], P('fsdp'), may hold values from 0 to 7, never falling along the last dimension, each value on 1 to 256 neighbouring positions
- skip_mask: int32 [24], P('fsdp'), may hold values 0 or 1
- attn_gain: bfloat16 [2048], P('fsdp'), may hold values from 0.5 to 1.5
- w_query: bfloat16 [2048, 2048], P('fsdp'), may hold values from -0.125 to 0.125
- w_key: bfloat16 [2048, 512], P('fsdp'), may hold values from -0.125 to 0.125
- w_value: bfloat16 [2048, 512], P('fsdp'), may hold values from -0.125 to 0.125
- w_out: bfloat16 [2048, 2048], P('fsdp'), may hold values from -1 to 1
- mlp_gain: bfloat16 [2048], P('fsdp'), may hold values from 0.5 to 1.5
- w_gate: bfloat16 [2048, 5632], P('fsdp'), may hold values from -0.125 to 0.125
- w_up: bfloat16 [2048, 5632], P('fsdp'), may hold values from -0.125 to 0.125
- w_down: bfloat16 [5632, 2048], P(None, 'fsdp'), may hold values from -0.078125 to 0.078125
Outputs:
- output: bfloat16 [24, 1024, 2048], P('fsdp', 'ulysses')
- grad_input: bfloat16 [24, 1024, 2048], P('fsdp', 'ulysses')
- grad_attn_gain: float32 [2048], P('fsdp')
- grad_w_query: float32 [2048, 2048], P('fsdp')
- grad_w_key: float32 [2048, 512], P('fsdp')
- grad_w_value: float32 [2048, 512], P('fsdp')
- grad_w_out: float32 [2048, 2048], P('fsdp')
- grad_mlp_gain: float32 [2048], P('fsdp')
- grad_w_gate: float32 [2048, 5632], P('fsdp')
- grad_w_up: float32 [2048, 5632], P('fsdp')
- grad_w_down: float32 [5632, 2048], P(None, 'fsdp')
Inputs may be any that keep to these rules, and one draw needn't show every extreme that they name: `block_ids`: within a sequence block numbers never fall, every number of 0 to 7 occurs, and a block has 1 to 256 tokens.
All inputs are finite; a program needn't handle non-finite values. No bound on the sum of `skip_mask` on one device may be relied on, other than what follows from the above.
Results may differ from a plain program's by a relative error of at most 0.022.
Values may be sent and summed in bfloat16 or wider, within the bound.
No kernel may reach another device: no remote copies, remote signals or barrier semaphores. Data moves between devices by JAX's collectives and lax.ppermute only.
A program may use at most 640 MiB of HBM per device.

v0:
```python
import math

import jax
import jax.numpy as jnp
from jax import lax
from jax.sharding import PartitionSpec as P

H = 16
KVH = 4
HD = 128


epsilon = 1e-05


def rotary_tables(token_positions, head_size):
    half_size = head_size // 2
    frequency = jnp.exp(
        jnp.arange(half_size, dtype=jnp.float32) * (-2.0 * math.log(10000.0) / head_size)
    )
    angles = token_positions.astype(jnp.float32)[..., None] * frequency
    cosine = jnp.concatenate([jnp.cos(angles), jnp.cos(angles)], -1)
    sine_table = jnp.concatenate([jnp.sin(angles), jnp.sin(angles)], -1)
    return (cosine, sine_table)


def rotate(values, cosine, sine_table):
    half_size = values.shape[-1] // 2
    turned = jnp.concatenate([-values[..., half_size:], values[..., :half_size]], -1)
    return values * cosine[..., None, :] + turned * sine_table[..., None, :]


def unrotate(gradients, cosine, sine_table):
    half_size = gradients.shape[-1] // 2
    scaled = gradients * sine_table[..., None, :]
    turned = jnp.concatenate([scaled[..., half_size:], -scaled[..., :half_size]], -1)
    return gradients * cosine[..., None, :] + turned


def on_device(
    layer_input,
    cotangent,
    positions,
    block_ids,
    skip_mask,
    attn_gain,
    w_query,
    w_key,
    w_value,
    w_out,
    mlp_gain,
    w_gate,
    w_up,
    w_down,
):
    seq_count, local_len, width = layer_input.shape
    row_total = seq_count * local_len
    fsdp_size = lax.axis_size("fsdp")
    ulysses_size = lax.axis_size("ulysses")
    repeat_count = max(1, ulysses_size // KVH)
    head_scale = 1.0 / math.sqrt(HD)
    query_width = H * HD
    pair_width = KVH * HD
    hidden_width = w_gate.shape[1]
    gain_one, query_full, key_full, value_full, out_full = (
        lax.all_gather(attn_gain, "fsdp", axis=0, tiled=True),
        lax.all_gather(w_query, "fsdp", axis=0, tiled=True),
        lax.all_gather(w_key, "fsdp", axis=0, tiled=True),
        lax.all_gather(w_value, "fsdp", axis=0, tiled=True),
        lax.all_gather(w_out, "fsdp", axis=0, tiled=True),
    )
    keep_rows = jnp.repeat((1 - skip_mask).astype(jnp.float32), local_len)[:, None]
    inputs_flat = layer_input.astype(jnp.float32).reshape(row_total, width)
    inv_one = lax.rsqrt(jnp.mean(inputs_flat * inputs_flat, -1, keepdims=True) + epsilon)
    unit_one = inputs_flat * inv_one
    normed_one = (unit_one * gain_one.astype(jnp.float32)).astype(jnp.bfloat16)
    query_pre = jnp.dot(normed_one, query_full, preferred_element_type=jnp.float32).reshape(
        seq_count, local_len, H, HD
    )
    key_pre = jnp.dot(normed_one, key_full, preferred_element_type=jnp.float32).reshape(
        seq_count, local_len, KVH, HD
    )
    value_pre = jnp.dot(normed_one, value_full, preferred_element_type=jnp.float32).reshape(
        seq_count, local_len, KVH, HD
    )
    cosine, sine_table = rotary_tables(positions, HD)
    query_sent = rotate(query_pre, cosine, sine_table).astype(jnp.bfloat16)
    key_sent = jnp.repeat(rotate(key_pre, cosine, sine_table), repeat_count, axis=2).astype(
        jnp.bfloat16
    )
    value_sent = jnp.repeat(value_pre, repeat_count, axis=2).astype(jnp.bfloat16)
    query_heads, key_heads, value_heads = (
        lax.all_to_all(query_sent, "ulysses", split_axis=2, concat_axis=1, tiled=True),
        lax.all_to_all(key_sent, "ulysses", split_axis=2, concat_axis=1, tiled=True),
        lax.all_to_all(value_sent, "ulysses", split_axis=2, concat_axis=1, tiled=True),
    )
    full_len = query_heads.shape[1]
    local_heads = query_heads.shape[2]
    local_slots = key_heads.shape[2]
    group_size = local_heads // local_slots

    def scores_for(query_seq, key_seq, block_row):
        grouped = query_seq.reshape(full_len, local_slots, group_size, HD)
        raw_scores = (
            jnp.einsum("qsgd,ksd->sgqk", grouped, key_seq, preferred_element_type=jnp.float32)
            * head_scale
        )
        allowed = block_row[None, :] <= block_row[:, None]
        return jnp.where(allowed, raw_scores, -1e30)

    def attend(record):
        query_seq, key_seq, value_seq, block_row = record
        scores = scores_for(query_seq, key_seq, block_row)
        largest = jnp.max(scores, -1, keepdims=True)
        exponent = jnp.exp(scores - largest)
        row_sums = jnp.sum(exponent, -1, keepdims=True)
        chances = (exponent / row_sums).astype(jnp.bfloat16)
        mixture = jnp.einsum(
            "sgqk,ksd->qsgd", chances, value_seq, preferred_element_type=jnp.float32
        )
        log_total = (largest + jnp.log(row_sums))[..., 0]
        return (mixture.reshape(full_len, local_heads, HD).astype(jnp.bfloat16), log_total)

    attn_heads, log_totals = lax.map(attend, (query_heads, key_heads, value_heads, block_ids))
    attended_tokens = lax.all_to_all(attn_heads, "ulysses", split_axis=1, concat_axis=2, tiled=True)
    attended = attended_tokens.reshape(row_total, query_width)
    branch_attn = jnp.dot(attended, out_full, preferred_element_type=jnp.float32)
    middle = inputs_flat + keep_rows * branch_attn
    inv_two = lax.rsqrt(jnp.mean(middle * middle, -1, keepdims=True) + epsilon)
    unit_two = middle * inv_two
    gain_piece = lax.all_gather(mlp_gain, "fsdp", axis=0, tiled=True)
    gate_piece = lax.all_gather(w_gate, "fsdp", axis=0, tiled=True)
    up_piece = lax.all_gather(w_up, "fsdp", axis=0, tiled=True)
    gain_float = gain_piece.astype(jnp.float32)
    normed_piece = (unit_two * gain_float).astype(jnp.bfloat16)
    gate_sum = jnp.dot(normed_piece, gate_piece, preferred_element_type=jnp.float32)
    up_sum = jnp.dot(normed_piece, up_piece, preferred_element_type=jnp.float32)
    sigmoid_gate = jax.nn.sigmoid(gate_sum)
    silu_gate = gate_sum * sigmoid_gate
    hidden = (silu_gate * up_sum).astype(jnp.bfloat16)
    branch_mlp = jnp.dot(
        hidden,
        lax.all_gather(w_down, "fsdp", axis=1, tiled=True),
        preferred_element_type=jnp.float32,
    )
    output = (middle + keep_rows * branch_mlp).astype(jnp.bfloat16).reshape(layer_input.shape)
    grad_out = cotangent.astype(jnp.float32).reshape(row_total, width)
    grad_mlp = (keep_rows * grad_out).astype(jnp.bfloat16)
    grad_hidden = jnp.einsum(
        "rc,fc->rf",
        grad_mlp,
        lax.all_gather(w_down, "fsdp", axis=1, tiled=True),
        preferred_element_type=jnp.float32,
    )
    grad_gate = (
        grad_hidden * up_sum * sigmoid_gate * (1.0 + gate_sum * (1.0 - sigmoid_gate))
    ).astype(jnp.bfloat16)
    grad_up = (grad_hidden * silu_gate).astype(jnp.bfloat16)
    stacked_in = jnp.stack([w_gate, w_up])
    shard_piece = lax.all_gather(stacked_in, "fsdp", axis=1, tiled=True)
    from_gate = jnp.einsum(
        "rf,cf->rc", grad_gate, shard_piece[0], preferred_element_type=jnp.float32
    )
    grad_normed_two = from_gate + jnp.einsum(
        "rf,cf->rc", grad_up, shard_piece[1], preferred_element_type=jnp.float32
    )
    grad_unit_two = grad_normed_two * gain_float
    grad_gain_two = jnp.sum(grad_normed_two * unit_two, 0)
    grad_middle = grad_out + inv_two * (
        grad_unit_two - unit_two * jnp.mean(grad_unit_two * unit_two, -1, keepdims=True)
    )
    grad_branch = (keep_rows * grad_middle).astype(jnp.bfloat16)
    grad_attended = jnp.einsum(
        "rd,cd->rc", grad_branch, out_full, preferred_element_type=jnp.float32
    )
    grad_attended = grad_attended.astype(jnp.bfloat16).reshape(seq_count, local_len, H, HD)
    grad_heads = lax.all_to_all(grad_attended, "ulysses", split_axis=2, concat_axis=1, tiled=True)

    def attend_back(record):
        query_seq, key_seq, value_seq, block_row, log_total, grad_seq = record
        scores = scores_for(query_seq, key_seq, block_row)
        chances = jnp.exp(scores - log_total[..., None])
        grouped = query_seq.reshape(full_len, local_slots, group_size, HD)
        grouped_grad = grad_seq.reshape(full_len, local_slots, group_size, HD)
        grad_chances = jnp.einsum(
            "qsgd,ksd->sgqk", grouped_grad, value_seq, preferred_element_type=jnp.float32
        )
        center = jnp.sum(chances * grad_chances, -1, keepdims=True)
        grad_scores = (chances * (grad_chances - center)).astype(jnp.bfloat16)
        grad_query = (
            jnp.einsum("sgqk,ksd->qsgd", grad_scores, key_seq, preferred_element_type=jnp.float32)
            * head_scale
        )
        grad_key = (
            jnp.einsum("sgqk,qsgd->ksd", grad_scores, grouped, preferred_element_type=jnp.float32)
            * head_scale
        )
        grad_value = jnp.einsum(
            "sgqk,qsgd->ksd",
            chances.astype(jnp.bfloat16),
            grouped_grad,
            preferred_element_type=jnp.float32,
        )
        return (
            grad_query.reshape(full_len, local_heads, HD).astype(jnp.bfloat16),
            grad_key.astype(jnp.bfloat16),
            grad_value.astype(jnp.bfloat16),
        )

    grad_query_heads, grad_key_heads, grad_value_heads = lax.map(
        attend_back, (query_heads, key_heads, value_heads, block_ids, log_totals, grad_heads)
    )
    grad_query_tok, grad_key_tok, grad_value_tok = (
        lax.all_to_all(grad_query_heads, "ulysses", split_axis=1, concat_axis=2, tiled=True),
        lax.all_to_all(grad_key_heads, "ulysses", split_axis=1, concat_axis=2, tiled=True),
        lax.all_to_all(grad_value_heads, "ulysses", split_axis=1, concat_axis=2, tiled=True),
    )
    grad_key_sum = (
        grad_key_tok.astype(jnp.float32).reshape(seq_count, local_len, KVH, repeat_count, HD).sum(3)
    )
    grad_value_sum = (
        grad_value_tok.astype(jnp.float32)
        .reshape(seq_count, local_len, KVH, repeat_count, HD)
        .sum(3)
    )
    grad_query_pre = (
        unrotate(grad_query_tok.astype(jnp.float32), cosine, sine_table)
        .astype(jnp.bfloat16)
        .reshape(row_total, query_width)
    )
    grad_key_pre = (
        unrotate(grad_key_sum, cosine, sine_table)
        .astype(jnp.bfloat16)
        .reshape(row_total, pair_width)
    )
    grad_value_pre = grad_value_sum.astype(jnp.bfloat16).reshape(row_total, pair_width)
    grad_normed_one = jnp.einsum(
        "rc,dc->rd", grad_query_pre, query_full, preferred_element_type=jnp.float32
    )
    grad_normed_one = grad_normed_one + jnp.einsum(
        "rc,dc->rd", grad_key_pre, key_full, preferred_element_type=jnp.float32
    )
    grad_normed_one = grad_normed_one + jnp.einsum(
        "rc,dc->rd", grad_value_pre, value_full, preferred_element_type=jnp.float32
    )
    grad_unit_one = grad_normed_one * gain_one.astype(jnp.float32)
    grad_gain_one = jnp.sum(grad_normed_one * unit_one, 0)
    grad_input = grad_middle + inv_one * (
        grad_unit_one - unit_one * jnp.mean(grad_unit_one * unit_one, -1, keepdims=True)
    )
    grad_input = grad_input.astype(jnp.bfloat16).reshape(layer_input.shape)
    gain_totals = lax.psum(jnp.stack([grad_gain_one, grad_gain_two]), ("fsdp", "ulysses"))
    owner_rows = width // fsdp_size
    gain_shard = lax.dynamic_slice_in_dim(
        gain_totals, lax.axis_index("fsdp") * owner_rows, owner_rows, 1
    )
    grad_attn_mid = jnp.concatenate([grad_query_pre, grad_key_pre, grad_value_pre], 1)
    grad_mlp_mid = jnp.concatenate([grad_gate, grad_up], 1)
    owner_sums = lax.psum_scatter(
        jnp.concatenate(
            [
                jnp.einsum(
                    "rc,re->ce", normed_one, grad_attn_mid, preferred_element_type=jnp.float32
                ),
                jnp.einsum("rc,re->ce", attended, grad_branch, preferred_element_type=jnp.float32),
                jnp.einsum(
                    "rc,re->ce", normed_piece, grad_mlp_mid, preferred_element_type=jnp.float32
                ),
                jnp.einsum("rc,re->ce", grad_mlp, hidden, preferred_element_type=jnp.float32),
            ],
            1,
        ).astype(jnp.bfloat16),
        "fsdp",
        scatter_dimension=0,
        tiled=True,
    ).astype(jnp.float32)
    owner_sums = lax.psum(owner_sums.astype(jnp.bfloat16), "ulysses").astype(jnp.float32)
    first_value = query_width + pair_width
    first_out = first_value + pair_width
    first_gate = first_out + width
    first_up = first_gate + hidden_width
    first_down = first_up + hidden_width
    return (
        output,
        grad_input,
        gain_shard[0],
        owner_sums[:, :query_width],
        owner_sums[:, query_width:first_value],
        owner_sums[:, first_value:first_out],
        owner_sums[:, first_out:first_gate],
        gain_shard[1],
        owner_sums[:, first_gate:first_up],
        owner_sums[:, first_up:first_down],
        owner_sums[:, first_down : first_down + hidden_width].T,
    )


def solution(mesh):
    return jax.shard_map(
        on_device,
        mesh=mesh,
        in_specs=(
            P("fsdp", "ulysses", None),
            P("fsdp", "ulysses", None),
            P("fsdp", "ulysses"),
            P("fsdp", None),
            P("fsdp"),
            P("fsdp"),
            P("fsdp", None),
            P("fsdp", None),
            P("fsdp", None),
            P("fsdp", None),
            P("fsdp"),
            P("fsdp", None),
            P("fsdp", None),
            P(None, "fsdp"),
        ),
        out_specs=(
            P("fsdp", "ulysses", None),
            P("fsdp", "ulysses", None),
            P("fsdp"),
            P("fsdp", None),
            P("fsdp", None),
            P("fsdp", None),
            P("fsdp", None),
            P("fsdp"),
            P("fsdp", None),
            P("fsdp", None),
            P(None, "fsdp"),
        ),
        check_vma=False,
    )
```

profile of v0, /device:TPU:0, one launch (start us, length us, event | category | flops | bytes accessed | tf_op | source)
XLA Modules:
  0.0 2315.6 jit_solution(7480973175895499666)
XLA Ops:
  12.0 5.9 pad_maximum_fusion.2
  17.9 10.4 all-gather
  30.5 10.0 all-gather.11.cloned.1.call-done
  55.5 14.9 all-gather.13.cloned.1.call-done
  79.3 47.4 %all-gather.15.cloned.1.call-done = bf16[2048,2048]{1,0:T(8,128)(2,1)} async-done(((bf16[256,2048]{1,0:T(8,128)(2,1)}), bf16[2048,2048]{1,0:T(8,128)(2,1)}) %all-gather.15.cloned.1.call-update) | async-done | bytes 8388624 | tf_op jit(solution)/shard_map/all_gather | solution.py:67
  126.7 12.4 copy.162
  143.6 9.3 fusion.102
  157.8 6.5 all-to-all-done.1
  172.7 66.7 %all-to-all-done.2 = bf16[3,256,16,128]{1,3,0,2:T(8,128)(2,1)} async-done(((bf16[3,256,16,128]{1,3,0,2:T(8,128)(2,1)}), bf16[3,256,16,128]{1,3,0,2:T(8,128)(2,1)}, u32[]{:S(2)}, u32[]{:S(2)}) %all-to-all-start.2) | async-done | bytes 3145760 | tf_op jit(solution)/shard_map/all_to_all | solution.py:93
  246.5 55.1 %while.26 = (s32[]{:T(128)}, bf16[3,1024,4,128]{3,2,0,1:T(4,128)(2,1)}, f32[3,1,4,1024]{3,2,1,0:T(4,128)}, bf16[3,1024,1,128]{3,1,0,2:T(8,128)(2,1)}, s32[3,1024...) while((s32[]{:T(128)}, ...), condition=%wide.region_4.5_spmd, body=%wide.region_1.4_spmd.sunk | while | flops 2199384064 | bytes 61486188 | solution.py:124
  255.8 6.4 fusion.174
  274.2 6.4 fusion.174
  292.5 6.4 fusion.174
  306.6 8.8 all-gather.1
  319.7 57.0 %all-to-all-done.3 = bf16[3,1024,4,128]{3,2,0,1:T(4,128)(2,1)} async-done(((bf16[3,1024,4,128]{3,2,0,1:T(4,128)(2,1)}), bf16[3,1024,4,128]{3,2,0,1:T(4,128)(2,1)}, u32[]{:S(2)}, u32[]{:S(2)}) %all-to-all-start.3) | async-done | bytes 3145760 | tf_op jit(solution)/shard_map/all_to_all | solution.py:125
  381.4 6.5 reshape.302
  388.0 10.4 multiply_reduce_fusion.2
  401.7 26.0 %fusion.115 = f32[768,5632]{1,0:T(8,128)} fusion(bf16[768,2048]{1,0:T(8,128)(2,1)S(1)} %multiply_convert_fusion.5, bf16[2048,5632]{1,0:T(8,128)(2,1)} %all-gather.21.cloned.1.call-done), kind=kOutput, calls=%fused_computation.174 | convolution fusion | flops 17716740096 | bytes 43515904 | tf_op jit(solution)/shard_map/dot_general | solution.py:137
  427.7 25.9 %fusion.116 = f32[768,5632]{1,0:T(8,128)} fusion(bf16[768,2048]{1,0:T(8,128)(2,1)} %fusion.73, bf16[5632,2048]{1,0:T(8,128)(2,1)} %all-gather.23.cloned.1.call-done), kind=kOutput, calls=%fused_computation.175 | convolution fusion | flops 17716740096 | bytes 43515904 | tf_op jit(solution)/shard_map/rc,fc->rf/dot_general | solution.py:149
  453.6 88.6 %all-gather.19.cloned.1.call-done = bf16[2048,5632]{1,0:T(8,128)(2,1)} async-done(((bf16[256,5632]{1,0:T(8,128)(2,1)}), bf16[2048,5632]{1,0:T(8,128)(2,1)}) %all-gather.19.cloned.1.call-update) | async-done | bytes 23068688 | tf_op jit(solution)/shard_map/all_gather | solution.py:132
  542.2 40.5 %multiply_convert_fusion.2 = (bf16[768,5632]{1,0:T(8,128)(2,1)}, bf16[768,5632]{1,0:T(8,128)(2,1)}, bf16[768,5632]{1,0:T(8,128)(2,1)}) fusion(f32[768,5632]{1,0:T(8,128)} %fusion.116, f32[768,5632]{1,0:T(8,128)} %fusion.115, bf16[768,2048]{1,0:T(8,128)(2,1)S(1)} %multiply_convert_fusion.5, bf16[2048,5632]{1,0:T(8,128)(2,1)} %all-gather.19.cloned.1.call-done), kind=kOutput, calls=%fused_computation.82 | convolution fusion | flops 17781620736 | bytes 86769664 | tf_op jit(solution)/shard_map/dot_general | solution.py:136
  582.7 176.1 %all-gather.25.cloned.1.call-done = bf16[2,2048,5632]{2,1,0:T(8,128)(2,1)} async-done(((bf16[2,256,5632]{2,1,0:T(8,128)(2,1)}), bf16[2,2048,5632]{2,1,0:T(8,128)(2,1)}) %all-gather.25.cloned.1.call-update) | async-done | bytes 46137360 | tf_op jit(solution)/shard_map/all_gather | solution.py:160
  758.8 25.1 %fusion.67 = f32[768,2048]{1,0:T(8,128)} fusion(bf16[768,5632]{1,0:T(8,128)(2,1)} %get-tuple-element.291, bf16[2,2048,5632]{2,1,0:T(8,128)(2,1)} %all-gather.25.cloned.1.call-done), kind=kOutput, calls=%fused_computation.74 | convolution fusion | flops 17716740096 | bytes 38010880 | tf_op jit(solution)/shard_map/rf,cf->rc/dot_general | solution.py:164
  784.0 27.1 %multiply_reduce_fusion = (f32[2048]{0:T(1024)}, f32[768]{0:T(1024)S(1)}, f32[768,2048]{1,0:T(8,128)}) fusion(f32[768,2048]{1,0:T(8,128)S(1)} %copy-done.8, f32[768]{0:T(1024)S(1)} %copy-done.31, f32[2048]{0:T(1024)S(1)} %bitcast.438, f32[768,2048]{1,0:T(8,128)} %fusion.67, bf16[768,5632]{1,0:T(8,128)(2,1)} %get-tuple-element.290, ...), kind=kOutput, calls=%fused_computation.117 | convolution fusion | flops 17727748096 | bytes 50616320 | tf_op jit(solution)/shard_map/rf,cf->rc/dot_general | solution.py:161
  815.7 11.4 fusion.98
  835.2 71.1 %all-to-all-done.4 = bf16[3,256,16,128]{3,1,0,2:T(8,128)(2,1)S(1)} async-done(((bf16[3,256,16,128]{3,1,0,2:T(8,128)(2,1)}), bf16[3,256,16,128]{3,1,0,2:T(8,128)(2,1)S(1)}, u32[]{:S(2)}, u32[]{:S(2)}) %all-to-all-start.4) | async-done | bytes 3145760 | tf_op jit(solution)/shard_map/all_to_all | solution.py:177
  912.5 179.7 %while.27 = (s32[]{:T(128)}, bf16[3,1024,4,128]{3,2,0,1:T(4,128)(2,1)}, bf16[3,1024,1,128]{1,3,2,0:T(8,128)(2,1)}, bf16[3,1024,1,128]{1,3,2,0:T(8,128)(2,1)}, bf...) while((s32[]{:T(128)}, ...), condition=%wide.region_9.10_spmd, body=%wide.region_7.9_spmd.sunk | while | flops 5408944128 | bytes 264601872 | solution.py:210
  912.9 9.3 fusion.183
  924.9 9.6 fusion.184
  934.5 13.6 fusion.185
  955.9 7.5 fusion.187
  963.4 9.3 fusion.188
  972.7 9.2 fusion.183
  984.6 9.6 fusion.184
  994.2 13.6 fusion.185
  1015.6 7.5 fusion.187
  1023.0 9.3 fusion.188
  1032.4 9.2 fusion.183
  1044.3 9.6 fusion.184
  1053.9 13.6 fusion.185
  1075.3 7.5 fusion.187
  1082.7 9.3 fusion.188
  1102.9 20.4 all-to-all-done.7
  1126.9 44.9 %convolution_convert_fusion = bf16[2048,11264]{1,0:T(8,128)(2,1)} fusion(bf16[768,2048]{1,0:T(8,128)(2,1)} %copy-done.22, bf16[768,5632]{1,0:T(8,128)(2,1)} %get-tuple-element.291, bf16[768,5632]{1,0:T(8,128)(2,1)} %get-tuple-element.290), kind=kOutput, calls=%fused_computation.72 | convolution fusion | flops 35491151872 | bytes 66584576 | tf_op jit(solution)/shard_map/rc,re->ce/dot_general | solution.py:266
  1172.8 5.0 all-to-all-start.5
  1177.8 26.2 %convolution_convert_fusion.1 = bf16[2048,5632]{1,0:T(8,128)(2,1)} fusion(bf16[768,2048]{1,0:T(8,128)(2,1)} %fusion.73, bf16[768,5632]{1,0:T(8,128)(2,1)} %get-tuple-element.292), kind=kOutput, calls=%fused_computation.77 | convolution fusion | flops 17728274432 | bytes 34865152 | tf_op jit(solution)/shard_map/rc,re->ce/dot_general | solution.py:269
  1204.0 12.4 convolution_convert_fusion.3
  1216.4 12.3 copy.187
  1262.7 7.7 copy.176
  1277.6 6.7 copy.177
  1284.3 8.1 reshape.310
  1295.6 10.2 fusion.74
  1305.9 10.9 fusion.117
  1316.9 5.3 fusion.86
  1322.2 5.1 fusion.87
  1327.3 13.3 convolution_convert_fusion.2
  1340.6 59.2 %pad_maximum_fusion = bf16[2048,22016]{1,0:T(8,128)(2,1)} fusion(bf16[2048,5632]{1,0:T(8,128)(2,1)} %convolution_convert_fusion.1, bf16[2048,11264]{1,0:T(8,128)(2,1)} %convolution_convert_fusion, bf16[2048,2048]{1,0:T(8,128)(2,1)} %copy.187, bf16[2048,3072]{1,0:T(8,128)(2,1)} %convolution_convert_fusion.2), kind=kLoop, calls=%fused_computation.71 | loop fusion | flops 360710144 | bytes 180355072 | tf_op jit(solution)/shard_map/concatenate | solution.py:260
  1400.0 490.8 %reduce-scatter.4.cloned.1.call-done = bf16[256,22016]{1,0:T(8,128)(2,1)} async-done(((bf16[2048,22016]{1,0:T(8,128)(2,1)}), bf16[256,22016]{1,0:T(8,128)(2,1)}) %reduce-scatter.4.cloned.1.call-update) | async-done | bytes 11272208
  1890.8 25.1 %add_convert_fusion = bf16[768,2048]{1,0:T(8,128)(2,1)} fusion(f32[768,2048]{1,0:T(8,128)} %copy-done.7, bf16[768,5632]{1,0:T(8,128)(2,1)} %get-tuple-element.292, bf16[5632,2048]{1,0:T(8,128)(2,1)} %all-gather.23.cloned.1.call-done, f32[768]{0:T(1024)S(1)} %copy-done.38), kind=kOutput, calls=%fused_computation.121 | convolution fusion | flops 17721458688 | bytes 41159680 | tf_op jit(solution)/shard_map/dot_general | solution.py:141
  1915.8 44.6 %psum.14 = f32[2,2048]{1,0:T(2,128)S(1)} all-reduce(f32[2,2048]{1,0:T(2,128)S(1)} %pad_maximum_fusion.6), channel_id=1, replica_groups=mesh['fsdp'=8,'ulysses'=4] {'fsdp','ulysses'}, use_global_device_ids=true, to_apply=%region_13.14 | all-reduce | flops 4096 | bytes 32768 | tf_op jit(solution)/shard_map/psum | solution.py:252
  1961.1 316.9 %all-reduce.3.cloned.1.call-done = bf16[256,22016]{1,0:T(8,128)(2,1)} async-done(((bf16[256,22016]{1,0:T(8,128)(2,1)}), bf16[256,22016]{1,0:T(8,128)(2,1)}) %all-reduce.3.cloned.1.call-update) | async-done | bytes 11272208 | tf_op jit(solution)/shard_map/psum | solution.py:277
  2277.9 6.6 convert_element_type.232
  2287.5 6.2 copy.188
  2299.9 8.6 fusion.109
  (251 shorter events, 228.4 us)
Async XLA Ops:
  7.2 33.4 %all-gather.11.cloned.1.call-start = ((), (), s32[]{:S(2)}) async-start(), calls=%async_computation.9 | async-start | bytes 2359296 | tf_op jit(solution)/shard_map/all_gather | solution.py:69
  7.9 62.5 %all-gather.13.cloned.1.call-start = ((), (), s32[]{:S(2)}) async-start(), calls=%async_computation.10 | async-start | bytes 2359296 | tf_op jit(solution)/shard_map/all_gather | solution.py:68
  8.7 118.0 %all-gather.15.cloned.1.call-start = ((), (), s32[]{:S(2)}) async-start(), calls=%async_computation.11 | async-start | bytes 9437184 | tf_op jit(solution)/shard_map/all_gather | solution.py:67
  9.4 378.6 %all-gather.17.cloned.1.call-start = ((), (), s32[]{:S(2)}) async-start(), calls=%async_computation.12 | async-start | bytes 9437184 | tf_op jit(solution)/shard_map/all_gather | solution.py:70
  10.0 391.7 %all-gather.21.cloned.1.call-start = ((), (), s32[]{:S(2)}) async-start(), calls=%async_computation.14 | async-start | bytes 25952256 | tf_op jit(solution)/shard_map/all_gather | solution.py:133
  10.6 417.1 %all-gather.23.cloned.1.call-start = ((), (), s32[]{:S(2)}) async-start(), calls=%async_computation.15 | async-start | bytes 25952256 | tf_op jit(solution)/shard_map/all_gather | solution.py:143
  11.1 531.1 %all-gather.19.cloned.1.call-start = ((), (), s32[]{:S(2)}) async-start(), calls=%async_computation.13 | async-start | bytes 25952256 | tf_op jit(solution)/shard_map/all_gather | solution.py:132
  11.9 747.0 %all-gather.25.cloned.1.call-start = ((), (), s32[]{:S(2)}) async-start(), calls=%async_computation.16 | async-start | bytes 51904512 | tf_op jit(solution)/shard_map/all_gather | solution.py:160
  11.9 5.9 copy-start.41
  11.9 16.3 copy-start.40
  12.0 16.4 copy-start.4
  28.3 115.3 %copy-start.26 = (f32[8,1,256]{2,1,0:T(1,128)}, f32[8,1,256]{2,1,0:T(1,128)S(1)}, u32[]{:S(2)}) copy-start(f32[8,1,256]{2,1,0:T(1,128)S(1)} %convert_element_type.245) | copy-start | bytes 24580
  29.0 114.6 %copy-start.33 = (f32[3,256]{1,0:T(4,128)}, f32[3,256]{1,0:T(4,128)S(1)}, u32[]{:S(2)}) copy-start(f32[3,256]{1,0:T(4,128)S(1)} %add_rsqrt_fusion.1) | copy-start | bytes 9220
  48.8 90.2 %all-to-all-start = ((bf16[3,256,4,128]{3,1,0,2:T(8,128)(2,1)}), bf16[3,256,4,128]{3,1,0,2:T(8,128)(2,1)}, u32[]{:S(2)}, u32[]{:S(2)}) async-start(bf16[3,256,4,128]{3,1,0,2:T(8,128)(2,1)} %copy.157), calls=%async_computation | async-start | bytes 1572864 | tf_op jit(solution)/shard_map/all_to_all | solution.py:95
  55.5 98.4 %copy-start.12 = (f32[3,256,128]{1,2,0:T(8,128)}, f32[3,256,128]{1,2,0:T(8,128)S(1)}, u32[]{:S(2)}) copy-start(f32[3,256,128]{1,2,0:T(8,128)S(1)} %get-tuple-element.318) | copy-start | bytes 1179652
  74.3 3.7 copy-start.17
  139.1 25.2 %all-to-all-start.1 = ((bf16[3,256,4,128]{1,3,0,2:T(8,128)(2,1)}), bf16[3,256,4,128]{1,3,0,2:T(8,128)(2,1)}, u32[]{:S(2)}, u32[]{:S(2)}) async-start(bf16[3,256,4,128]{1,3,0,2:T(8,128)(2,1)} %copy.160), calls=%async_computation.1 | async-start | bytes 1572864 | tf_op jit(solution)/shard_map/all_to_all | solution.py:94
  164.3 75.2 %all-to-all-start.2 = ((bf16[3,256,16,128]{1,3,0,2:T(8,128)(2,1)}), bf16[3,256,16,128]{1,3,0,2:T(8,128)(2,1)}, u32[]{:S(2)}, u32[]{:S(2)}) async-start(bf16[3,256,16,128]{1,3,0,2:T(8,128)(2,1)} %copy.163), calls=%async_computation.2 | async-start | bytes 6291456 | tf_op jit(solution)/shard_map/all_to_all | solution.py:93
  301.6 18.0 copy-start.10
  301.6 4.8 copy-start.42
  301.6 4.9 copy-start.43
  301.7 75.0 %all-to-all-start.3 = ((bf16[3,1024,4,128]{3,2,0,1:T(4,128)(2,1)}), bf16[3,1024,4,128]{3,2,0,1:T(4,128)(2,1)}, u32[]{:S(2)}, u32[]{:S(2)}) async-start(bf16[3,1024,4,128]{3,2,0,1:T(4,128)(2,1)} %get-tuple-element.103), calls=%async_computation.3 | async-start | bytes 6291456 | tf_op jit(solution)/shard_map/all_to_all | solution.py:125
  306.5 81.4 %copy-start.35 = (f32[768]{0:T(1024)}, f32[768]{0:T(1024)S(1)}, u32[]{:S(2)}) copy-start(f32[768]{0:T(1024)S(1)} %mul.276) | copy-start | bytes 9220
  315.4 83.0 %copy-start.28 = (f32[8,1,256]{2,1,0:T(1,128)}, f32[8,1,256]{2,1,0:T(1,128)S(1)}, u32[]{:S(2)}) copy-start(f32[8,1,256]{2,1,0:T(1,128)S(1)} %convert_element_type.246) | copy-start | bytes 24580
  376.7 11.3 copy-start.5
  401.7 140.5 %copy-start.22 = (bf16[768,2048]{1,0:T(8,128)(2,1)}, bf16[768,2048]{1,0:T(8,128)(2,1)S(1)}, u32[]{:S(2)}) copy-start(bf16[768,2048]{1,0:T(8,128)(2,1)S(1)} %multiply_convert_fusion.5) | copy-start | bytes 9437188
  758.8 25.2 %copy-start.8 = (f32[768,2048]{1,0:T(8,128)S(1)}, f32[768,2048]{1,0:T(8,128)}, u32[]{:S(2)}) copy-start(f32[768,2048]{1,0:T(8,128)} %copy-done.7) | copy-start | bytes 18874372
  758.8 25.2 %copy-start.29 = (f32[8,1,256]{2,1,0:T(1,128)S(1)}, f32[8,1,256]{2,1,0:T(1,128)}, u32[]{:S(2)}) copy-start(f32[8,1,256]{2,1,0:T(1,128)} %copy-done.28) | copy-start | bytes 24580
  758.8 25.2 %copy-start.31 = (f32[768]{0:T(1024)S(1)}, f32[768]{0:T(1024)}, u32[]{:S(2)}) copy-start(f32[768]{0:T(1024)} %copy-done.30) | copy-start | bytes 9220
  811.1 4.6 copy-start.36
  815.7 11.4 copy-start.9
  830.6 75.7 %all-to-all-start.4 = ((bf16[3,256,16,128]{3,1,0,2:T(8,128)(2,1)}), bf16[3,256,16,128]{3,1,0,2:T(8,128)(2,1)S(1)}, u32[]{:S(2)}, u32[]{:S(2)}) async-start(bf16[3,256,16,128]{3,1,0,2:T(8,128)(2,1)} %copy.169), calls=%async_computation.4 | async-start | bytes 6291456 | tf_op jit(solution)/shard_map/all_to_all | solution.py:177
  912.5 185.6 %copy-start.34 = (f32[3,256]{1,0:T(4,128)S(1)}, f32[3,256]{1,0:T(4,128)}, u32[]{:S(2)}) copy-start(f32[3,256]{1,0:T(4,128)} %copy-done.33) | copy-start | bytes 9220
  912.9 9.3 copy-start.2
  934.5 13.6 copy-start
  948.1 3.3 copy-start.1
  955.9 7.5 copy-start.3
  972.7 9.2 copy-start.2
  994.2 13.6 copy-start
  1015.6 7.5 copy-start.3
  1032.4 9.2 copy-start.2
  1053.9 13.6 copy-start
  1075.3 7.5 copy-start.3
  1094.6 28.8 %all-to-all-start.7 = ((bf16[3,1024,1,128]{3,0,2,1:T(4,128)(2,1)}), bf16[3,1024,1,128]{3,0,2,1:T(4,128)(2,1)S(1)}, u32[]{:S(2)}, u32[]{:S(2)}) async-start(bf16[3,1024,1,128]{3,0,2,1:T(4,128)(2,1)} %copy.184), calls=%async_computation.7 | async-start | bytes 2097152 | tf_op jit(solution)/shard_map/all_to_all | solution.py:216
  1123.4 48.4 %copy-start.19 = (bf16[3,1024,1,128]{3,0,2,1:T(4,128)(2,1)}, bf16[3,1024,1,128]{3,0,2,1:T(4,128)(2,1)S(1)}, u32[]{:S(2)}) copy-start(bf16[3,1024,1,128]{3,0,2,1:T(4,128)(2,1)S(1)} %all-to-all-done.7) | copy-start | bytes 2359300
  1123.4 48.4 %all-to-all-start.6 = ((bf16[3,1024,1,128]{3,0,2,1:T(4,128)(2,1)}), bf16[3,1024,1,128]{3,0,2,1:T(4,128)(2,1)S(1)}, u32[]{:S(2)}, u32[]{:S(2)}) async-start(bf16[3,1024,1,128]{3,0,2,1:T(4,128)(2,1)} %copy.178), calls=%async_computation.6 | async-start | bytes 2097152 | tf_op jit(solution)/shard_map/all_to_all | solution.py:215
  1172.8 82.8 %all-to-all-start.5 = ((bf16[3,1024,4,128]{3,2,0,1:T(4,128)(2,1)}), bf16[3,1024,4,128]{3,2,0,1:T(4,128)(2,1)S(1)}, u32[]{:S(2)}, u32[]{:S(2)}) async-start(bf16[3,1024,4,128]{3,2,0,1:T(4,128)(2,1)} %get-tuple-element.105), calls=%async_computation.5 | async-start | bytes 6291456 | tf_op jit(solution)/shard_map/all_to_all | solution.py:214
  1177.8 712.9 %reduce-scatter.4.cloned.1.call-start = ((), (), s32[]{:S(2)}) async-start(), calls=%async_computation.18 | async-start | bytes 101449728
  1177.8 26.2 %copy-start.37 = (f32[768]{0:T(1024)S(1)}, f32[768]{0:T(1024)}, u32[]{:S(2)}) copy-start(f32[768]{0:T(1024)} %copy-done.35) | copy-start | bytes 9220
  1228.7 7.7 copy-start.13
  1244.4 6.8 copy-start.15
  1284.3 8.1 copy-start.21
  1295.6 21.3 slice-start
  1305.8 11.0 copy-start.6
  1305.8 11.0 slice-start.1
  1305.8 11.0 copy-start.14
  1305.8 11.0 copy-start.16
  1305.8 11.0 copy-start.27
  1305.9 11.0 copy-start.32
  1322.1 5.1 copy-start.24
  1322.2 5.1 copy-start.25
  1399.9 490.9 %copy-start.38 = (f32[768]{0:T(1024)S(1)}, f32[768]{0:T(1024)}, u32[]{:S(2)}) copy-start(f32[768]{0:T(1024)} %copy-done.35) | copy-start | bytes 9220
  1399.9 878.0 %all-reduce.3.cloned.1.call-start = ((), (), s32[]{:S(2)}) async-start(), calls=%async_computation.17 | async-start | bytes 22544384 | tf_op jit(solution)/shard_map/psum | solution.py:277
  1890.8 25.1 %copy-start.39 = (f32[2048]{0:T(1024)S(1)}, f32[2048]{0:T(1024)}, u32[]{:S(2)}) copy-start(f32[2048]{0:T(1024)} %get-tuple-element.248) | copy-start | bytes 24580
  (8 other events, 16.5 us)
Sparse Core Ops, SparseCore 0:
  9.9 30.6 all-gather.10
  42.4 27.8 all-gather.12
  72.3 54.3 all-gather.14
  128.4 54.3 all-gather.16
  184.6 116.4 all-gather.20
  302.8 120.9 all-gather.22
  425.7 116.4 all-gather.18
  544.7 214.1 all-gather.24
  1400.0 490.6 reduce-scatter.3
  1893.1 384.8 all-reduce.2
where the time goes:
time: 2330 us; the launch traced here: 2320 us
  waiting for transfers between devices  1370 us (59%)
  matrix products  471 us (20%)
  other arithmetic  181 us (8%)
  local copies, waits for them, and re-layouts  178 us (8%)
  blocking collectives  63.8 us (3%)
  starting transfers between devices  35.8 us (2%)
    unnamed x11, waiting for transfers between devices  495 us
    psum x1, waiting for transfers between devices, on_device(): lax.psum(owner_sums.astype(jnp.bfloat16), 'ulysses').astype(jnp.float32)  317 us
    all_gather x1, waiting for transfers between devices, on_device(): shard_piece = lax.all_gather(stacked_in, 'fsdp', axis=1, tiled=True)  176 us
    all_gather x1, waiting for transfers between devices, on_device(): gate_piece = lax.all_gather(w_gate, 'fsdp', axis=0, tiled=True)  88.6 us
    all_to_all x1, waiting for transfers between devices, on_device(): lax.all_to_all(grad_attended, 'ulysses', split_axis=2, concat_axis=1, til...  71.1 us
    all_to_all x1, waiting for transfers between devices, on_device(): lax.all_to_all(query_sent, 'ulysses', split_axis=2, concat_axis=1, tiled=...  66.7 us
    concatenate x1, other arithmetic, on_device(): jnp.concatenate([jnp.einsum('rc,re->ce', normed_one, grad_attn_mid, prefe...  59.2 us
    all_to_all x1, waiting for transfers between devices, on_device(): lax.all_to_all(attn_heads, 'ulysses', split_axis=1, concat_axis=2, tiled=...  57 us
  transfers between devices with their start and end apart: 18, of which 12 were waited for; matrix products, arithmetic and copies ran while one was open for 17% of the time, Pallas kernels for 0%

commit v1 on v0

v1 whole, which is shorter than its diff:
```python
import math

import jax
import jax.numpy as jnp
from jax import lax
from jax.experimental import pallas as pl
from jax.experimental.pallas import tpu as pltpu
from jax.sharding import PartitionSpec as P

H = 16
KVH = 4
HD = 128
GROUP = H // KVH
BLOCK = 256
EPS = 1e-05
F32 = jnp.float32
BF16 = jnp.bfloat16
LOG2E = math.log2(math.e)

NT = (((1,), (1,)), ((), ()))
NN = (((1,), (0,)), ((), ()))


def dot(a, b, dims=NN):
    return lax.dot_general(a, b, dims, preferred_element_type=F32)


def cost(flops, nbytes, trans=0):
    return pl.CostEstimate(flops=int(flops), bytes_accessed=int(nbytes), transcendentals=int(trans))


def const_spec(shape):
    zeros = (0,) * len(shape)
    return pl.BlockSpec(shape, lambda *_: zeros)


def sds(shape, dtype):
    return jax.ShapeDtypeStruct(shape, dtype)


def project(normed, weights, cosine, sine):
    rows, width = normed.shape
    tile = KVH * HD
    steps = weights.shape[1] // tile
    q_steps = H * HD // tile

    def body(x_ref, w_ref, c_ref, s_ref, q_ref, kv_ref):
        j = pl.program_id(0)
        y = dot(x_ref[...], w_ref[...])

        def turned():
            c, s = c_ref[...], s_ref[...]
            parts = []
            for h in range(KVH):
                v = y[:, h * HD : (h + 1) * HD]
                parts.append(v * c + pltpu.roll(v, HD // 2, 1) * s)
            return jnp.concatenate(parts, 1).astype(BF16)

        @pl.when(j < q_steps)
        def _():
            q_ref[...] = turned()

        @pl.when(j == q_steps)
        def _():
            kv_ref[...] = turned()

        @pl.when(j > q_steps)
        def _():
            kv_ref[...] = y.astype(BF16)

    return pl.pallas_call(
        body,
        grid=(steps,),
        in_specs=[
            const_spec((rows, width)),
            pl.BlockSpec((width, tile), lambda j: (0, j)),
            const_spec((rows, HD)),
            const_spec((rows, HD)),
        ],
        out_specs=[
            pl.BlockSpec((rows, tile), lambda j: (0, jnp.minimum(j, q_steps - 1))),
            pl.BlockSpec((rows, tile), lambda j: (0, jnp.maximum(j - q_steps, 0))),
        ],
        out_shape=[sds((rows, H * HD), BF16), sds((rows, 2 * KVH * HD), BF16)],
        cost_estimate=cost(2 * rows * width * steps * tile, 2 * (width * steps * tile + 2 * rows * width)),
        name="project",
    )(normed, weights, cosine, sine)


def slot_specs(count, local, shift):
    return [pl.BlockSpec((local, HD), lambda s, j: (s, shift + j)) for _ in range(count)]


def attend(q, slots, block_keys, block_mine, seqs):
    rows = q.shape[0]
    local = rows // seqs
    parts = len(slots)
    full = parts * local
    scale = LOG2E / math.sqrt(HD)

    def body(q_ref, *refs):
        k_refs, v_refs = refs[:parts], refs[parts : 2 * parts]
        kid_ref, qid_ref, o_ref, lse_ref, bias_ref = refs[2 * parts :]

        @pl.when(pl.program_id(1) == 0)
        def _():
            bias_ref[...] = jnp.where(kid_ref[0] <= qid_ref[0], 0.0, -1e30)

        keys = jnp.concatenate([r[...] for r in k_refs], 0)
        values_t = jnp.concatenate([r[...] for r in v_refs], 0).T
        for h in range(GROUP):
            qh = q_ref[:, h * HD : (h + 1) * HD]
            s = dot(keys, qh, NT) * scale + bias_ref[...]
            top = jnp.max(s, 0, keepdims=True)
            e = jnp.exp2(s - top)
            total = jnp.sum(e, 0, keepdims=True)
            out_t = dot(values_t, e.astype(BF16)) * (1.0 / total)
            o_ref[:, h * HD : (h + 1) * HD] = out_t.T.astype(BF16)
            lse_ref[0, 0, h : h + 1, :] = top + jnp.log2(total)

    return pl.pallas_call(
        body,
        grid=(seqs, KVH),
        in_specs=[pl.BlockSpec((local, GROUP * HD), lambda s, j: (s, j))]
        + slot_specs(parts, local, 0)
        + slot_specs(parts, local, KVH)
        + [
            pl.BlockSpec((1, full, 1), lambda s, j: (s, 0, 0)),
            pl.BlockSpec((1, 1, local), lambda s, j: (s, 0, 0)),
        ],
        out_specs=[
            pl.BlockSpec((local, GROUP * HD), lambda s, j: (s, j)),
            pl.BlockSpec((1, 1, GROUP, local), lambda s, j: (s, j, 0, 0)),
        ],
        out_shape=[sds((rows, H * HD), BF16), sds((seqs, KVH, GROUP, local), F32)],
        scratch_shapes=[pltpu.VMEM((full, local), F32)],
        cost_estimate=cost(8 * rows * full * H * HD, 4 * rows * H * HD, rows * full * H),
        name="attend",
    )(q, *slots, *slots, block_keys, block_mine)


def attend_back(q, slots, block_keys, block_mine, lse, grad, cosine, sine, seqs):
    rows = q.shape[0]
    local = rows // seqs
    parts = len(slots)
    full = parts * local
    head_scale = 1.0 / math.sqrt(HD)
    scale = LOG2E * head_scale

    def body(q_ref, *refs):
        k_refs, v_refs = refs[:parts], refs[parts : 2 * parts]
        kid_ref, qid_ref, lse_ref, g_ref, c_ref, s_ref, dq_ref = refs[2 * parts : 2 * parts + 7]
        dkv_refs, bias_ref = refs[2 * parts + 7 : -1], refs[-1]
        j = pl.program_id(1)

        @pl.when(j == 0)
        def _():
            bias_ref[...] = jnp.where(kid_ref[0] <= qid_ref[0], 0.0, -1e30)

        keys = jnp.concatenate([r[...] for r in k_refs], 0)
        values = jnp.concatenate([r[...] for r in v_refs], 0)
        keys_t = keys.T
        c, sn = c_ref[...], s_ref[...]
        dk = jnp.zeros((full, HD), F32)
        dv = jnp.zeros((full, HD), F32)
        for h in range(GROUP):
            cols = slice(h * HD, (h + 1) * HD)
            qh = q_ref[:, cols]
            gh = g_ref[:, cols]
            p = jnp.exp2(dot(keys, qh, NT) * scale + bias_ref[...] - lse_ref[0, 0, h : h + 1, :])
            dp = dot(values, gh, NT)
            center = jnp.sum(p * dp, 0, keepdims=True)
            ds = (p * (dp - center)).astype(BF16)
            dv = dv + dot(p.astype(BF16), gh)
            dk = dk + dot(ds, qh)
            dq = dot(keys_t, ds).T * head_scale
            dq_ref[:, cols] = (dq * c + pltpu.roll(dq * sn, HD // 2, 1)).astype(BF16)
        k_at = pl.ds(pl.multiple_of(j * HD, HD), HD)
        v_at = pl.ds(pl.multiple_of((KVH + j) * HD, HD), HD)
        for part, ref in enumerate(dkv_refs):
            own = slice(part * local, (part + 1) * local)
            ref[:, k_at] = (dk[own] * head_scale).astype(BF16)
            ref[:, v_at] = dv[own].astype(BF16)

    row = lambda s, j: (s, 0)
    return pl.pallas_call(
        body,
        grid=(seqs, KVH),
        in_specs=[pl.BlockSpec((local, GROUP * HD), lambda s, j: (s, j))]
        + slot_specs(parts, local, 0)
        + slot_specs(parts, local, KVH)
        + [
            pl.BlockSpec((1, full, 1), lambda s, j: (s, 0, 0)),
            pl.BlockSpec((1, 1, local), lambda s, j: (s, 0, 0)),
            pl.BlockSpec((1, 1, GROUP, local), lambda s, j: (s, j, 0, 0)),
            pl.BlockSpec((local, GROUP * HD), lambda s, j: (s, j)),
            pl.BlockSpec((local, HD), row),
            pl.BlockSpec((local, HD), row),
        ],
        out_specs=[pl.BlockSpec((local, GROUP * HD), lambda s, j: (s, j))]
        + [pl.BlockSpec((local, 2 * KVH * HD), row)] * parts,
        out_shape=[sds((rows, H * HD), BF16)] + [sds((rows, 2 * KVH * HD), BF16)] * parts,
        scratch_shapes=[pltpu.VMEM((full, local), F32)],
        cost_estimate=cost(20 * rows * full * H * HD, 8 * rows * H * HD, rows * full * H),
        name="attend_back",
    )(q, *slots, *slots, block_keys, block_mine, lse, grad, cosine, sine)


def out_project(attended, w_out, x, keep, gain, tile):
    rows, width = x.shape
    depth = attended.shape[1]

    def body(a_ref, w_ref, x_ref, k_ref, g_ref, m_ref, n_ref):
        mid = x_ref[...].astype(F32) + k_ref[...] * dot(a_ref[...], w_ref[...])
        inv = lax.rsqrt(jnp.mean(mid * mid, -1, keepdims=True) + EPS)
        m_ref[...] = mid
        n_ref[...] = (mid * inv * g_ref[...]).astype(BF16)

    return pl.pallas_call(
        body,
        grid=(rows // tile,),
        in_specs=[
            pl.BlockSpec((tile, depth), lambda i: (i, 0)),
            const_spec((depth, width)),
            pl.BlockSpec((tile, width), lambda i: (i, 0)),
            pl.BlockSpec((tile, 1), lambda i: (i, 0)),
            const_spec((1, width)),
        ],
        out_specs=[pl.BlockSpec((tile, width), lambda i: (i, 0))] * 2,
        out_shape=[sds((rows, width), F32), sds((rows, width), BF16)],
        cost_estimate=cost(2 * rows * depth * width, 2 * depth * width + 10 * rows * width),
        name="out_project",
    )(attended, w_out, x, keep, gain)


def gate_matmul(normed, w_gate, tile):
    rows, width = normed.shape
    hidden = w_gate.shape[1]

    def body(x_ref, w_ref, g_ref):
        g_ref[...] = dot(x_ref[...], w_ref[...]).astype(BF16)

    return pl.pallas_call(
        body,
        grid=(hidden // tile,),
        in_specs=[const_spec((rows, width)), pl.BlockSpec((width, tile), lambda j: (0, j))],
        out_specs=pl.BlockSpec((rows, tile), lambda j: (0, j)),
        out_shape=sds((rows, hidden), BF16),
        cost_estimate=cost(2 * rows * width * hidden, 2 * width * hidden + 2 * rows * hidden),
        name="gate_matmul",
    )(normed, w_gate)


def up_matmul(normed, w_up, gate, tile):
    rows, width = normed.shape
    hidden = w_up.shape[1]

    def body(x_ref, w_ref, g_ref, u_ref, h_ref):
        up = dot(x_ref[...], w_ref[...])
        g = g_ref[...].astype(F32)
        u_ref[...] = up.astype(BF16)
        h_ref[...] = (g * jax.nn.sigmoid(g) * up).astype(BF16)

    return pl.pallas_call(
        body,
        grid=(hidden // tile,),
        in_specs=[
            const_spec((rows, width)),
            pl.BlockSpec((width, tile), lambda j: (0, j)),
            pl.BlockSpec((rows, tile), lambda j: (0, j)),
        ],
        out_specs=[pl.BlockSpec((rows, tile), lambda j: (0, j))] * 2,
        out_shape=[sds((rows, hidden), BF16)] * 2,
        cost_estimate=cost(2 * rows * width * hidden, 2 * width * hidden + 6 * rows * hidden, rows * hidden),
        name="up_matmul",
    )(normed, w_up, gate)


def down_matmul(hidden, w_down, middle, keep):
    rows, depth = hidden.shape
    pieces, _, tile = w_down.shape

    def body(h_ref, w_ref, m_ref, k_ref, o_ref):
        o_ref[...] = (m_ref[...] + k_ref[...] * dot(h_ref[...], w_ref[0])).astype(BF16)

    return pl.pallas_call(
        body,
        grid=(pieces,),
        in_specs=[
            const_spec((rows, depth)),
            pl.BlockSpec((1, depth, tile), lambda i: (i, 0, 0)),
            pl.BlockSpec((rows, tile), lambda i: (0, i)),
            const_spec((rows, 1)),
        ],
        out_specs=pl.BlockSpec((rows, tile), lambda i: (0, i)),
        out_shape=sds((rows, pieces * tile), BF16),
        cost_estimate=cost(2 * rows * depth * pieces * tile, 2 * depth * pieces * tile + 2 * rows * depth),
        name="down_matmul",
    )(hidden, w_down, middle, keep)


def hidden_back(grad_mlp, w_down, gate, up, tile):
    rows, width = grad_mlp.shape
    pieces, hidden, part = w_down.shape

    def body(m_ref, w_ref, g_ref, u_ref, gg_ref, gu_ref):
        acc = dot(m_ref[:, :part], w_ref[0], NT)
        for i in range(1, pieces):
            acc = acc + dot(m_ref[:, i * part : (i + 1) * part], w_ref[i], NT)
        g = g_ref[...].astype(F32)
        u = u_ref[...].astype(F32)
        sig = jax.nn.sigmoid(g)
        gg_ref[...] = (acc * u * sig * (1.0 + g * (1.0 - sig))).astype(BF16)
        gu_ref[...] = (acc * g * sig).astype(BF16)

    return pl.pallas_call(
        body,
        grid=(hidden // tile,),
        in_specs=[
            const_spec((rows, width)),
            pl.BlockSpec((pieces, tile, part), lambda j: (0, j, 0)),
            pl.BlockSpec((rows, tile), lambda j: (0, j)),
            pl.BlockSpec((rows, tile), lambda j: (0, j)),
        ],
        out_specs=[pl.BlockSpec((rows, tile), lambda j: (0, j))] * 2,
        out_shape=[sds((rows, hidden), BF16)] * 2,
        cost_estimate=cost(2 * rows * width * hidden, 2 * width * hidden + 8 * rows * hidden, rows * hidden),
        name="hidden_back",
    )(grad_mlp, w_down, gate, up)


def mlp_back(grad_gate, grad_up, w_gate, w_up, tile):
    rows, hidden = grad_gate.shape
    width = w_gate.shape[0]

    def body(a_ref, b_ref, wa_ref, wb_ref, o_ref):
        o_ref[...] = dot(a_ref[...], wa_ref[...], NT) + dot(b_ref[...], wb_ref[...], NT)

    once = pl.Buffered(1)
    return pl.pallas_call(
        body,
        grid=(width // tile,),
        in_specs=[
            pl.BlockSpec((rows, hidden), lambda i: (0, 0), pipeline_mode=once),
            pl.BlockSpec((rows, hidden), lambda i: (0, 0), pipeline_mode=once),
            pl.BlockSpec((tile, hidden), lambda i: (i, 0)),
            pl.BlockSpec((tile, hidden), lambda i: (i, 0)),
        ],
        out_specs=pl.BlockSpec((rows, tile), lambda i: (0, i)),
        out_shape=sds((rows, width), F32),
        cost_estimate=cost(4 * rows * width * hidden, 4 * width * hidden + 4 * rows * hidden),
        name="mlp_back",
    )(grad_gate, grad_up, w_gate, w_up)


def middle_back(grad_normed, middle, cotangent, keep, gain, w_out, tile):
    rows, width = middle.shape
    depth = w_out.shape[0]

    def body(n_ref, m_ref, c_ref, k_ref, g_ref, w_ref, gm_ref, gb_ref, ga_ref, gg_ref):
        mid = m_ref[...]
        inv = lax.rsqrt(jnp.mean(mid * mid, -1, keepdims=True) + EPS)
        unit = mid * inv
        grad = n_ref[...]
        u = grad * g_ref[...]
        gmid = c_ref[...].astype(F32) + inv * (u - unit * jnp.mean(u * unit, -1, keepdims=True))
        branch = (k_ref[...] * gmid).astype(BF16)
        gm_ref[...] = gmid
        gb_ref[...] = branch
        ga_ref[...] = dot(branch, w_ref[...], NT).astype(BF16)
        total = jnp.sum(grad * unit, 0, keepdims=True)

        @pl.when(pl.program_id(0) == 0)
        def _():
            gg_ref[...] = total

        @pl.when(pl.program_id(0) > 0)
        def _():
            gg_ref[...] += total

    row = lambda i: (i, 0)
    return pl.pallas_call(
        body,
        grid=(rows // tile,),
        in_specs=[
            pl.BlockSpec((tile, width), row),
            pl.BlockSpec((tile, width), row),
            pl.BlockSpec((tile, width), row),
            pl.BlockSpec((tile, 1), row),
            const_spec((1, width)),
            const_spec((depth, width)),
        ],
        out_specs=[
            pl.BlockSpec((tile, width), row),
            pl.BlockSpec((tile, width), row),
            pl.BlockSpec((tile, depth), row),
            const_spec((1, width)),
        ],
        out_shape=[sds((rows, width), F32), sds((rows, width), BF16), sds((rows, depth), BF16), sds((1, width), F32)],
        cost_estimate=cost(2 * rows * depth * width, 2 * depth * width + 18 * rows * width),
        name="middle_back",
    )(grad_normed, middle, cotangent, keep, gain, w_out)


def input_back(grad_q, grad_kv, weights, x, grad_middle, gain, tile):
    rows, width = x.shape
    depth_q, depth_kv = grad_q.shape[1], grad_kv.shape[1]

    def body(q_ref, kv_ref, wq_ref, x_ref, m_ref, g_ref, o_ref, gg_ref):
        grad = dot(q_ref[...], wq_ref[:, :depth_q], NT) + dot(kv_ref[...], wq_ref[:, depth_q:], NT)
        xin = x_ref[...].astype(F32)
        inv = lax.rsqrt(jnp.mean(xin * xin, -1, keepdims=True) + EPS)
        unit = xin * inv
        u = grad * g_ref[...]
        o_ref[...] = (m_ref[...] + inv * (u - unit * jnp.mean(u * unit, -1, keepdims=True))).astype(BF16)
        total = jnp.sum(grad * unit, 0, keepdims=True)

        @pl.when(pl.program_id(0) == 0)
        def _():
            gg_ref[...] = total

        @pl.when(pl.program_id(0) > 0)
        def _():
            gg_ref[...] += total

    row = lambda i: (i, 0)
    return pl.pallas_call(
        body,
        grid=(rows // tile,),
        in_specs=[
            pl.BlockSpec((tile, depth_q), row),
            pl.BlockSpec((tile, depth_kv), row),
            pl.BlockSpec((width, depth_q + depth_kv), lambda i: (0, 0), pipeline_mode=pl.Buffered(1)),
            pl.BlockSpec((tile, width), row),
            pl.BlockSpec((tile, width), row),
            const_spec((1, width)),
        ],
        out_specs=[pl.BlockSpec((tile, width), row), const_spec((1, width))],
        out_shape=[sds((rows, width), BF16), sds((1, width), F32)],
        cost_estimate=cost(2 * rows * width * (depth_q + depth_kv), 2 * width * (depth_q + depth_kv) + 10 * rows * width),
        name="input_back",
    )(grad_q, grad_kv, weights, x, grad_middle, gain)


def weight_grad(side, chips, a_own, a_pair, b_own, b_pair, tile):
    rows, depth = a_own.shape
    width = b_own.shape[1]
    part = depth // (2 * len(chips))
    out_rows = depth // 2

    def body(side_ref, ao_ref, ap_ref, bo_ref, bp_ref, o_ref, to_ref, tp_ref):
        @pl.when(pl.program_id(0) == 0)
        def _():
            for k, chip in enumerate(chips):
                at = pl.ds(pl.multiple_of((2 * chip + side_ref[0]) * part, part), part)
                own = slice(k * part, (k + 1) * part)
                to_ref[own, :] = ao_ref[:, at].T
                tp_ref[own, :] = ap_ref[:, at].T

        o_ref[...] = (dot(to_ref[...], bo_ref[...]) + dot(tp_ref[...], bp_ref[...])).astype(BF16)

    return pl.pallas_call(
        body,
        grid_spec=pltpu.PrefetchScalarGridSpec(
            num_scalar_prefetch=1,
            grid=(width // tile,),
            in_specs=[
                pl.BlockSpec((rows, depth), lambda j, _: (0, 0), pipeline_mode=pl.Buffered(1)),
                pl.BlockSpec((rows, depth), lambda j, _: (0, 0), pipeline_mode=pl.Buffered(1)),
                pl.BlockSpec((rows, tile), lambda j, _: (0, j)),
                pl.BlockSpec((rows, tile), lambda j, _: (0, j)),
            ],
            out_specs=pl.BlockSpec((out_rows, tile), lambda j, _: (0, j)),
            scratch_shapes=[pltpu.VMEM((out_rows, rows), BF16)] * 2,
        ),
        out_shape=sds((out_rows, width), BF16),
        cost_estimate=cost(4 * rows * out_rows * width, 2 * out_rows * width + 4 * rows * width + 4 * rows * depth),
        name="weight_grad",
    )(side, a_own, a_pair, b_own, b_pair)


def on_device(
    layer_input,
    cotangent,
    positions,
    block_ids,
    skip_mask,
    attn_gain,
    w_query,
    w_key,
    w_value,
    w_out,
    mlp_gain,
    w_gate,
    w_up,
    w_down,
):
    seqs, local, width = layer_input.shape
    rows = seqs * local
    fsdp = lax.axis_size("fsdp")
    parts = lax.axis_size("ulysses")
    place = lax.axis_index("ulysses")
    side = lax.rem(lax.axis_index("fsdp"), 2).astype(jnp.int32).reshape(1)
    chips = fsdp // 2
    ring = [0, 1, 3, 2] if chips == 4 else list(range(chips))
    groups = [[2 * chip + core for chip in ring] for core in range(2)]
    pairs = [(i, i ^ 1) for i in range(fsdp)]
    ahead = min(parts - 1, -(-(BLOCK - 1) // local))
    query_width, pair_width = H * HD, KVH * HD
    tile = 512

    def after(v, *others):
        return lax.optimization_barrier((v,) + others)[0]

    def gather(v, tiled=True):
        return lax.all_gather(v, "fsdp", axis=0, tiled=tiled)

    def swap(v):
        return lax.ppermute(v, "fsdp", pairs)

    def scatter(v):
        return lax.psum_scatter(
            v, "fsdp", scatter_dimension=0, tiled=True, axis_index_groups=groups
        )

    def finish(v):
        middle = parts // 2
        if parts % 2:
            return lax.psum(v, "ulysses")

        def add(a, b):
            return (a.astype(F32) + b.astype(F32)).astype(BF16)

        for d in range(middle - 1):
            v = add(v, lax.ppermute(v, "ulysses", [(d, d + 1), (parts - 1 - d, parts - 2 - d)]))
        v = add(v, lax.ppermute(v, "ulysses", [(middle - 1, middle), (middle, middle - 1)]))
        for d in range(middle - 1, 0, -1):
            came = lax.ppermute(v, "ulysses", [(d, d - 1), (parts - 1 - d, parts - d)])
            v = jnp.where((place == d - 1) | (place == parts - d), came, v)
        return v

    def finish_in(v, pieces):
        step = v.shape[0] // pieces
        return jnp.concatenate([finish(v[i * step : (i + 1) * step]) for i in range(pieces)], 0)

    def grad_of(a, a_pair, b, b_pair):
        return weight_grad(side, ring, a, a_pair, b, b_pair, tile)

    def spread(v):
        ups, held = [], v
        for r in range(1, parts):
            held = lax.ppermute(held, "ulysses", [(i, i + 1) for i in range(r - 1, parts - 1)])
            ups.append(held)
        slots = [v] + ups
        for i in range(1, ahead + 1):
            down = lax.ppermute(v, "ulysses", [(z + i, z) for z in range(parts - i)])
            slots[parts - i] = jnp.where(place >= parts - i, slots[parts - i], down)
        return slots

    def collect(slots):
        total = slots[0].astype(F32)
        for i in range(1, ahead + 1):
            up = lax.ppermute(slots[parts - i], "ulysses", [(z, z + i) for z in range(parts - i)])
            total = total + up.astype(F32)
        held = slots[parts - 1]
        for r in range(parts - 1, 0, -1):
            came = lax.ppermute(held, "ulysses", [(i, i - 1) for i in range(r, parts)])
            if r > 1:
                held = (slots[r - 1].astype(F32) + came.astype(F32)).astype(BF16)
            else:
                total = total + came.astype(F32)
        return total

    gains = lax.all_gather(jnp.stack([attn_gain, mlp_gain]), "fsdp", axis=1, tiled=True).astype(F32)
    gain_one, gain_two = gains[0:1], gains[1:2]
    qkv_full = gather(jnp.concatenate([w_query, w_key, w_value], 1))
    out_full = gather(after(w_out, qkv_full))

    x = layer_input.reshape(rows, width)
    xf = x.astype(F32)
    inv_one = lax.rsqrt(jnp.mean(xf * xf, -1, keepdims=True) + EPS)
    normed_one = (xf * inv_one * gain_one).astype(BF16)
    keep = jnp.repeat((1 - skip_mask).astype(F32), local)[:, None]
    cot = cotangent.reshape(rows, width)
    grad_mlp = (keep * cot.astype(F32)).astype(BF16)

    half = HD // 2
    frequency = jnp.exp(jnp.arange(half, dtype=F32) * (-2.0 * math.log(10000.0) / HD))
    angles = positions.reshape(rows, 1).astype(F32) * frequency
    cosine = jnp.concatenate([jnp.cos(angles)] * 2, -1)
    sine = jnp.sin(angles)
    sine = jnp.concatenate([-sine, sine], -1)
    by_part = block_ids.reshape(seqs, parts, local)
    block_mine = lax.dynamic_slice_in_dim(by_part, place, 1, 1)
    order = lax.rem(place - jnp.arange(parts) + parts, parts)
    block_keys = jnp.take(by_part, order, 1).reshape(seqs, parts * local, 1)

    query, kv = project(normed_one, qkv_full, cosine, sine)
    slots = spread(kv)
    gate_full = gather(after(w_gate, out_full, slots[1]))
    one_pair, mlp_pair = swap(normed_one), swap(grad_mlp)
    attended, lse = attend(query, slots, block_keys, block_mine, seqs)
    middle, normed_two = out_project(attended, out_full, x, keep, gain_two, local)
    up_full = gather(after(w_up, gate_full, normed_two))
    gate = gate_matmul(normed_two, gate_full, tile)
    down_full = gather(after(w_down, up_full, gate), False)
    two_pair, att_pair = swap(normed_two), swap(attended)
    up, hidden = up_matmul(normed_two, up_full, gate, tile)

    hidden_pair = swap(hidden)
    down_part = grad_of(grad_mlp, mlp_pair, hidden, hidden_pair)
    down_sum = scatter(down_part)
    grad_gate, grad_up = hidden_back(after(grad_mlp, down_part), down_full, gate, up, tile)
    gate_pair, up_pair = swap(grad_gate), swap(grad_up)
    grad_normed_two = mlp_back(grad_gate, grad_up, gate_full, up_full, 256)
    gate_part = grad_of(normed_two, two_pair, after(grad_gate, grad_normed_two), gate_pair)
    gate_sum = scatter(after(gate_part, down_sum))
    grad_middle, grad_branch, grad_attended, grad_gain_two = middle_back(
        after(grad_normed_two, gate_part), middle, cot, keep, gain_two, out_full, local
    )
    branch_pair = swap(grad_branch)
    grad_query, *grad_slots = attend_back(
        query, slots, block_keys, block_mine, lse, grad_attended, cosine, sine, seqs
    )
    query_pair = swap(grad_query)
    up_part = grad_of(normed_two, two_pair, after(grad_up, grad_query), up_pair)
    up_sum = scatter(after(up_part, gate_sum))
    out_part = grad_of(attended, att_pair, after(grad_branch, up_part), branch_pair)
    out_sum = scatter(after(out_part, up_sum))
    query_part = grad_of(normed_one, one_pair, after(grad_query, out_part), query_pair)
    query_sum = scatter(after(query_part, out_sum))
    output = down_matmul(after(hidden, query_part), down_full, middle, keep)

    grad_kv = collect(grad_slots)
    grad_key = grad_kv[:, :pair_width].reshape(rows, KVH, HD)
    turned = grad_key * sine[:, None, :]
    turned = jnp.concatenate([turned[..., half:], turned[..., :half]], -1)
    grad_key = (grad_key * cosine[:, None, :] + turned).reshape(rows, pair_width)
    grad_kv = jnp.concatenate([grad_key, grad_kv[:, pair_width:]], 1).astype(BF16)
    kv_pair = swap(grad_kv)
    kv_part = grad_of(normed_one, one_pair, grad_kv, kv_pair)
    kv_sum = scatter(after(kv_part, query_sum))
    grad_input, grad_gain_one = input_back(
        grad_query, after(grad_kv, kv_part), qkv_full, x, grad_middle, gain_one, local
    )

    gain_sums = lax.psum(jnp.concatenate([grad_gain_one, grad_gain_two], 0), ("fsdp", "ulysses"))
    own = width // fsdp
    gain_shard = lax.dynamic_slice_in_dim(gain_sums, lax.axis_index("fsdp") * own, own, 1)
    out_down, out_gate, out_up, out_out, out_query, out_kv = (
        finish_in(v, pieces).astype(F32)
        for v, pieces in (
            (down_sum, 2),
            (gate_sum, 2),
            (up_sum, 2),
            (out_sum, 1),
            (query_sum, 1),
            (kv_sum, 1),
        )
    )
    return (
        output.reshape(layer_input.shape),
        grad_input.reshape(layer_input.shape),
        gain_shard[0],
        out_query,
        out_kv[:, :pair_width],
        out_kv[:, pair_width:],
        out_out,
        gain_shard[1],
        out_gate,
        out_up,
        out_down.T,
    )


def solution(mesh):
    return jax.shard_map(
        on_device,
        mesh=mesh,
        in_specs=(
            P("fsdp", "ulysses", None),
            P("fsdp", "ulysses", None),
            P("fsdp", "ulysses"),
            P("fsdp", None),
            P("fsdp"),
            P("fsdp"),
            P("fsdp", None),
            P("fsdp", None),
            P("fsdp", None),
            P("fsdp", None),
            P("fsdp"),
            P("fsdp", None),
            P("fsdp", None),
            P(None, "fsdp"),
        ),
        out_specs=(
            P("fsdp", "ulysses", None),
            P("fsdp", "ulysses", None),
            P("fsdp"),
            P("fsdp", None),
            P("fsdp", None),
            P("fsdp", None),
            P("fsdp", None),
            P("fsdp"),
            P("fsdp", None),
            P("fsdp", None),
            P(None, "fsdp"),
        ),
        check_vma=False,
    )
```

time: 2330 us -> 1400 us (0.60)
  waiting for transfers between devices: 1370 us -> 654 us
  matrix products: 471 us -> 0 us
  Pallas kernels: 0 us -> 421 us
  local copies, waits for them, and re-layouts: 178 us -> 26.2 us
  starting transfers between devices: 35.8 us -> 166 us
  other arithmetic: 181 us -> 61.6 us
    unnamed x11, waiting for transfers between devices: 495 us -> 0.18 us
    dot_general x39 -> x0, matrix products: 471 us -> none  [the longest x1 44.9 us: on_device(): jnp.einsum('rc,re->ce', normed_piece, grad_mlp_mid, preferred_element_typ...]
    pallas_call x0 -> x17, Pallas kernels: none -> 421 us  [the longest x6 110 us: weight_grad(): pl.pallas_call(body, grid_spec=pltpu.PrefetchScalarGridSpec(num_scalar_pr...]
    ppermute x0 -> x45, waiting for transfers between devices: none -> 394 us  [the longest x9 186 us: finish(): lax.ppermute(v, 'ulysses', [(d, d + 1), (parts - 1 - d, parts - 2 - d)])]
    psum x1 -> x0, waiting for transfers between devices: 317 us -> none  [on_device(): lax.psum(owner_sums.astype(jnp.bfloat16), 'ulysses').astype(jnp.float32)]
    all_to_all x8 -> x0, waiting for transfers between devices: 222 us -> none  [the longest x1 71.1 us: on_device(): lax.all_to_all(grad_attended, 'ulysses', split_axis=2, concat_axis=1, til...]
    ppermute x0 -> x45, starting transfers between devices: none -> 165 us  [the longest x9 121 us: finish(): lax.ppermute(v, 'ulysses', [(d, d + 1), (parts - 1 - d, parts - 2 - d)])]
    all_gather x8 -> x5, waiting for transfers between devices: 337 us -> 246 us  [gather(): return lax.all_gather(v, 'fsdp', axis=0, tiled=tiled)]
  transfers between devices with their start and end apart: 18 -> 56, of which waited for: 12 -> 24; matrix products, arithmetic and copies ran while one was open for 17% -> 6% of each run, Pallas kernels for 0% -> 30%
where the time goes in v1:
time: 1400 us
  waiting for transfers between devices  654 us (47%)
  Pallas kernels  421 us (30%)
  starting transfers between devices  166 us (12%)
  other arithmetic  61.6 us (4%)
  blocking collectives  51.7 us (4%)
  local copies, waits for them, and re-layouts  26.2 us (2%)
  between operations  15.2 us (1%)
    all_gather x5, waiting for transfers between devices, gather(): return lax.all_gather(v, 'fsdp', axis=0, tiled=tiled)  246 us
    ppermute x9, waiting for transfers between devices, finish(): lax.ppermute(v, 'ulysses', [(d, d + 1), (parts - 1 - d, parts - 2 - d)])  186 us
    ppermute x9, waiting for transfers between devices, finish(): came = lax.ppermute(v, 'ulysses', [(d, d - 1), (parts - 1 - d, parts - d)])  125 us
    ppermute x9, starting transfers between devices, finish(): lax.ppermute(v, 'ulysses', [(d, d + 1), (parts - 1 - d, parts - 2 - d)])  121 us
    pallas_call x6, Pallas kernels, weight_grad(): pl.pallas_call(body, grid_spec=pltpu.PrefetchScalarGridSpec(num_scalar_pr...  110 us
    pallas_call x1, Pallas kernels, attend_back(): pl.pallas_call(body, grid=(seqs, KVH), in_specs=[pl.BlockSpec((local, GRO...  48.6 us
    pallas_call x1, Pallas kernels, mlp_back(): pl.pallas_call(body, grid=(width // tile,), in_specs=[pl.BlockSpec((rows,...  46.1 us
    psum x1, blocking collectives, on_device(): lax.psum(jnp.concatenate([grad_gain_one, grad_gain_two], 0), ('fsdp', 'ul...  42.8 us
  transfers between devices with their start and end apart: 56, of which 24 were waited for; matrix products, arithmetic and copies ran while one was open for 6% of the time, Pallas kernels for 30%

profile of v1, /device:TPU:0, one launch (start us, length us, event | category | flops | bytes accessed | tf_op | source)
XLA Modules:
  0.0 1396.8 jit_solution(3778993714902465416)
XLA Ops:
  7.2 2.8 pad_maximum_fusion
  10.1 75.2 %all-gather.7.cloned.1.call-done.w_ref.wq_ref = bf16[2048,3072]{1,0:T(8,128)(2,1)} async-done(((bf16[256,3072]{1,0:T(8,128)(2,1)}), bf16[2048,3072]{1,0:T(8,128)(2,1)}) %all-gather.7.cloned.1.call-update) | async-done | bytes 12582928 | tf_op jit(solution)/shard_map/all_gather | solution.py:516
  86.2 8.8 all_gather.21
  98.3 2.5 multiply_convert_fusion.1.x_ref.ao_ref
  100.8 17.4 %project.1 = (bf16[768,2048]{1,0:T(8,128)(2,1)}, bf16[768,1024]{1,0:T(8,128)(2,1)}) custom-call(bf16[768,2048]{1,0:T(8,128)(2,1)} %multiply_convert_fusion.1.x_ref.ao_ref, bf16[2048,3072]{1,0:T(8,128)(2,1)} %all-gather.7.cloned.1.call-done.w_ref.wq_ref, f32[768,128]{1,0:T(8,128)} %get-tuple-element.132.c_ref.refs_12_, ...), custom_call_target="tpu_custom_call" | custom-call | flops 9663676416 | bytes 18874368 | tf_op jit(solution)/shard_map/project/pallas_call | solution.py:71
  118.1 4.7 collective-permute-start
  122.8 33.3 %collective-permute-done.refs_1_.refs_5_ = bf16[768,1024]{1,0:T(8,128)(2,1)} collective-permute-done((bf16[768,1024]{1,0:T(8,128)(2,1)}, bf16[768,1024]{1,0:T(8,128)(2,1)}, u32[]{:S(2)}, u32[]{:S(2)}) %collective-permute-start) | collective-permute-done | bytes 1572896 | tf_op jit(solution)/shard_map/ppermute | solution.py:552
  159.3 2.1 collective-permute-start.2
  165.7 33.4 %collective-permute-done.3 = bf16[768,1024]{1,0:T(8,128)(2,1)S(1)} collective-permute-done((bf16[768,1024]{1,0:T(8,128)(2,1)}, bf16[768,1024]{1,0:T(8,128)(2,1)S(1)}, u32[]{:S(2)}, u32[]{:S(2)}) %collective-permute-start.3) | collective-permute-done | bytes 1572896 | tf_op jit(solution)/shard_map/ppermute | solution.py:556
  200.5 39.0 %attend.1 = (bf16[768,2048]{1,0:T(8,128)(2,1)}, f32[3,4,4,256]{3,2,1,0:T(4,128)}) custom-call(bf16[768,2048]{1,0:T(8,128)(2,1)} %get-tuple-element.49.q_ref, bf16[768,1024]{1,0:T(8,128)(2,1)} %get-tuple-element.50.refs_0_.refs_4_, bf16[768,1024]{1,0:T(8,128)(2,1)} %collective-permute-done.refs_1_.refs_5_, ...), custom_call_target="tpu_custom_call" | custom-call | flops 12884901888 | bytes 6291456 | tf_op jit(solution)/shard_map/attend/pallas_call | solution.py:121
  239.5 14.0 %out_project.1 = (f32[768,2048]{1,0:T(8,128)}, bf16[768,2048]{1,0:T(8,128)(2,1)}) custom-call(bf16[768,2048]{1,0:T(8,128)(2,1)} %get-tuple-element.51.a_ref.ao_ref, bf16[2048,2048]{1,0:T(8,128)(2,1)} %all-gather.9.cloned.1.call-done.w_ref, bf16[768,2048]{1,0:T(8,128)(2,1)} %bitcast.34, f32[768,1]{1,0:T(8,128)} %bitcast.39, f32[1,2048]{1,0:T(1,128)} %get-tuple-element.127.g_ref), custom_call_target="tpu_custom_call" | custom-call | flops 6442450944 | bytes 24117248 | tf_op jit(solution)/shard_map/out_project/pallas_call | solution.py:219
  253.5 20.3 %all-gather.11.cloned.1.call-done.w_ref.wa_ref = bf16[2048,5632]{1,0:T(8,128)(2,1)} async-done(((bf16[256,5632]{1,0:T(8,128)(2,1)}), bf16[2048,5632]{1,0:T(8,128)(2,1)}) %all-gather.11.cloned.1.call-update) | async-done | bytes 23068688 | tf_op jit(solution)/shard_map/all_gather | solution.py:516
  273.8 24.0 %gate_matmul.1.g_ref = bf16[768,5632]{1,0:T(8,128)(2,1)} custom-call(bf16[768,2048]{1,0:T(8,128)(2,1)} %get-tuple-element.53.x_ref.ao_ref, bf16[2048,5632]{1,0:T(8,128)(2,1)} %all-gather.11.cloned.1.call-done.w_ref.wa_ref), custom_call_target="tpu_custom_call" | custom-call | flops 17716740096 | bytes 31719424 | tf_op jit(solution)/shard_map/gate_matmul/pallas_call | solution.py:243
  297.8 106.5 %all-gather.13.cloned.1.call-done.w_ref.wb_ref = bf16[2048,5632]{1,0:T(8,128)(2,1)} async-done(((bf16[256,5632]{1,0:T(8,128)(2,1)}), bf16[2048,5632]{1,0:T(8,128)(2,1)}) %all-gather.13.cloned.1.call-update) | async-done | bytes 23068688 | tf_op jit(solution)/shard_map/all_gather | solution.py:516
  404.4 28.2 %up_matmul.1 = (bf16[768,5632]{1,0:T(8,128)(2,1)}, bf16[768,5632]{1,0:T(8,128)(2,1)}) custom-call(bf16[768,2048]{1,0:T(8,128)(2,1)} %get-tuple-element.53.x_ref.ao_ref, bf16[2048,5632]{1,0:T(8,128)(2,1)} %all-gather.13.cloned.1.call-done.w_ref.wb_ref, bf16[768,5632]{1,0:T(8,128)(2,1)} %gate_matmul.1.g_ref), custom_call_target="tpu_custom_call" | custom-call | flops 17716740096 | bytes 49020928 | tf_op jit(solution)/shard_map/up_matmul/pallas_call | solution.py:264
  433.0 2.3 multiply_convert_fusion.ao_ref.m_ref
  435.5 15.4 %collective-permute-done.5.ap_ref = bf16[768,2048]{1,0:T(8,128)(2,1)S(1)} collective-permute-done((bf16[768,2048]{1,0:T(8,128)(2,1)}, bf16[768,2048]{1,0:T(8,128)(2,1)S(1)}, u32[]{:S(2)}, u32[]{:S(2)}) %collective-permute-start.5) | collective-permute-done | bytes 3145760 | tf_op jit(solution)/shard_map/ppermute | solution.py:519
  452.5 25.7 %weight_grad.6 = bf16[1024,5632]{1,0:T(8,128)(2,1)} custom-call(s32[1]{0:T(128)} %bitcast.6.side_ref, bf16[768,2048]{1,0:T(8,128)(2,1)} %multiply_convert_fusion.ao_ref.m_ref, bf16[768,2048]{1,0:T(8,128)(2,1)} %copy-done.21, bf16[768,5632]{1,0:T(8,128)(2,1)} %get-tuple-element.72.bo_ref.h_ref, bf16[768,5632]{1,0:T(8,128)(2,1)} %collective-permute-done.6.bp_ref), custom_call_target="tpu_custom_call" | custom-call | flops 17716740096 | bytes 35127296 | tf_op jit(solution)/shard_map/weight_grad/pallas_call | solution.py:462
  478.7 43.8 %all-gather.15.cloned.1.call-done = bf16[45056,256]{1,0:T(8,128)(2,1)} async-done(((bf16[5632,256]{1,0:T(8,128)(2,1)}), bf16[45056,256]{1,0:T(8,128)(2,1)}) %all-gather.15.cloned.1.call-update) | async-done | bytes 23068688 | tf_op jit(solution)/shard_map/all_gather | solution.py:516
  522.5 31.3 %hidden_back.1 = (bf16[768,5632]{1,0:T(8,128)(2,1)}, bf16[768,5632]{1,0:T(8,128)(2,1)}) custom-call(bf16[768,2048]{1,0:T(8,128)(2,1)} %multiply_convert_fusion.ao_ref.m_ref, bf16[8,5632,256]{2,1,0:T(8,128)(2,1)} %bitcast.48, bf16[768,5632]{1,0:T(8,128)(2,1)} %gate_matmul.1.g_ref, bf16[768,5632]{1,0:T(8,128)(2,1)} %get-tuple-element.60.u_ref), custom_call_target="tpu_custom_call" | custom-call | flops 17716740096 | bytes 57671680 | tf_op jit(solution)/shard_map/hidden_back/pallas_call | solution.py:316
  554.4 46.1 %mlp_back.1.n_ref = f32[768,2048]{1,0:T(8,128)} custom-call(bf16[768,5632]{1,0:T(8,128)(2,1)} %get-tuple-element.63.a_ref.bo_ref, bf16[768,5632]{1,0:T(8,128)(2,1)} %get-tuple-element.69.b_ref.bo_ref, bf16[2048,5632]{1,0:T(8,128)(2,1)} %all-gather.11.cloned.1.call-done.w_ref.wa_ref, bf16[2048,5632]{1,0:T(8,128)(2,1)} %all-gather.13.cloned.1.call-done.w_ref.wb_ref), custom_call_target="tpu_custom_call" | custom-call | flops 35433480192 | bytes 63438848 | tf_op jit(solution)/shard_map/mlp_back/pallas_call | solution.py:340
  600.5 25.3 %weight_grad.7 = bf16[1024,5632]{1,0:T(8,128)(2,1)} custom-call(s32[1]{0:T(128)} %bitcast.6.side_ref, bf16[768,2048]{1,0:T(8,128)(2,1)} %get-tuple-element.53.x_ref.ao_ref, bf16[768,2048]{1,0:T(8,128)(2,1)} %collective-permute-done.7.ap_ref, bf16[768,5632]{1,0:T(8,128)(2,1)} %get-tuple-element.63.a_ref.bo_ref, bf16[768,5632]{1,0:T(8,128)(2,1)} %collective-permute-done.8.bp_ref), custom_call_target="tpu_custom_call" | custom-call | flops 17716740096 | bytes 35127296 | tf_op jit(solution)/shard_map/weight_grad/pallas_call | solution.py:462
  627.5 18.3 %middle_back.1 = (f32[768,2048]{1,0:T(8,128)}, bf16[768,2048]{1,0:T(8,128)(2,1)}, bf16[768,2048]{1,0:T(8,128)(2,1)}, f32[1,2048]{1,0:T(1,128)}) custom-call(f32[768,2048]{1,0:T(8,128)} %mlp_back.1.n_ref, f32[768,2048]{1,0:T(8,128)} %get-tuple-element.65.m_ref, bf16[768,2048]{1,0:T(8,128)(2,1)} %bitcast.36, f32[768,1]{1,0:T(8,128)} %bitcast.40, ...), custom_call_target="tpu_custom_call" | custom-call | flops 6442450944 | bytes 36700160 | tf_op jit(solution)/shard_map/middle_back/pallas_call | solution.py:382
  645.8 48.6 %attend_back.1 = (bf16[768,2048]{1,0:T(8,128)(2,1)}, bf16[768,1024]{1,0:T(8,128)(2,1)}, bf16[768,1024]{1,0:T(8,128)(2,1)}, bf16[768,1024]{1,0:T(8,128)(2,1)}, bf16[768,1024]{1,0:T(8,128)(2,1)}) custom-call(bf16[768,2048]{1,0:T(8,128)(2,1)} %get-tuple-element.49.q_ref, bf16[768,1024]{1,0:T(8,128)(2,1)} %get-tuple-element.50.refs_0_.refs_4_, ...), custom_call_target="tpu_custom_call" | custom-call | flops 32212254720 | bytes 12582912 | tf_op jit(solution)/shard_map/attend_back/pallas_call | solution.py:186
  694.5 25.2 %weight_grad.8 = bf16[1024,5632]{1,0:T(8,128)(2,1)} custom-call(s32[1]{0:T(128)} %bitcast.6.side_ref, bf16[768,2048]{1,0:T(8,128)(2,1)} %get-tuple-element.53.x_ref.ao_ref, bf16[768,2048]{1,0:T(8,128)(2,1)} %collective-permute-done.7.ap_ref, bf16[768,5632]{1,0:T(8,128)(2,1)} %get-tuple-element.69.b_ref.bo_ref, bf16[768,5632]{1,0:T(8,128)(2,1)} %collective-permute-done.10.bp_ref), custom_call_target="tpu_custom_call" | custom-call | flops 17716740096 | bytes 35127296 | tf_op jit(solution)/shard_map/weight_grad/pallas_call | solution.py:462
  719.6 12.6 reduce-scatter.9.cloned.1.call-done
  734.2 3.5 collective-permute-start.39
  739.1 30.5 %collective-permute-done.39 = bf16[128,5632]{1,0:T(8,128)(2,1)S(1)} collective-permute-done((bf16[128,5632]{1,0:T(8,128)(2,1)S(1)}, bf16[128,5632]{1,0:T(8,128)(2,1)S(1)}, u32[]{:S(2)}, u32[]{:S(2)}) %collective-permute-start.39) | collective-permute-done | bytes 1441824 | tf_op jit(solution)/shard_map/ppermute | solution.py:535
  769.6 29.8 %collective-permute-done.42 = bf16[128,5632]{1,0:T(8,128)(2,1)S(1)} collective-permute-done((bf16[128,5632]{1,0:T(8,128)(2,1)S(1)}, bf16[128,5632]{1,0:T(8,128)(2,1)S(1)}, u32[]{:S(2)}, u32[]{:S(2)}) %collective-permute-start.42) | collective-permute-done | bytes 1441824 | tf_op jit(solution)/shard_map/ppermute | solution.py:535
  799.4 2.3 add_convert_fusion.5
  810.5 62.9 %collective-permute-done.41 = bf16[128,5632]{1,0:T(8,128)(2,1)S(1)} collective-permute-done((bf16[128,5632]{1,0:T(8,128)(2,1)S(1)}, bf16[128,5632]{1,0:T(8,128)(2,1)S(1)}, u32[]{:S(2)}, u32[]{:S(2)}) %collective-permute-start.41) | collective-permute-done | bytes 1441824 | tf_op jit(solution)/shard_map/ppermute | solution.py:538
  874.3 28.5 %collective-permute-done.44 = bf16[128,5632]{1,0:T(8,128)(2,1)S(1)} collective-permute-done((bf16[128,5632]{1,0:T(8,128)(2,1)S(1)}, bf16[128,5632]{1,0:T(8,128)(2,1)S(1)}, u32[]{:S(2)}, u32[]{:S(2)}) %collective-permute-start.44) | collective-permute-done | bytes 1441824 | tf_op jit(solution)/shard_map/ppermute | solution.py:538
  903.0 10.1 collective-permute-start.13
  915.5 3.2 convert_bitcast_fusion
  918.7 6.2 copy.32
  925.0 12.4 weight_grad.9
  937.4 12.4 weight_grad.10
  951.1 3.3 convert_add_fusion
  956.8 2.8 reshape.160
  969.6 5.2 collective-permute-start.27
  974.8 2.6 collective-permute-start.30
  977.4 24.9 %down_matmul.1 = bf16[768,2048]{1,0:T(8,128)(2,1)} custom-call(bf16[768,5632]{1,0:T(8,128)(2,1)} %get-tuple-element.72.bo_ref.h_ref, bf16[8,5632,256]{2,1,0:T(8,128)(2,1)} %bitcast.49, f32[768,2048]{1,0:T(8,128)} %get-tuple-element.65.m_ref, f32[768,1]{1,0:T(8,128)} %bitcast.41), custom_call_target="tpu_custom_call" | custom-call | flops 17716740096 | bytes 31719424 | tf_op jit(solution)/shard_map/down_matmul/pallas_call | solution.py:286
  1002.4 3.7 collective-permute-done.27
  1006.1 28.6 %collective-permute-done.30 = bf16[128,5632]{1,0:T(8,128)(2,1)} collective-permute-done((bf16[128,5632]{1,0:T(8,128)(2,1)}, bf16[128,5632]{1,0:T(8,128)(2,1)}, u32[]{:S(2)}, u32[]{:S(2)}) %collective-permute-start.30) | collective-permute-done | bytes 1441824 | tf_op jit(solution)/shard_map/ppermute | solution.py:535
  1034.7 4.0 add_convert_fusion.13
  1039.5 8.8 weight_grad.11
  1048.3 19.7 %input_back.1 = (bf16[768,2048]{1,0:T(8,128)(2,1)}, f32[1,2048]{1,0:T(1,128)}) custom-call(bf16[768,2048]{1,0:T(8,128)(2,1)} %get-tuple-element.71.bo_ref.q_ref, bf16[768,1024]{1,0:T(8,128)(2,1)} %pad_maximum_fusion.2.bo_ref.kv_ref, bf16[2048,3072]{1,0:T(8,128)(2,1)} %all-gather.7.cloned.1.call-done.w_ref.wq_ref, bf16[768,2048]{1,0:T(8,128)(2,1)} %bitcast.35, ...), custom_call_target="tpu_custom_call" | custom-call | flops 9663676416 | bytes 28311552 | tf_op jit(solution)/shard_map/input_back/pallas_call | solution.py:427
  1068.7 42.8 %psum.7 = f32[2,2048]{1,0:T(2,128)S(1)} all-reduce(f32[2,2048]{1,0:T(2,128)S(1)} %pad_maximum_fusion.5), channel_id=1, replica_groups=mesh['fsdp'=8,'ulysses'=4] {'fsdp','ulysses'}, use_global_device_ids=true, to_apply=%region_1.2 | all-reduce | flops 4096 | bytes 32768 | tf_op jit(solution)/shard_map/psum | solution.py:647
  1113.0 2.8 add_convert_fusion.12
  1120.6 32.4 %collective-permute-start.33 = (bf16[128,5632]{1,0:T(8,128)(2,1)S(1)}, bf16[128,5632]{1,0:T(8,128)(2,1)S(1)}, u32[]{:S(2)}, u32[]{:S(2)}) collective-permute-start(bf16[128,5632]{1,0:T(8,128)(2,1)S(1)} %get-tuple-element.115), channel_id=1, source_target_pairs={{0,1},{3,2},{4,5},{7,6},{8,9},{11,10},{12,13},{15,14},{16,17},{19,... | collective-permute-start | bytes 4325384 | tf_op jit(solution)/shard_map/ppermute | solution.py:535
  1156.2 28.7 %collective-permute-done.33 = bf16[128,5632]{1,0:T(8,128)(2,1)S(1)} collective-permute-done((bf16[128,5632]{1,0:T(8,128)(2,1)S(1)}, bf16[128,5632]{1,0:T(8,128)(2,1)S(1)}, u32[]{:S(2)}, u32[]{:S(2)}) %collective-permute-start.33) | collective-permute-done | bytes 1441824 | tf_op jit(solution)/shard_map/ppermute | solution.py:535
  1184.9 28.0 %collective-permute-done.36 = bf16[128,5632]{1,0:T(8,128)(2,1)S(1)} collective-permute-done((bf16[128,5632]{1,0:T(8,128)(2,1)S(1)}, bf16[128,5632]{1,0:T(8,128)(2,1)S(1)}, u32[]{:S(2)}, u32[]{:S(2)}) %collective-permute-start.36) | collective-permute-done | bytes 1441824 | tf_op jit(solution)/shard_map/ppermute | solution.py:535
  1216.2 3.2 maximum_convert_fusion
  1223.4 61.8 %collective-permute-start.24 = (bf16[256,2048]{1,0:T(8,128)(2,1)}, bf16[256,2048]{1,0:T(8,128)(2,1)}, u32[]{:S(2)}, u32[]{:S(2)}) collective-permute-start(bf16[256,2048]{1,0:T(8,128)(2,1)} %reduce-scatter.13.cloned.1.call-done), channel_id=1, source_target_pairs={{0,1},{3,2},{4,5},{7,6},{8,9},{11,10},{12,13},{15,14},{16,17},{19,... | collective-permute-start | bytes 3145736 | tf_op jit(solution)/shard_map/ppermute | solution.py:535
  1286.8 16.6 %collective-permute-done.24 = bf16[256,2048]{1,0:T(8,128)(2,1)} collective-permute-done((bf16[256,2048]{1,0:T(8,128)(2,1)}, bf16[256,2048]{1,0:T(8,128)(2,1)}, u32[]{:S(2)}, u32[]{:S(2)}) %collective-permute-start.24) | collective-permute-done | bytes 1048608 | tf_op jit(solution)/shard_map/ppermute | solution.py:535
  1303.4 1.9 add_convert_fusion.15
  1306.1 6.3 collective-permute-start.18
  1313.9 16.1 %collective-permute-done.18 = bf16[256,2048]{1,0:T(8,128)(2,1)S(1)} collective-permute-done((bf16[256,2048]{1,0:T(8,128)(2,1)S(1)}, bf16[256,2048]{1,0:T(8,128)(2,1)S(1)}, u32[]{:S(2)}, u32[]{:S(2)}) %collective-permute-start.18) | collective-permute-done | bytes 1048608 | tf_op jit(solution)/shard_map/ppermute | solution.py:535
  1333.7 3.2 maximum_convert_fusion.1
  1336.9 6.2 collective-permute-start.21
  1346.1 4.0 collective-permute-done.21
  1351.0 7.8 collective-permute-done.26
  1361.8 19.5 %collective-permute-done.20 = bf16[256,2048]{1,0:T(8,128)(2,1)S(1)} collective-permute-done((bf16[256,2048]{1,0:T(8,128)(2,1)S(1)}, bf16[256,2048]{1,0:T(8,128)(2,1)S(1)}, u32[]{:S(2)}, u32[]{:S(2)}) %collective-permute-start.20) | collective-permute-done | bytes 1048608 | tf_op jit(solution)/shard_map/ppermute | solution.py:538
  1382.7 5.9 collective-permute-done.23
  (206 shorter events, 82.0 us)
Async XLA Ops:
  7.2 78.2 %all-gather.7.cloned.1.call-start = ((), (), s32[]{:S(2)}) async-start(), calls=%async_computation.6 | async-start | bytes 14155776 | tf_op jit(solution)/shard_map/all_gather | solution.py:516
  7.2 78.3 %copy-start = (bf16[3,256,2048]{2,1,0:T(8,128)(2,1)S(1)}, bf16[3,256,2048]{2,1,0:T(8,128)(2,1)}, u32[]{:S(2)}) copy-start(bf16[3,256,2048]{2,1,0:T(8,128)(2,1)} %param.14) | copy-start | bytes 9437188
  10.1 75.4 %copy-start.18 = (s32[3,256]{1,0:T(4,128)S(1)}, s32[3,256]{1,0:T(4,128)}, u32[]{:S(2)}) copy-start(s32[3,256]{1,0:T(4,128)} %param.16) | copy-start | bytes 9220
  10.1 75.4 %copy-start.22 = (bf16[256]{0:T(256)(128)(2,1)S(1)}, bf16[256]{0:T(256)(128)(2,1)}, u32[]{:S(2)}) copy-start(bf16[256]{0:T(256)(128)(2,1)} %param.24) | copy-start | bytes 1540
  10.1 75.4 %copy-start.23 = (bf16[256]{0:T(256)(128)(2,1)S(1)}, bf16[256]{0:T(256)(128)(2,1)}, u32[]{:S(2)}) copy-start(bf16[256]{0:T(256)(128)(2,1)} %param.19) | copy-start | bytes 1540
  10.1 146.0 %all-gather.9.cloned.1.call-start = ((), (), s32[]{:S(2)}) async-start(), calls=%async_computation.7 | async-start | bytes 9437184 | tf_op jit(solution)/shard_map/all_gather | solution.py:516
  85.4 188.4 %all-gather.11.cloned.1.call-start = ((), (), s32[]{:S(2)}) async-start(), calls=%async_computation.8 | async-start | bytes 25952256 | tf_op jit(solution)/shard_map/all_gather | solution.py:516
  118.1 43.3 %copy-start.15 = (s32[3,1024]{1,0:T(4,128)S(1)}, s32[3,1024]{1,0:T(4,128)}, u32[]{:S(2)}) copy-start(s32[3,1024]{1,0:T(4,128)} %param.17) | copy-start | bytes 36868
  118.1 44.6 %copy-start.24 = (s32[3]{0:T(128)S(1)}, s32[3]{0:T(128)}, u32[]{:S(2)}) copy-start(s32[3]{0:T(128)} %param.18) | copy-start | bytes 40
  118.1 38.0 %collective-permute-start = (bf16[768,1024]{1,0:T(8,128)(2,1)}, bf16[768,1024]{1,0:T(8,128)(2,1)}, u32[]{:S(2)}, u32[]{:S(2)}) collective-permute-start(bf16[768,1024]{1,0:T(8,128)(2,1)} %get-tuple-element.50.refs_0_.refs_4_), channel_id=1, source_target_pairs={{0,1},{1,2},{2,3},{4,5},{5,6},{6,7},{8,9},{9,10},{10,11},{12,13},{... | collective-permute-start | bytes 4718600 | tf_op jit(solution)/shard_map/ppermute | solution.py:552
  156.1 248.2 %all-gather.13.cloned.1.call-start = ((), (), s32[]{:S(2)}) async-start(), calls=%async_computation.9 | async-start | bytes 25952256 | tf_op jit(solution)/shard_map/all_gather | solution.py:516
  156.2 3.2 collective-permute-start.1
  158.0 41.1 %collective-permute-start.3 = (bf16[768,1024]{1,0:T(8,128)(2,1)}, bf16[768,1024]{1,0:T(8,128)(2,1)S(1)}, u32[]{:S(2)}, u32[]{:S(2)}) collective-permute-start(bf16[768,1024]{1,0:T(8,128)(2,1)} %get-tuple-element.50.refs_0_.refs_4_), channel_id=1, source_target_pairs={{1,0},{2,1},{3,2},{5,4},{6,5},{7,6},{9,8},{10,9},{11,10},{13,12},{... | collective-permute-start | bytes 4718600 | tf_op jit(solution)/shard_map/ppermute | solution.py:556
  159.3 39.8 %collective-permute-start.2 = (bf16[768,1024]{1,0:T(8,128)(2,1)}, bf16[768,1024]{1,0:T(8,128)(2,1)}, u32[]{:S(2)}, u32[]{:S(2)}) collective-permute-start(bf16[768,1024]{1,0:T(8,128)(2,1)} %collective-permute-done.1.refs_2_.refs_6_), channel_id=1, source_target_pairs={{2,3},{6,7},{10,11},{14,15},{18,19},{22,23},{26,27},{30,31}} | collective-permute-start | bytes 4718600 | tf_op jit(solution)/shard_map/ppermute | solution.py:552
  273.8 248.7 %all-gather.15.cloned.1.call-start = ((), (), s32[]{:S(2)}) async-start(), calls=%async_computation.16 | async-start | bytes 25952256 | tf_op jit(solution)/shard_map/all_gather | solution.py:516
  404.3 223.0 %reduce-scatter.7.cloned.1.call-start = ((), (), s32[]{:S(2)}) async-start(), calls=%async_computation.10 | async-start | bytes 14417920 | tf_op jit(solution)/shard_map/reduce_scatter | solution.py:522
  432.6 18.2 %collective-permute-start.6 = (bf16[768,5632]{1,0:T(8,128)(2,1)}, bf16[768,5632]{1,0:T(8,128)(2,1)}, u32[]{:S(2)}, u32[]{:S(2)}) collective-permute-start(bf16[768,5632]{1,0:T(8,128)(2,1)} %get-tuple-element.72.bo_ref.h_ref), channel_id=1, source_target_pairs={{0,4},{4,0},{8,12},{12,8},{16,20},{20,16},{24,28},{28,24},{1,5},{5... | collective-permute-start | bytes 25952264 | tf_op jit(solution)/shard_map/ppermute | solution.py:519
  435.2 15.6 %collective-permute-start.5 = (bf16[768,2048]{1,0:T(8,128)(2,1)}, bf16[768,2048]{1,0:T(8,128)(2,1)S(1)}, u32[]{:S(2)}, u32[]{:S(2)}) collective-permute-start(bf16[768,2048]{1,0:T(8,128)(2,1)} %multiply_convert_fusion.ao_ref.m_ref), channel_id=1, source_target_pairs={{0,4},{4,0},{8,12},{12,8},{16,20},{20,16},{24,28},{28,24},{1,5},{5... | collective-permute-start | bytes 9437192 | tf_op jit(solution)/shard_map/ppermute | solution.py:519
  478.2 254.0 %reduce-scatter.9.cloned.1.call-start = ((), (), s32[]{:S(2)}) async-start(), calls=%async_computation.11 | async-start | bytes 14417920 | tf_op jit(solution)/shard_map/reduce_scatter | solution.py:522
  553.8 46.7 %collective-permute-start.8 = (bf16[768,5632]{1,0:T(8,128)(2,1)}, bf16[768,5632]{1,0:T(8,128)(2,1)}, u32[]{:S(2)}, u32[]{:S(2)}) collective-permute-start(bf16[768,5632]{1,0:T(8,128)(2,1)} %get-tuple-element.63.a_ref.bo_ref), channel_id=1, source_target_pairs={{0,4},{4,0},{8,12},{12,8},{16,20},{20,16},{24,28},{28,24},{1,5},{5... | collective-permute-start | bytes 25952264 | tf_op jit(solution)/shard_map/ppermute | solution.py:519
  554.1 46.4 %collective-permute-start.7 = (bf16[768,2048]{1,0:T(8,128)(2,1)S(1)}, bf16[768,2048]{1,0:T(8,128)(2,1)}, u32[]{:S(2)}, u32[]{:S(2)}) collective-permute-start(bf16[768,2048]{1,0:T(8,128)(2,1)S(1)} %copy-done.19), channel_id=1, source_target_pairs={{0,4},{4,0},{8,12},{12,8},{16,20},{20,16},{24,28},{28,24},{1,5},{5... | collective-permute-start | bytes 9437192 | tf_op jit(solution)/shard_map/ppermute | solution.py:519
  627.4 338.7 %reduce-scatter.11.cloned.1.call-start = ((), (), s32[]{:S(2)}) async-start(), calls=%async_computation.12 | async-start | bytes 14417920 | tf_op jit(solution)/shard_map/reduce_scatter | solution.py:522
  627.4 67.1 %collective-permute-start.10 = (bf16[768,5632]{1,0:T(8,128)(2,1)}, bf16[768,5632]{1,0:T(8,128)(2,1)}, u32[]{:S(2)}, u32[]{:S(2)}) collective-permute-start(bf16[768,5632]{1,0:T(8,128)(2,1)} %get-tuple-element.69.b_ref.bo_ref), channel_id=1, source_target_pairs={{0,4},{4,0},{8,12},{12,8},{16,20},{20,16},{24,28},{28,24},{1,5},{5... | collective-permute-start | bytes 25952264 | tf_op jit(solution)/shard_map/ppermute | solution.py:519
  732.2 387.9 %reduce-scatter.13.cloned.1.call-start = ((), (), s32[]{:S(2)}) async-start(), calls=%async_computation.13 | async-start | bytes 5242880 | tf_op jit(solution)/shard_map/reduce_scatter | solution.py:522
  734.2 35.4 %collective-permute-start.39 = (bf16[128,5632]{1,0:T(8,128)(2,1)S(1)}, bf16[128,5632]{1,0:T(8,128)(2,1)S(1)}, u32[]{:S(2)}, u32[]{:S(2)}) collective-permute-start(bf16[128,5632]{1,0:T(8,128)(2,1)S(1)} %get-tuple-element.111), channel_id=1, source_target_pairs={{0,1},{3,2},{4,5},{7,6},{8,9},{11,10},{12,13},{15,14},{16,17},{19,... | collective-permute-start | bytes 4325384 | tf_op jit(solution)/shard_map/ppermute | solution.py:535
  737.7 61.7 %collective-permute-start.42 = (bf16[128,5632]{1,0:T(8,128)(2,1)S(1)}, bf16[128,5632]{1,0:T(8,128)(2,1)S(1)}, u32[]{:S(2)}, u32[]{:S(2)}) collective-permute-start(bf16[128,5632]{1,0:T(8,128)(2,1)S(1)} %get-tuple-element.112), channel_id=1, source_target_pairs={{0,1},{3,2},{4,5},{7,6},{8,9},{11,10},{12,13},{15,14},{16,17},{19,... | collective-permute-start | bytes 4325384 | tf_op jit(solution)/shard_map/ppermute | solution.py:535
  801.6 3.0 collective-permute-start.40
  802.4 135.0 %collective-permute-start.4 = (bf16[768,2048]{1,0:T(8,128)(2,1)}, bf16[768,2048]{1,0:T(8,128)(2,1)}, u32[]{:S(2)}, u32[]{:S(2)}) collective-permute-start(bf16[768,2048]{1,0:T(8,128)(2,1)} %multiply_convert_fusion.1.x_ref.ao_ref), channel_id=1, source_target_pairs={{0,4},{4,0},{8,12},{12,8},{16,20},{20,16},{24,28},{28,24},{1,5},{5... | collective-permute-start | bytes 9437192 | tf_op jit(solution)/shard_map/ppermute | solution.py:519
  802.5 111.4 %collective-permute-start.9 = (bf16[768,2048]{1,0:T(8,128)(2,1)}, bf16[768,2048]{1,0:T(8,128)(2,1)S(1)}, u32[]{:S(2)}, u32[]{:S(2)}) collective-permute-start(bf16[768,2048]{1,0:T(8,128)(2,1)} %get-tuple-element.51.a_ref.ao_ref), channel_id=1, source_target_pairs={{0,4},{4,0},{8,12},{12,8},{16,20},{20,16},{24,28},{28,24},{1,5},{5... | collective-permute-start | bytes 9437192 | tf_op jit(solution)/shard_map/ppermute | solution.py:519
  803.0 4.8 collective-permute-start.43
  803.7 5.9 collective-permute-start.14
  806.3 67.0 %collective-permute-start.41 = (bf16[128,5632]{1,0:T(8,128)(2,1)S(1)}, bf16[128,5632]{1,0:T(8,128)(2,1)S(1)}, u32[]{:S(2)}, u32[]{:S(2)}) collective-permute-start(bf16[128,5632]{1,0:T(8,128)(2,1)S(1)} %add_convert_fusion.4), channel_id=1, source_target_pairs={{1,0},{2,3},{5,4},{6,7},{9,8},{10,11},{13,12},{14,15},{17,16},{18,... | collective-permute-start | bytes 4325384 | tf_op jit(solution)/shard_map/ppermute | solution.py:538
  808.1 94.7 %collective-permute-start.44 = (bf16[128,5632]{1,0:T(8,128)(2,1)S(1)}, bf16[128,5632]{1,0:T(8,128)(2,1)S(1)}, u32[]{:S(2)}, u32[]{:S(2)}) collective-permute-start(bf16[128,5632]{1,0:T(8,128)(2,1)S(1)} %add_convert_fusion.2), channel_id=1, source_target_pairs={{1,0},{2,3},{5,4},{6,7},{9,8},{10,11},{13,12},{14,15},{17,16},{18,... | collective-permute-start | bytes 4325384 | tf_op jit(solution)/shard_map/ppermute | solution.py:538
  809.6 115.3 %collective-permute-start.11 = (bf16[768,2048]{1,0:T(8,128)(2,1)}, bf16[768,2048]{1,0:T(8,128)(2,1)}, u32[]{:S(2)}, u32[]{:S(2)}) collective-permute-start(bf16[768,2048]{1,0:T(8,128)(2,1)} %get-tuple-element.70.bo_ref), channel_id=1, source_target_pairs={{0,4},{4,0},{8,12},{12,8},{16,20},{20,16},{24,28},{28,24},{1,5},{5... | collective-permute-start | bytes 9437192 | tf_op jit(solution)/shard_map/ppermute | solution.py:519
  873.4 29.6 %collective-permute-start.15 = (bf16[768,1024]{1,0:T(8,128)(2,1)S(1)}, bf16[768,1024]{1,0:T(8,128)(2,1)S(1)}, u32[]{:S(2)}, u32[]{:S(2)}) collective-permute-start(bf16[768,1024]{1,0:T(8,128)(2,1)S(1)} %add_convert_fusion.1), channel_id=1, source_target_pairs={{2,1},{3,2},{6,5},{7,6},{10,9},{11,10},{14,13},{15,14},{18,17},{19... | collective-permute-start | bytes 4718600 | tf_op jit(solution)/shard_map/ppermute | solution.py:567
  874.3 38.8 %copy-start.8 = (bf16[768,1024]{1,0:T(8,128)(2,1)S(1)}, bf16[768,1024]{1,0:T(8,128)(2,1)}, u32[]{:S(2)}) copy-start(bf16[768,1024]{1,0:T(8,128)(2,1)} %get-tuple-element.75) | copy-start | bytes 4718596
  902.8 34.6 %collective-permute-start.12 = (bf16[768,2048]{1,0:T(8,128)(2,1)}, bf16[768,2048]{1,0:T(8,128)(2,1)}, u32[]{:S(2)}, u32[]{:S(2)}) collective-permute-start(bf16[768,2048]{1,0:T(8,128)(2,1)} %get-tuple-element.71.bo_ref.q_ref), channel_id=1, source_target_pairs={{0,4},{4,0},{8,12},{12,8},{16,20},{20,16},{24,28},{28,24},{1,5},{5... | collective-permute-start | bytes 9437192 | tf_op jit(solution)/shard_map/ppermute | solution.py:519
  903.0 46.8 %collective-permute-start.13 = (bf16[768,1024]{1,0:T(8,128)(2,1)}, bf16[768,1024]{1,0:T(8,128)(2,1)S(1)}, u32[]{:S(2)}, u32[]{:S(2)}) collective-permute-start(bf16[768,1024]{1,0:T(8,128)(2,1)} %get-tuple-element.74), channel_id=1, source_target_pairs={{0,1},{1,2},{2,3},{4,5},{5,6},{6,7},{8,9},{9,10},{10,11},{12,13},{... | collective-permute-start | bytes 4718600 | tf_op jit(solution)/shard_map/ppermute | solution.py:563
  913.9 37.2 %collective-permute-start.16 = (bf16[768,1024]{1,0:T(8,128)(2,1)S(1)}, bf16[768,1024]{1,0:T(8,128)(2,1)}, u32[]{:S(2)}, u32[]{:S(2)}) collective-permute-start(bf16[768,1024]{1,0:T(8,128)(2,1)S(1)} %add_convert_fusion), channel_id=1, source_target_pairs={{1,0},{2,1},{3,2},{5,4},{6,5},{7,6},{9,8},{10,9},{11,10},{13,12},{... | collective-permute-start | bytes 4718600 | tf_op jit(solution)/shard_map/ppermute | solution.py:567
  966.0 73.5 %collective-permute-start.17 = (bf16[768,1024]{1,0:T(8,128)(2,1)}, bf16[768,1024]{1,0:T(8,128)(2,1)}, u32[]{:S(2)}, u32[]{:S(2)}) collective-permute-start(bf16[768,1024]{1,0:T(8,128)(2,1)} %pad_maximum_fusion.2.bo_ref.kv_ref), channel_id=1, source_target_pairs={{0,4},{4,0},{8,12},{12,8},{16,20},{20,16},{24,28},{28,24},{1,5},{5... | collective-permute-start | bytes 4718600 | tf_op jit(solution)/shard_map/ppermute | solution.py:519
  966.1 319.1 %reduce-scatter.15.cloned.1.call-start = ((), (), s32[]{:S(2)}) async-start(), calls=%async_computation.14 | async-start | bytes 5242880 | tf_op jit(solution)/shard_map/reduce_scatter | solution.py:522
  969.6 36.4 %collective-permute-start.27 = (bf16[128,5632]{1,0:T(8,128)(2,1)}, bf16[128,5632]{1,0:T(8,128)(2,1)}, u32[]{:S(2)}, u32[]{:S(2)}) collective-permute-start(bf16[128,5632]{1,0:T(8,128)(2,1)} %get-tuple-element.119), channel_id=1, source_target_pairs={{0,1},{3,2},{4,5},{7,6},{8,9},{11,10},{12,13},{15,14},{16,17},{19,... | collective-permute-start | bytes 4325384 | tf_op jit(solution)/shard_map/ppermute | solution.py:535
  974.8 59.9 %collective-permute-start.30 = (bf16[128,5632]{1,0:T(8,128)(2,1)}, bf16[128,5632]{1,0:T(8,128)(2,1)}, u32[]{:S(2)}, u32[]{:S(2)}) collective-permute-start(bf16[128,5632]{1,0:T(8,128)(2,1)} %get-tuple-element.120), channel_id=1, source_target_pairs={{0,1},{3,2},{4,5},{7,6},{8,9},{11,10},{12,13},{15,14},{16,17},{19,... | collective-permute-start | bytes 4325384 | tf_op jit(solution)/shard_map/ppermute | solution.py:535
  1038.8 74.2 %collective-permute-start.28 = (bf16[128,5632]{1,0:T(8,128)(2,1)}, bf16[128,5632]{1,0:T(8,128)(2,1)S(1)}, u32[]{:S(2)}, u32[]{:S(2)}) collective-permute-start(bf16[128,5632]{1,0:T(8,128)(2,1)} %get-tuple-element.117), channel_id=1, source_target_pairs={{1,2},{2,1},{5,6},{6,5},{9,10},{10,9},{13,14},{14,13},{17,18},{18,... | collective-permute-start | bytes 4325384 | tf_op jit(solution)/shard_map/ppermute | solution.py:536
  1048.3 63.9 %copy-start.6 = (bf16[128,5632]{1,0:T(8,128)(2,1)S(1)}, bf16[128,5632]{1,0:T(8,128)(2,1)}, u32[]{:S(2)}) copy-start(bf16[128,5632]{1,0:T(8,128)(2,1)} %get-tuple-element.118) | copy-start | bytes 4325380
  1112.2 4.8 collective-permute-start.31
  1115.7 38.7 %collective-permute-start.29 = (bf16[128,5632]{1,0:T(8,128)(2,1)}, bf16[128,5632]{1,0:T(8,128)(2,1)}, u32[]{:S(2)}, u32[]{:S(2)}) collective-permute-start(bf16[128,5632]{1,0:T(8,128)(2,1)} %add_convert_fusion.12), channel_id=1, source_target_pairs={{1,0},{2,3},{5,4},{6,7},{9,8},{10,11},{13,12},{14,15},{17,16},{18,... | collective-permute-start | bytes 4325384 | tf_op jit(solution)/shard_map/ppermute | solution.py:538
  1118.6 96.0 %collective-permute-start.32 = (bf16[128,5632]{1,0:T(8,128)(2,1)}, bf16[128,5632]{1,0:T(8,128)(2,1)}, u32[]{:S(2)}, u32[]{:S(2)}) collective-permute-start(bf16[128,5632]{1,0:T(8,128)(2,1)} %add_convert_fusion.10), channel_id=1, source_target_pairs={{1,0},{2,3},{5,4},{6,7},{9,8},{10,11},{13,12},{14,15},{17,16},{18,... | collective-permute-start | bytes 4325384 | tf_op jit(solution)/shard_map/ppermute | solution.py:538
  1120.2 216.7 %reduce-scatter.17.cloned.1.call-start = ((), (), s32[]{:S(2)}) async-start(), calls=%async_computation.15 | async-start | bytes 2621440 | tf_op jit(solution)/shard_map/reduce_scatter | solution.py:522
  1120.6 64.4 %collective-permute-start.33 = (bf16[128,5632]{1,0:T(8,128)(2,1)S(1)}, bf16[128,5632]{1,0:T(8,128)(2,1)S(1)}, u32[]{:S(2)}, u32[]{:S(2)}) collective-permute-start(bf16[128,5632]{1,0:T(8,128)(2,1)S(1)} %get-tuple-element.115), channel_id=1, source_target_pairs={{0,1},{3,2},{4,5},{7,6},{8,9},{11,10},{12,13},{15,14},{16,17},{19,... | collective-permute-start | bytes 4325384 | tf_op jit(solution)/shard_map/ppermute | solution.py:535
  1153.0 59.9 %collective-permute-start.36 = (bf16[128,5632]{1,0:T(8,128)(2,1)S(1)}, bf16[128,5632]{1,0:T(8,128)(2,1)S(1)}, u32[]{:S(2)}, u32[]{:S(2)}) collective-permute-start(bf16[128,5632]{1,0:T(8,128)(2,1)S(1)} %get-tuple-element.116), channel_id=1, source_target_pairs={{0,1},{3,2},{4,5},{7,6},{8,9},{11,10},{12,13},{15,14},{16,17},{19,... | collective-permute-start | bytes 4325384 | tf_op jit(solution)/shard_map/ppermute | solution.py:535
  1213.6 6.5 collective-permute-start.34
  1219.4 2.4 collective-permute-start.37
  1220.5 64.7 %collective-permute-start.35 = (bf16[128,5632]{1,0:T(8,128)(2,1)S(1)}, bf16[128,5632]{1,0:T(8,128)(2,1)}, u32[]{:S(2)}, u32[]{:S(2)}) collective-permute-start(bf16[128,5632]{1,0:T(8,128)(2,1)S(1)} %add_convert_fusion.8), channel_id=1, source_target_pairs={{1,0},{2,3},{5,4},{6,7},{9,8},{10,11},{13,12},{14,15},{17,16},{18,... | collective-permute-start | bytes 4325384 | tf_op jit(solution)/shard_map/ppermute | solution.py:538
  1222.1 90.2 %collective-permute-start.38 = (bf16[128,5632]{1,0:T(8,128)(2,1)S(1)}, bf16[128,5632]{1,0:T(8,128)(2,1)}, u32[]{:S(2)}, u32[]{:S(2)}) collective-permute-start(bf16[128,5632]{1,0:T(8,128)(2,1)S(1)} %add_convert_fusion.6), channel_id=1, source_target_pairs={{1,0},{2,3},{5,4},{6,7},{9,8},{10,11},{13,12},{14,15},{17,16},{18,... | collective-permute-start | bytes 4325384 | tf_op jit(solution)/shard_map/ppermute | solution.py:538
  1223.4 80.0 %collective-permute-start.24 = (bf16[256,2048]{1,0:T(8,128)(2,1)}, bf16[256,2048]{1,0:T(8,128)(2,1)}, u32[]{:S(2)}, u32[]{:S(2)}) collective-permute-start(bf16[256,2048]{1,0:T(8,128)(2,1)} %reduce-scatter.13.cloned.1.call-done), channel_id=1, source_target_pairs={{0,1},{3,2},{4,5},{7,6},{8,9},{11,10},{12,13},{15,14},{16,17},{19,... | collective-permute-start | bytes 3145736 | tf_op jit(solution)/shard_map/ppermute | solution.py:535
  1305.3 26.7 %collective-permute-start.25 = (bf16[256,2048]{1,0:T(8,128)(2,1)S(1)}, bf16[256,2048]{1,0:T(8,128)(2,1)S(1)}, u32[]{:S(2)}, u32[]{:S(2)}) collective-permute-start(bf16[256,2048]{1,0:T(8,128)(2,1)S(1)} %add_convert_fusion.15), channel_id=1, source_target_pairs={{1,2},{2,1},{5,6},{6,5},{9,10},{10,9},{13,14},{14,13},{17,18},{18,... | collective-permute-start | bytes 3145736 | tf_op jit(solution)/shard_map/ppermute | solution.py:536
  1306.1 23.9 %collective-permute-start.18 = (bf16[256,2048]{1,0:T(8,128)(2,1)S(1)}, bf16[256,2048]{1,0:T(8,128)(2,1)S(1)}, u32[]{:S(2)}, u32[]{:S(2)}) collective-permute-start(bf16[256,2048]{1,0:T(8,128)(2,1)S(1)} %copy-done.13), channel_id=1, source_target_pairs={{0,1},{3,2},{4,5},{7,6},{8,9},{11,10},{12,13},{15,14},{16,17},{19,... | collective-permute-start | bytes 3145736 | tf_op jit(solution)/shard_map/ppermute | solution.py:535
  1330.3 12.8 collective-permute-start.19
  1332.4 26.4 %collective-permute-start.26 = (bf16[256,2048]{1,0:T(8,128)(2,1)S(1)}, bf16[256,2048]{1,0:T(8,128)(2,1)S(1)}, u32[]{:S(2)}, u32[]{:S(2)}) collective-permute-start(bf16[256,2048]{1,0:T(8,128)(2,1)S(1)} %add_convert_fusion.14), channel_id=1, source_target_pairs={{1,0},{2,3},{5,4},{6,7},{9,8},{10,11},{13,12},{14,15},{17,16},{18,... | collective-permute-start | bytes 3145736 | tf_op jit(solution)/shard_map/ppermute | solution.py:538
  1336.9 13.2 collective-permute-start.21
  1344.8 36.5 %collective-permute-start.20 = (bf16[256,2048]{1,0:T(8,128)(2,1)S(1)}, bf16[256,2048]{1,0:T(8,128)(2,1)S(1)}, u32[]{:S(2)}, u32[]{:S(2)}) collective-permute-start(bf16[256,2048]{1,0:T(8,128)(2,1)S(1)} %add_convert_fusion.16), channel_id=1, source_target_pairs={{1,0},{2,3},{5,4},{6,7},{9,8},{10,11},{13,12},{14,15},{17,16},{18,... | collective-permute-start | bytes 3145736 | tf_op jit(solution)/shard_map/ppermute | solution.py:538
  1350.3 10.0 collective-permute-start.22
  1360.5 28.2 %collective-permute-start.23 = (bf16[256,1024]{1,0:T(8,128)(2,1)S(1)}, bf16[256,1024]{1,0:T(8,128)(2,1)S(1)}, u32[]{:S(2)}, u32[]{:S(2)}) collective-permute-start(bf16[256,1024]{1,0:T(8,128)(2,1)S(1)} %add_convert_fusion.18), channel_id=1, source_target_pairs={{1,0},{2,3},{5,4},{6,7},{9,8},{10,11},{13,12},{14,15},{17,16},{18,... | collective-permute-start | bytes 1572872 | tf_op jit(solution)/shard_map/ppermute | solution.py:538
  (17 other events, 137.3 us)
Sparse Core Ops, SparseCore 0:
  10.5 74.8 all-gather.6
  87.2 54.3 all-gather.8
  156.2 117.4 all-gather.10
  275.5 128.7 all-gather.12
  406.0 116.4 all-gather.14
  524.8 102.5 reduce-scatter.6
  629.7 102.4 reduce-scatter.8
  734.6 102.5 reduce-scatter.10
  966.2 43.6 reduce-scatter.12
  1120.3 71.3 reduce-scatter.14
  1285.3 24.2 reduce-scatter.16

commit v2 on v1

--- a/solution.py
+++ b/solution.py
@@ -38,10 +38,10 @@
     return jax.ShapeDtypeStruct(shape, dtype)
 
 
-def project(normed, weights, cosine, sine):
+def project(normed, weights, start, cosine, sine):
     rows, width = normed.shape
     tile = KVH * HD
-    steps = weights.shape[1] // tile
+    steps = (weights.shape[1] - start) // tile
     q_steps = H * HD // tile
 
     def body(x_ref, w_ref, c_ref, s_ref, q_ref, kv_ref):
@@ -73,7 +73,7 @@
         grid=(steps,),
         in_specs=[
             const_spec((rows, width)),
-            pl.BlockSpec((width, tile), lambda j: (0, j)),
+            pl.BlockSpec((width, tile), lambda j: (0, start // tile + j)),
             const_spec((rows, HD)),
             const_spec((rows, HD)),
         ],
@@ -233,9 +233,8 @@
     )(attended, w_out, x, keep, gain)
 
 
-def gate_matmul(normed, w_gate, tile):
+def gate_matmul(normed, w_gate, hidden, tile):
     rows, width = normed.shape
-    hidden = w_gate.shape[1]
 
     def body(x_ref, w_ref, g_ref):
         g_ref[...] = dot(x_ref[...], w_ref[...]).astype(BF16)
@@ -251,9 +250,9 @@
     )(normed, w_gate)
 
 
-def up_matmul(normed, w_up, gate, tile):
+def up_matmul(normed, w_up, start, gate, tile):
     rows, width = normed.shape
-    hidden = w_up.shape[1]
+    hidden = gate.shape[1]
 
     def body(x_ref, w_ref, g_ref, u_ref, h_ref):
         up = dot(x_ref[...], w_ref[...])
@@ -266,7 +265,7 @@
         grid=(hidden // tile,),
         in_specs=[
             const_spec((rows, width)),
-            pl.BlockSpec((width, tile), lambda j: (0, j)),
+            pl.BlockSpec((width, tile), lambda j: (0, start // tile + j)),
             pl.BlockSpec((rows, tile), lambda j: (0, j)),
         ],
         out_specs=[pl.BlockSpec((rows, tile), lambda j: (0, j))] * 2,
@@ -329,9 +328,9 @@
     )(grad_mlp, w_down, gate, up)
 
 
-def mlp_back(grad_gate, grad_up, w_gate, w_up, tile):
+def mlp_back(grad_gate, grad_up, weights, tile):
     rows, hidden = grad_gate.shape
-    width = w_gate.shape[0]
+    width = weights.shape[0]
 
     def body(a_ref, b_ref, wa_ref, wb_ref, o_ref):
         o_ref[...] = dot(a_ref[...], wa_ref[...], NT) + dot(b_ref[...], wb_ref[...], NT)
@@ -344,13 +343,13 @@
             pl.BlockSpec((rows, hidden), lambda i: (0, 0), pipeline_mode=once),
             pl.BlockSpec((rows, hidden), lambda i: (0, 0), pipeline_mode=once),
             pl.BlockSpec((tile, hidden), lambda i: (i, 0)),
-            pl.BlockSpec((tile, hidden), lambda i: (i, 0)),
+            pl.BlockSpec((tile, hidden), lambda i: (i, 1)),
         ],
         out_specs=pl.BlockSpec((rows, tile), lambda i: (0, i)),
         out_shape=sds((rows, width), F32),
         cost_estimate=cost(4 * rows * width * hidden, 4 * width * hidden + 4 * rows * hidden),
         name="mlp_back",
-    )(grad_gate, grad_up, w_gate, w_up)
+    )(grad_gate, grad_up, weights, weights)
 
 
 def middle_back(grad_normed, middle, cotangent, keep, gain, w_out, tile):
@@ -402,12 +401,12 @@
     )(grad_normed, middle, cotangent, keep, gain, w_out)
 
 
-def input_back(grad_q, grad_kv, weights, x, grad_middle, gain, tile):
+def input_back(grad_q, grad_kv, weights, start, x, grad_middle, gain, tile):
     rows, width = x.shape
     depth_q, depth_kv = grad_q.shape[1], grad_kv.shape[1]
 
-    def body(q_ref, kv_ref, wq_ref, x_ref, m_ref, g_ref, o_ref, gg_ref):
-        grad = dot(q_ref[...], wq_ref[:, :depth_q], NT) + dot(kv_ref[...], wq_ref[:, depth_q:], NT)
+    def body(q_ref, kv_ref, wq_ref, wkv_ref, x_ref, m_ref, g_ref, o_ref, gg_ref):
+        grad = dot(q_ref[...], wq_ref[...], NT) + dot(kv_ref[...], wkv_ref[...], NT)
         xin = x_ref[...].astype(F32)
         inv = lax.rsqrt(jnp.mean(xin * xin, -1, keepdims=True) + EPS)
         unit = xin * inv
@@ -430,7 +429,10 @@
         in_specs=[
             pl.BlockSpec((tile, depth_q), row),
             pl.BlockSpec((tile, depth_kv), row),
-            pl.BlockSpec((width, depth_q + depth_kv), lambda i: (0, 0), pipeline_mode=pl.Buffered(1)),
+            pl.BlockSpec((width, depth_q), lambda i: (0, start // depth_q), pipeline_mode=pl.Buffered(1)),
+            pl.BlockSpec(
+                (width, depth_kv), lambda i: (0, (start + depth_q) // depth_kv), pipeline_mode=pl.Buffered(1)
+            ),
             pl.BlockSpec((tile, width), row),
             pl.BlockSpec((tile, width), row),
             const_spec((1, width)),
@@ -439,16 +441,19 @@
         out_shape=[sds((rows, width), BF16), sds((1, width), F32)],
         cost_estimate=cost(2 * rows * width * (depth_q + depth_kv), 2 * width * (depth_q + depth_kv) + 10 * rows * width),
         name="input_back",
-    )(grad_q, grad_kv, weights, x, grad_middle, gain)
-
-
-def weight_grad(side, chips, a_own, a_pair, b_own, b_pair, tile):
+    )(grad_q, grad_kv, weights, weights, x, grad_middle, gain)
+
+
+def weight_grad(side, chips, a_own, a_pair, b_own, b_pair, tile, total=None, first=0, into=None):
     rows, depth = a_own.shape
     width = b_own.shape[1]
     part = depth // (2 * len(chips))
     out_rows = depth // 2
-
-    def body(side_ref, ao_ref, ap_ref, bo_ref, bp_ref, o_ref, to_ref, tp_ref):
+    held = [] if into is None else [into]
+
+    def body(side_ref, ao_ref, ap_ref, bo_ref, bp_ref, *refs):
+        o_ref, to_ref, tp_ref = refs[len(held) :]
+
         @pl.when(pl.program_id(0) == 0)
         def _():
             for k, chip in enumerate(chips):
@@ -469,14 +474,16 @@
                 pl.BlockSpec((rows, depth), lambda j, _: (0, 0), pipeline_mode=pl.Buffered(1)),
                 pl.BlockSpec((rows, tile), lambda j, _: (0, j)),
                 pl.BlockSpec((rows, tile), lambda j, _: (0, j)),
-            ],
-            out_specs=pl.BlockSpec((out_rows, tile), lambda j, _: (0, j)),
+            ]
+            + [pl.BlockSpec(memory_space=pl.ANY)] * len(held),
+            out_specs=pl.BlockSpec((out_rows, tile), lambda j, _: (0, first + j)),
             scratch_shapes=[pltpu.VMEM((out_rows, rows), BF16)] * 2,
         ),
-        out_shape=sds((out_rows, width), BF16),
+        out_shape=sds((out_rows, width if total is None else total), BF16),
+        input_output_aliases={5: 0} if held else {},
         cost_estimate=cost(4 * rows * out_rows * width, 2 * out_rows * width + 4 * rows * width + 4 * rows * depth),
         name="weight_grad",
-    )(side, a_own, a_pair, b_own, b_pair)
+    )(side, a_own, a_pair, b_own, b_pair, *held)
 
 
 def on_device(
@@ -507,6 +514,7 @@
     pairs = [(i, i ^ 1) for i in range(fsdp)]
     ahead = min(parts - 1, -(-(BLOCK - 1) // local))
     query_width, pair_width = H * HD, KVH * HD
+    hidden_width = w_gate.shape[1]
     tile = 512
 
     def after(v, *others):
@@ -524,27 +532,48 @@
         )
 
     def finish(v):
-        middle = parts // 2
-        if parts % 2:
-            return lax.psum(v, "ulysses")
-
-        def add(a, b):
-            return (a.astype(F32) + b.astype(F32)).astype(BF16)
-
-        for d in range(middle - 1):
-            v = add(v, lax.ppermute(v, "ulysses", [(d, d + 1), (parts - 1 - d, parts - 2 - d)]))
-        v = add(v, lax.ppermute(v, "ulysses", [(middle - 1, middle), (middle, middle - 1)]))
-        for d in range(middle - 1, 0, -1):
-            came = lax.ppermute(v, "ulysses", [(d, d - 1), (parts - 1 - d, parts - d)])
-            v = jnp.where((place == d - 1) | (place == parts - d), came, v)
-        return v
-
-    def finish_in(v, pieces):
-        step = v.shape[0] // pieces
-        return jnp.concatenate([finish(v[i * step : (i + 1) * step]) for i in range(pieces)], 0)
-
-    def grad_of(a, a_pair, b, b_pair):
-        return weight_grad(side, ring, a, a_pair, b, b_pair, tile)
+        return lax.psum(v, "ulysses")
+
+    middle_part = parts // 2
+    hops = [
+        ([(d, d + 1), (parts - 1 - d, parts - 2 - d)], None) for d in range(middle_part - 1)
+    ]
+    hops.append(([(middle_part - 1, middle_part), (middle_part, middle_part - 1)], None))
+    hops += [
+        ([(d, d - 1), (parts - 1 - d, parts - d)], (place == d - 1) | (place == parts - d))
+        for d in range(middle_part - 1, 0, -1)
+    ]
+    under_way = []
+
+    def add(a, b):
+        return (a.astype(F32) + b.astype(F32)).astype(BF16)
+
+    def tick(new, *gates):
+        for chunk in under_way:
+            came, takes = chunk["came"], hops[chunk["hop"] - 1][1]
+            chunk["v"] = add(chunk["v"], came) if takes is None else jnp.where(takes, came, chunk["v"])
+        for out, k, v in new:
+            under_way.append({"out": out, "k": k, "v": v, "hop": 0})
+        held = lax.optimization_barrier(tuple(c["v"] for c in under_way) + gates)
+        for chunk, v in zip(list(under_way), held):
+            chunk["v"] = v
+            if chunk["hop"] == len(hops):
+                chunk["out"][chunk["k"]] = v
+                under_way.remove(chunk)
+            else:
+                chunk["came"] = lax.ppermute(v, "ulysses", hops[chunk["hop"]][0])
+                chunk["hop"] += 1
+        return held[0]
+
+    def chunks(v, count):
+        out, step = {}, v.shape[0] // count
+        return out, [(out, k, v[k * step : (k + 1) * step]) for k in range(count)]
+
+    def joined(out):
+        return jnp.concatenate([out[k] for k in range(len(out))], 0)
+
+    def grad_of(*operands, **where):
+        return weight_grad(side, ring, *operands, tile, **where)
 
     def spread(v):
         ups, held = [], v
@@ -559,23 +588,26 @@
 
     def collect(slots):
         total = slots[0].astype(F32)
-        for i in range(1, ahead + 1):
-            up = lax.ppermute(slots[parts - i], "ulysses", [(z, z + i) for z in range(parts - i)])
-            total = total + up.astype(F32)
+        ups = [
+            lax.ppermute(slots[parts - i], "ulysses", [(z, z + i) for z in range(parts - i)])
+            for i in range(1, ahead + 1)
+        ]
         held = slots[parts - 1]
         for r in range(parts - 1, 0, -1):
             came = lax.ppermute(held, "ulysses", [(i, i - 1) for i in range(r, parts)])
             if r > 1:
-                held = (slots[r - 1].astype(F32) + came.astype(F32)).astype(BF16)
+                held = yield add(slots[r - 1], came)
             else:
-                total = total + came.astype(F32)
-        return total
+                for up in ups:
+                    total = total + up.astype(F32)
+                yield total + came.astype(F32)
 
     gains = lax.all_gather(jnp.stack([attn_gain, mlp_gain]), "fsdp", axis=1, tiled=True).astype(F32)
     gain_one, gain_two = gains[0:1], gains[1:2]
-    qkv_full = gather(jnp.concatenate([w_query, w_key, w_value], 1))
-    out_full = gather(after(w_out, qkv_full))
-
+    att_full = gather(jnp.concatenate([w_out, w_query, w_key, w_value], 1))
+    mlp_full = gather(after(jnp.concatenate([w_gate, w_up], 1), att_full))
+
+    first_sum = finish(w_key)
     x = layer_input.reshape(rows, width)
     xf = x.astype(F32)
     inv_one = lax.rsqrt(jnp.mean(xf * xf, -1, keepdims=True) + EPS)
@@ -595,81 +627,98 @@
     order = lax.rem(place - jnp.arange(parts) + parts, parts)
     block_keys = jnp.take(by_part, order, 1).reshape(seqs, parts * local, 1)
 
-    query, kv = project(normed_one, qkv_full, cosine, sine)
+    query, kv = project(normed_one, att_full, width, cosine, sine)
     slots = spread(kv)
-    gate_full = gather(after(w_gate, out_full, slots[1]))
     one_pair, mlp_pair = swap(normed_one), swap(grad_mlp)
     attended, lse = attend(query, slots, block_keys, block_mine, seqs)
-    middle, normed_two = out_project(attended, out_full, x, keep, gain_two, local)
-    up_full = gather(after(w_up, gate_full, normed_two))
-    gate = gate_matmul(normed_two, gate_full, tile)
-    down_full = gather(after(w_down, up_full, gate), False)
+    middle, normed_two = out_project(attended, att_full, x, keep, gain_two, local)
+    gate = gate_matmul(normed_two, mlp_full, hidden_width, tile)
+    down_full = gather(after(w_down, mlp_full, normed_two), False)
     two_pair, att_pair = swap(normed_two), swap(attended)
-    up, hidden = up_matmul(normed_two, up_full, gate, tile)
+    up, hidden = up_matmul(normed_two, mlp_full, hidden_width, gate, tile)
 
     hidden_pair = swap(hidden)
     down_part = grad_of(grad_mlp, mlp_pair, hidden, hidden_pair)
     down_sum = scatter(down_part)
     grad_gate, grad_up = hidden_back(after(grad_mlp, down_part), down_full, gate, up, tile)
     gate_pair, up_pair = swap(grad_gate), swap(grad_up)
-    grad_normed_two = mlp_back(grad_gate, grad_up, gate_full, up_full, 256)
+    grad_normed_two = mlp_back(grad_gate, grad_up, mlp_full, 256)
     gate_part = grad_of(normed_two, two_pair, after(grad_gate, grad_normed_two), gate_pair)
     gate_sum = scatter(after(gate_part, down_sum))
+    down_all = finish(after(down_sum, gate_part, first_sum))
     grad_middle, grad_branch, grad_attended, grad_gain_two = middle_back(
-        after(grad_normed_two, gate_part), middle, cot, keep, gain_two, out_full, local
+        after(grad_normed_two, gate_part), middle, cot, keep, gain_two, att_full, local
     )
     branch_pair = swap(grad_branch)
     grad_query, *grad_slots = attend_back(
         query, slots, block_keys, block_mine, lse, grad_attended, cosine, sine, seqs
     )
     query_pair = swap(grad_query)
+    collecting = collect(grad_slots)
+    kv_held = next(collecting)
     up_part = grad_of(normed_two, two_pair, after(grad_up, grad_query), up_pair)
     up_sum = scatter(after(up_part, gate_sum))
-    out_part = grad_of(attended, att_pair, after(grad_branch, up_part), branch_pair)
-    out_sum = scatter(after(out_part, up_sum))
-    query_part = grad_of(normed_one, one_pair, after(grad_query, out_part), query_pair)
-    query_sum = scatter(after(query_part, out_sum))
-    output = down_matmul(after(hidden, query_part), down_full, middle, keep)
-
-    grad_kv = collect(grad_slots)
+    columns = query_width + width
+    att_part = grad_of(
+        attended, att_pair, after(grad_branch, up_part, gate_sum), branch_pair, total=columns, first=query_width // tile
+    )
+    gate_all = finish(after(gate_sum, up_part, down_all))
+    att_part = grad_of(
+        normed_one, one_pair, after(grad_query, down_all, kv_held), query_pair, total=columns, into=att_part
+    )
+    for _ in range(parts - 3):
+        kv_held = collecting.send(kv_held)
+    att_sum = scatter(after(att_part, up_sum))
+    up_all, fresh = chunks(up_sum, 2)
+    token = tick(fresh[:1], att_part, kv_held, gate_all)
+    grad_kv = collecting.send(after(kv_held, token))
+    output = down_matmul(after(hidden, token), down_full, middle, keep)
+    token = tick(fresh[1:], output)
+    grad_kv = after(grad_kv, token)
+    out_down = after(down_all, token).astype(F32).T
     grad_key = grad_kv[:, :pair_width].reshape(rows, KVH, HD)
     turned = grad_key * sine[:, None, :]
     turned = jnp.concatenate([turned[..., half:], turned[..., :half]], -1)
     grad_key = (grad_key * cosine[:, None, :] + turned).reshape(rows, pair_width)
     grad_kv = jnp.concatenate([grad_key, grad_kv[:, pair_width:]], 1).astype(BF16)
     kv_pair = swap(grad_kv)
-    kv_part = grad_of(normed_one, one_pair, grad_kv, kv_pair)
-    kv_sum = scatter(after(kv_part, query_sum))
+    kv_part = grad_of(normed_one, one_pair, after(grad_kv, token), kv_pair)
     grad_input, grad_gain_one = input_back(
-        grad_query, after(grad_kv, kv_part), qkv_full, x, grad_middle, gain_one, local
+        grad_query, after(grad_kv, kv_part, out_down), att_full, width, x, grad_middle, gain_one, local
     )
-
-    gain_sums = lax.psum(jnp.concatenate([grad_gain_one, grad_gain_two], 0), ("fsdp", "ulysses"))
-    own = width // fsdp
-    gain_shard = lax.dynamic_slice_in_dim(gain_sums, lax.axis_index("fsdp") * own, own, 1)
-    out_down, out_gate, out_up, out_out, out_query, out_kv = (
-        finish_in(v, pieces).astype(F32)
-        for v, pieces in (
-            (down_sum, 2),
-            (gate_sum, 2),
-            (up_sum, 2),
-            (out_sum, 1),
-            (query_sum, 1),
-            (kv_sum, 1),
-        )
-    )
+    gain_grads = jnp.concatenate([grad_gain_one, grad_gain_two], 0)
+    gain_grads = (gain_grads + swap(gain_grads)).reshape(2, chips, 2, width // fsdp)
+    gain_grads = lax.dynamic_index_in_dim(gain_grads, side[0], 2, False)
+    gain_grads = jnp.stack([gain_grads[:, chip] for chip in ring], 1).reshape(2, width // 2)
+    gain_part = jnp.pad(gain_grads.T, ((0, 0), (0, HD - 2))).astype(BF16)
+    kv_sum = scatter(after(jnp.concatenate([kv_part, gain_part], 1), att_sum))
+    att_all, fresh = chunks(att_sum, 2)
+    token = tick(fresh[:1], grad_input)
+    out_gate = after(gate_all, token).astype(F32)
+    token = tick(fresh[1:], out_gate)
+    kv_sums, fresh = chunks(kv_sum, 1)
+    token = tick(fresh)
+    while under_way:
+        token = tick([])
+    out_up = joined(up_all).astype(F32)
+    att_all, kv_sums = joined(att_all), joined(kv_sums)
+    out_query = att_all[:, :query_width].astype(F32)
+    out_out = att_all[:, query_width:].astype(F32)
+    out_key = kv_sums[:, :pair_width].astype(F32)
+    out_value = kv_sums[:, pair_width : 2 * pair_width].astype(F32)
+    out_gains = kv_sums[:, 2 * pair_width : 2 * pair_width + 2].astype(F32).T + 0.0 * first_sum[0, 0].astype(F32)
     return (
         output.reshape(layer_input.shape),
         grad_input.reshape(layer_input.shape),
-        gain_shard[0],
+        out_gains[0],
         out_query,
-        out_kv[:, :pair_width],
-        out_kv[:, pair_width:],
+        out_key,
+        out_value,
         out_out,
-        gain_shard[1],
+        out_gains[1],
         out_gate,
         out_up,
-        out_down.T,
+        out_down,
     )
 
 

time: 1400 us -> 1160 us (0.83)
  starting transfers between devices: 166 us -> 60.7 us
  waiting for transfers between devices: 654 us -> 551 us
  blocking collectives: 51.7 us -> 8.85 us
    ppermute x27 -> x15, waiting for transfers between devices: 311 us -> 145 us  [tick(): chunk['came'] = lax.ppermute(v, 'ulysses', hops[chunk['hop']][0])]
    ppermute x27 -> x15, starting transfers between devices: 141 us -> 39.7 us  [tick(): chunk['came'] = lax.ppermute(v, 'ulysses', hops[chunk['hop']][0])]
    all_gather x5 -> x3, waiting for transfers between devices: 246 us -> 166 us  [gather(): return lax.all_gather(v, 'fsdp', axis=0, tiled=tiled)]
    psum x0 -> x3, waiting for transfers between devices: none -> 69.6 us  [finish(): return lax.psum(v, 'ulysses')]
    reduce_scatter x6 -> x5, waiting for transfers between devices: 14.2 us -> 77 us  [scatter(): lax.psum_scatter(v, 'fsdp', scatter_dimension=0, tiled=True, axis_index_g...]
    psum x1 -> x0, blocking collectives: 42.8 us -> none  [on_device(): lax.psum(jnp.concatenate([grad_gain_one, grad_gain_two], 0), ('fsdp', 'ul...]
  transfers between devices with their start and end apart: 56 -> 45, of which waited for: 24 -> 22; matrix products, arithmetic and copies ran while one was open for 6% -> 7% of each run, Pallas kernels for 30% -> 37%
where the time goes in v2:
time: 1160 us; the launch traced here: 1150 us
  waiting for transfers between devices  551 us (48%)
  Pallas kernels  422 us (36%)
  other arithmetic  67.4 us (6%)
  starting transfers between devices  60.7 us (5%)
  local copies, waits for them, and re-layouts  26 us (2%)
  between operations  17.4 us (1%)
    all_gather x3, waiting for transfers between devices, gather(): return lax.all_gather(v, 'fsdp', axis=0, tiled=tiled)  166 us
    ppermute x15, waiting for transfers between devices, tick(): chunk['came'] = lax.ppermute(v, 'ulysses', hops[chunk['hop']][0])  145 us
    pallas_call x6, Pallas kernels, weight_grad(): pl.pallas_call(body, grid_spec=pltpu.PrefetchScalarGridSpec(num_scalar_pr...  110 us
    reduce_scatter x5, waiting for transfers between devices, scatter(): lax.psum_scatter(v, 'fsdp', scatter_dimension=0, tiled=True, axis_index_g...  77 us
    psum x3, waiting for transfers between devices, finish(): return lax.psum(v, 'ulysses')  69.6 us
    pallas_call x1, Pallas kernels, attend_back(): pl.pallas_call(body, grid=(seqs, KVH), in_specs=[pl.BlockSpec((local, GRO...  48.7 us
    pallas_call x1, Pallas kernels, mlp_back(): pl.pallas_call(body, grid=(width // tile,), in_specs=[pl.BlockSpec((rows,...  46.2 us
    ppermute x15, starting transfers between devices, tick(): chunk['came'] = lax.ppermute(v, 'ulysses', hops[chunk['hop']][0])  39.7 us
  transfers between devices with their start and end apart: 45, of which 22 were waited for; matrix products, arithmetic and copies ran while one was open for 7% of the time, Pallas kernels for 37%

profile of v2, /device:TPU:0, one launch (start us, length us, event | category | flops | bytes accessed | tf_op | source)
XLA Modules:
  0.0 1153.0 jit_solution(2365966462508177095)
XLA Ops:
  8.1 3.1 pad_maximum_fusion.1
  11.2 5.1 pad_maximum_fusion
  16.4 105.3 %all-gather.5.cloned.1.call-done.w_ref.wq_ref.wkv_ref = bf16[2048,5120]{1,0:T(8,128)(2,1)} async-done(((bf16[256,5120]{1,0:T(8,128)(2,1)}), bf16[2048,5120]{1,0:T(8,128)(2,1)}) %all-gather.5.cloned.1.call-update) | async-done | bytes 20971536 | tf_op jit(solution)/shard_map/all_gather | solution.py:524
  122.5 8.8 all_gather.15
  134.6 2.6 multiply_convert_fusion.1.x_ref.ao_ref
  137.2 18.2 %project.1 = (bf16[768,2048]{1,0:T(8,128)(2,1)}, bf16[768,1024]{1,0:T(8,128)(2,1)}) custom-call(bf16[768,2048]{1,0:T(8,128)(2,1)} %multiply_convert_fusion.1.x_ref.ao_ref, bf16[2048,5120]{1,0:T(8,128)(2,1)} %all-gather.5.cloned.1.call-done.w_ref.wq_ref.wkv_ref, f32[768,128]{1,0:T(8,128)} %get-tuple-element.174.c_ref.refs_12_, ...), custom_call_target="tpu_custom_call" | custom-call | flops 9663676416 | bytes 18874368 | tf_op jit(solution)/shard_map/project/pallas_call | solution.py:71
  155.5 3.5 collective-permute-start
  158.9 34.4 %collective-permute-done.refs_1_.refs_5_ = bf16[768,1024]{1,0:T(8,128)(2,1)S(1)} collective-permute-done((bf16[768,1024]{1,0:T(8,128)(2,1)}, bf16[768,1024]{1,0:T(8,128)(2,1)S(1)}, u32[]{:S(2)}, u32[]{:S(2)}) %collective-permute-start) | collective-permute-done | bytes 1572896 | tf_op jit(solution)/shard_map/ppermute | solution.py:581
  197.6 2.0 collective-permute-start.2
  203.9 33.6 %collective-permute-done.3 = bf16[768,1024]{1,0:T(8,128)(2,1)S(1)} collective-permute-done((bf16[768,1024]{1,0:T(8,128)(2,1)}, bf16[768,1024]{1,0:T(8,128)(2,1)S(1)}, u32[]{:S(2)}, u32[]{:S(2)}) %collective-permute-start.3) | collective-permute-done | bytes 1572896 | tf_op jit(solution)/shard_map/ppermute | solution.py:585
  238.8 39.0 %attend.1 = (bf16[768,2048]{1,0:T(8,128)(2,1)}, f32[3,4,4,256]{3,2,1,0:T(4,128)}) custom-call(bf16[768,2048]{1,0:T(8,128)(2,1)} %get-tuple-element.72.q_ref, bf16[768,1024]{1,0:T(8,128)(2,1)} %get-tuple-element.73.refs_0_.refs_4_, bf16[768,1024]{1,0:T(8,128)(2,1)} %copy-done.24, bf16[768,1024]{1,0:T(8,128)(2,1)} %collective-permute-done.1.refs_2_.refs_6_, ...), custom_call_target="tpu_custom_call" | custom-call | flops 12884901888 | bytes 6291456 | tf_op jit(solution)/shard_map/attend/pallas_call | solution.py:121
  277.8 13.6 %out_project.1 = (f32[768,2048]{1,0:T(8,128)}, bf16[768,2048]{1,0:T(8,128)(2,1)}) custom-call(bf16[768,2048]{1,0:T(8,128)(2,1)} %get-tuple-element.74.a_ref.ao_ref, bf16[2048,5120]{1,0:T(8,128)(2,1)} %all-gather.5.cloned.1.call-done.w_ref.wq_ref.wkv_ref, bf16[768,2048]{1,0:T(8,128)(2,1)} %bitcast.41, f32[768,1]{1,0:T(8,128)} %bitcast.46, ...), custom_call_target="tpu_custom_call" | custom-call | flops 6442450944 | bytes 24117248 | tf_op jit(solution)/shard_map/out_project/pallas_call | solution.py:219
  291.5 47.4 %all-gather.7.cloned.1.call-done.w_ref.wa_ref.wb_ref = bf16[2048,11264]{1,0:T(8,128)(2,1)} async-done(((bf16[256,11264]{1,0:T(8,128)(2,1)}), bf16[2048,11264]{1,0:T(8,128)(2,1)}) %all-gather.7.cloned.1.call-update) | async-done | bytes 46137360 | tf_op jit(solution)/shard_map/all_gather | solution.py:524
  338.9 24.4 %gate_matmul.1.g_ref = bf16[768,5632]{1,0:T(8,128)(2,1)} custom-call(bf16[768,2048]{1,0:T(8,128)(2,1)} %get-tuple-element.75.x_ref.ao_ref, bf16[2048,11264]{1,0:T(8,128)(2,1)} %all-gather.7.cloned.1.call-done.w_ref.wa_ref.wb_ref), custom_call_target="tpu_custom_call" | custom-call | flops 17716740096 | bytes 31719424 | tf_op jit(solution)/shard_map/gate_matmul/pallas_call | solution.py:242
  363.3 27.6 %up_matmul.1 = (bf16[768,5632]{1,0:T(8,128)(2,1)}, bf16[768,5632]{1,0:T(8,128)(2,1)}) custom-call(bf16[768,2048]{1,0:T(8,128)(2,1)} %get-tuple-element.75.x_ref.ao_ref, bf16[2048,11264]{1,0:T(8,128)(2,1)} %all-gather.7.cloned.1.call-done.w_ref.wa_ref.wb_ref, bf16[768,5632]{1,0:T(8,128)(2,1)} %gate_matmul.1.g_ref), custom_call_target="tpu_custom_call" | custom-call | flops 17716740096 | bytes 49020928 | tf_op jit(solution)/shard_map/up_matmul/pallas_call | solution.py:263
  391.2 2.7 multiply_convert_fusion.ao_ref.m_ref
  394.1 14.6 %collective-permute-done.5.ap_ref = bf16[768,2048]{1,0:T(8,128)(2,1)S(1)} collective-permute-done((bf16[768,2048]{1,0:T(8,128)(2,1)}, bf16[768,2048]{1,0:T(8,128)(2,1)S(1)}, u32[]{:S(2)}, u32[]{:S(2)}) %collective-permute-start.5) | collective-permute-done | bytes 3145760 | tf_op jit(solution)/shard_map/ppermute | solution.py:527
  408.8 9.2 collective-permute-done.6.bp_ref
  418.0 25.2 %weight_grad.6 = bf16[1024,5632]{1,0:T(8,128)(2,1)} custom-call(s32[1]{0:T(128)} %bitcast.6.side_ref, bf16[768,2048]{1,0:T(8,128)(2,1)} %multiply_convert_fusion.ao_ref.m_ref, bf16[768,2048]{1,0:T(8,128)(2,1)} %copy-done.23, bf16[768,5632]{1,0:T(8,128)(2,1)} %get-tuple-element.101.bo_ref.h_ref, bf16[768,5632]{1,0:T(8,128)(2,1)} %collective-permute-done.6.bp_ref), custom_call_target="tpu_custom_call" | custom-call | flops 17716740096 | bytes 35127296 | tf_op jit(solution)/shard_map/weight_grad/pallas_call | solution.py:467
  443.5 13.7 %all-gather.9.cloned.1.call-done = bf16[45056,256]{1,0:T(8,128)(2,1)} async-done(((bf16[5632,256]{1,0:T(8,128)(2,1)}), bf16[45056,256]{1,0:T(8,128)(2,1)}) %all-gather.9.cloned.1.call-update) | async-done | bytes 23068688 | tf_op jit(solution)/shard_map/all_gather | solution.py:524
  457.2 31.4 %hidden_back.1 = (bf16[768,5632]{1,0:T(8,128)(2,1)}, bf16[768,5632]{1,0:T(8,128)(2,1)}) custom-call(bf16[768,2048]{1,0:T(8,128)(2,1)} %multiply_convert_fusion.ao_ref.m_ref, bf16[8,5632,256]{2,1,0:T(8,128)(2,1)} %bitcast.56, bf16[768,5632]{1,0:T(8,128)(2,1)} %gate_matmul.1.g_ref, bf16[768,5632]{1,0:T(8,128)(2,1)} %get-tuple-element.80.u_ref), custom_call_target="tpu_custom_call" | custom-call | flops 17716740096 | bytes 57671680 | tf_op jit(solution)/shard_map/hidden_back/pallas_call | solution.py:315
  489.3 46.2 %mlp_back.1.n_ref = f32[768,2048]{1,0:T(8,128)} custom-call(bf16[768,5632]{1,0:T(8,128)(2,1)} %get-tuple-element.84.a_ref.bo_ref, bf16[768,5632]{1,0:T(8,128)(2,1)} %get-tuple-element.89.b_ref.bo_ref, bf16[2048,11264]{1,0:T(8,128)(2,1)} %all-gather.7.cloned.1.call-done.w_ref.wa_ref.wb_ref, bf16[2048,11264]{1,0:T(8,128)(2,1)} %all-gather.7.cloned.1.call-done.w_ref.wa_ref.wb_ref), custom_call_target="tpu_custom_call" | custom-call | flops 35433480192 | bytes 63438848 | tf_op jit(solution)/shard_map/mlp_back/pallas_call | solution.py:339
  535.5 25.2 %weight_grad.7 = bf16[1024,5632]{1,0:T(8,128)(2,1)} custom-call(s32[1]{0:T(128)} %bitcast.6.side_ref, bf16[768,2048]{1,0:T(8,128)(2,1)} %get-tuple-element.75.x_ref.ao_ref, bf16[768,2048]{1,0:T(8,128)(2,1)} %collective-permute-done.4.ap_ref, bf16[768,5632]{1,0:T(8,128)(2,1)} %get-tuple-element.84.a_ref.bo_ref, bf16[768,5632]{1,0:T(8,128)(2,1)} %collective-permute-done.7.bp_ref), custom_call_target="tpu_custom_call" | custom-call | flops 17716740096 | bytes 35127296 | tf_op jit(solution)/shard_map/weight_grad/pallas_call | solution.py:467
  562.9 18.5 %middle_back.1 = (f32[768,2048]{1,0:T(8,128)}, bf16[768,2048]{1,0:T(8,128)(2,1)}, bf16[768,2048]{1,0:T(8,128)(2,1)}, f32[1,2048]{1,0:T(1,128)}) custom-call(f32[768,2048]{1,0:T(8,128)} %mlp_back.1.n_ref, f32[768,2048]{1,0:T(8,128)} %get-tuple-element.86.m_ref, bf16[768,2048]{1,0:T(8,128)(2,1)} %bitcast.43, f32[768,1]{1,0:T(8,128)} %bitcast.47, ...), custom_call_target="tpu_custom_call" | custom-call | flops 6442450944 | bytes 36700160 | tf_op jit(solution)/shard_map/middle_back/pallas_call | solution.py:381
  581.4 48.7 %attend_back.1 = (bf16[768,2048]{1,0:T(8,128)(2,1)}, bf16[768,1024]{1,0:T(8,128)(2,1)}, bf16[768,1024]{1,0:T(8,128)(2,1)}, bf16[768,1024]{1,0:T(8,128)(2,1)}, bf16[768,1024]{1,0:T(8,128)(2,1)}) custom-call(bf16[768,2048]{1,0:T(8,128)(2,1)} %get-tuple-element.72.q_ref, bf16[768,1024]{1,0:T(8,128)(2,1)} %get-tuple-element.73.refs_0_.refs_4_, ...), custom_call_target="tpu_custom_call" | custom-call | flops 32212254720 | bytes 12582912 | tf_op jit(solution)/shard_map/attend_back/pallas_call | solution.py:186
  630.1 25.3 %weight_grad.8 = bf16[1024,5632]{1,0:T(8,128)(2,1)} custom-call(s32[1]{0:T(128)} %bitcast.6.side_ref, bf16[768,2048]{1,0:T(8,128)(2,1)} %get-tuple-element.75.x_ref.ao_ref, bf16[768,2048]{1,0:T(8,128)(2,1)} %collective-permute-done.4.ap_ref, bf16[768,5632]{1,0:T(8,128)(2,1)} %get-tuple-element.89.b_ref.bo_ref, bf16[768,5632]{1,0:T(8,128)(2,1)} %collective-permute-done.8.bp_ref), custom_call_target="tpu_custom_call" | custom-call | flops 17716740096 | bytes 35127296 | tf_op jit(solution)/shard_map/weight_grad/pallas_call | solution.py:467
  655.4 11.3 reduce-scatter.8.cloned.1.call-done
  670.4 6.9 all-reduce.7.cloned.1.call-done
  677.9 3.7 add_convert_fusion.1
  681.9 12.7 %weight_grad.9.refs_0_ = bf16[1024,4096]{1,0:T(8,128)(2,1)} custom-call(s32[1]{0:T(128)} %bitcast.6.side_ref, bf16[768,2048]{1,0:T(8,128)(2,1)} %get-tuple-element.74.a_ref.ao_ref, bf16[768,2048]{1,0:T(8,128)(2,1)} %collective-permute-done.12.ap_ref, bf16[768,2048]{1,0:T(8,128)(2,1)} %get-tuple-element.97.bo_ref, ...), custom_call_target="tpu_custom_call" | custom-call | flops 6442450944 | bytes 16777216 | tf_op jit(solution)/shard_map/weight_grad/pallas_call | solution.py:467
  694.5 12.6 %weight_grad.10 = bf16[1024,4096]{1,0:T(8,128)(2,1)} custom-call(s32[1]{0:T(128)} %bitcast.6.side_ref, bf16[768,2048]{1,0:T(8,128)(2,1)} %multiply_convert_fusion.1.x_ref.ao_ref, bf16[768,2048]{1,0:T(8,128)(2,1)} %collective-permute-done.9.ap_ref, bf16[768,2048]{1,0:T(8,128)(2,1)} %get-tuple-element.95.bo_ref.q_ref, ...), custom_call_target="tpu_custom_call", output_to_operand_aliasing={{}: (5, {})} | custom-call | flops 6442450944 | bytes 16777216 | tf_op jit(solution)/shard_map/weight_grad/pallas_call | solution.py:467
  707.1 64.3 %reduce-scatter.10.cloned.1.call-done = bf16[256,5632]{1,0:T(8,128)(2,1)} async-done(((bf16[1024,5632]{1,0:T(8,128)(2,1)}), bf16[256,5632]{1,0:T(8,128)(2,1)}) %reduce-scatter.10.cloned.1.call-update) | async-done | bytes 2883600 | tf_op jit(solution)/shard_map/reduce_scatter | solution.py:530
  773.4 4.0 collective-permute-start.15
  777.4 2.2 add_convert_fusion
  781.1 62.6 %all-reduce.9.cloned.1.call-done = bf16[256,5632]{1,0:T(8,128)(2,1)} async-done(((bf16[256,5632]{1,0:T(8,128)(2,1)}), bf16[256,5632]{1,0:T(8,128)(2,1)}) %all-reduce.9.cloned.1.call-update) | async-done | bytes 2883600 | tf_op jit(solution)/shard_map/psum | solution.py:535
  843.7 10.7 collective-permute-start.17
  855.7 24.9 %down_matmul.1 = bf16[768,2048]{1,0:T(8,128)(2,1)} custom-call(bf16[768,5632]{1,0:T(8,128)(2,1)} %get-tuple-element.101.bo_ref.h_ref, bf16[8,5632,256]{2,1,0:T(8,128)(2,1)} %bitcast.57, f32[768,2048]{1,0:T(8,128)} %get-tuple-element.86.m_ref, f32[768,1]{1,0:T(8,128)} %bitcast.48), custom_call_target="tpu_custom_call" | custom-call | flops 17716740096 | bytes 31719424 | tf_op jit(solution)/shard_map/down_matmul/pallas_call | solution.py:285
  880.6 3.7 collective-permute-done.17
  884.3 2.8 add_convert_fusion.5
  887.1 1.9 collective-permute-start.19
  889.1 6.2 collective-permute-start.20
  895.3 3.2 convert_bitcast_fusion
  898.5 2.9 convert_add_fusion
  903.8 2.7 reshape.170
  912.0 12.2 %collective-permute-done.20 = bf16[128,5632]{1,0:T(8,128)(2,1)} collective-permute-done((bf16[128,5632]{1,0:T(8,128)(2,1)}, bf16[128,5632]{1,0:T(8,128)(2,1)}, u32[]{:S(2)}, u32[]{:S(2)}) %collective-permute-start.20) | collective-permute-done | bytes 1441824 | tf_op jit(solution)/shard_map/ppermute | solution.py:564
  924.2 2.1 add_convert_fusion.3
  926.3 2.1 add_convert_fusion.4
  928.5 8.8 weight_grad.11
  937.3 19.6 %input_back.1 = (bf16[768,2048]{1,0:T(8,128)(2,1)}, f32[1,2048]{1,0:T(1,128)}) custom-call(bf16[768,2048]{1,0:T(8,128)(2,1)} %get-tuple-element.95.bo_ref.q_ref, bf16[768,1024]{1,0:T(8,128)(2,1)} %copy-done.3, bf16[2048,5120]{1,0:T(8,128)(2,1)} %all-gather.5.cloned.1.call-done.w_ref.wq_ref.wkv_ref, ...), custom_call_target="tpu_custom_call" | custom-call | flops 9663676416 | bytes 28311552 | tf_op jit(solution)/shard_map/input_back/pallas_call | solution.py:426
  957.8 3.1 fusion.10
  960.9 5.6 collective-permute-start.23
  968.6 3.2 fusion.1
  973.1 5.0 convert_element_type.212
  978.2 10.7 collective-permute-done.23
  992.4 35.4 %collective-permute-done.21 = bf16[128,5632]{1,0:T(8,128)(2,1)S(1)} collective-permute-done((bf16[128,5632]{1,0:T(8,128)(2,1)S(1)}, bf16[128,5632]{1,0:T(8,128)(2,1)S(1)}, u32[]{:S(2)}, u32[]{:S(2)}) %collective-permute-start.21) | collective-permute-done | bytes 1441824 | tf_op jit(solution)/shard_map/ppermute | solution.py:564
  1031.5 20.3 %collective-permute-done.26 = bf16[128,4096]{1,0:T(8,128)(2,1)S(1)} collective-permute-done((bf16[128,4096]{1,0:T(8,128)(2,1)S(1)}, bf16[128,4096]{1,0:T(8,128)(2,1)S(1)}, u32[]{:S(2)}, u32[]{:S(2)}) %collective-permute-start.26) | collective-permute-done | bytes 1048608 | tf_op jit(solution)/shard_map/ppermute | solution.py:564
  1054.2 12.4 %collective-permute-done.24 = bf16[128,5632]{1,0:T(8,128)(2,1)S(1)} collective-permute-done((bf16[128,5632]{1,0:T(8,128)(2,1)S(1)}, bf16[128,5632]{1,0:T(8,128)(2,1)S(1)}, u32[]{:S(2)}, u32[]{:S(2)}) %collective-permute-start.24) | collective-permute-done | bytes 1441824 | tf_op jit(solution)/shard_map/ppermute | solution.py:564
  1066.8 2.3 collective-permute-start.30
  1072.6 6.3 copy.36
  1083.0 21.4 %collective-permute-done.28 = bf16[128,4096]{1,0:T(8,128)(2,1)S(1)} collective-permute-done((bf16[128,4096]{1,0:T(8,128)(2,1)}, bf16[128,4096]{1,0:T(8,128)(2,1)S(1)}, u32[]{:S(2)}, u32[]{:S(2)}) %collective-permute-start.28) | collective-permute-done | bytes 1048608 | tf_op jit(solution)/shard_map/ppermute | solution.py:564
  1106.6 3.2 maximum_convert_fusion
  1110.0 19.6 %collective-permute-done.31 = bf16[128,4096]{1,0:T(8,128)(2,1)S(1)} collective-permute-done((bf16[128,4096]{1,0:T(8,128)(2,1)S(1)}, bf16[128,4096]{1,0:T(8,128)(2,1)S(1)}, u32[]{:S(2)}, u32[]{:S(2)}) %collective-permute-start.31) | collective-permute-done | bytes 1048608 | tf_op jit(solution)/shard_map/ppermute | solution.py:564
  1131.1 2.5 slice_convert_fusion.1
  1133.6 9.6 collective-permute-done.33
  (194 shorter events, 61.4 us)
Async XLA Ops:
  8.0 113.6 %all-gather.5.cloned.1.call-start = ((), (), s32[]{:S(2)}) async-start(), calls=%async_computation.5 | async-start | bytes 23592960 | tf_op jit(solution)/shard_map/all_gather | solution.py:524
  11.2 327.6 %all-gather.7.cloned.1.call-start = ((), (), s32[]{:S(2)}) async-start(), calls=%async_computation.6 | async-start | bytes 51904512 | tf_op jit(solution)/shard_map/all_gather | solution.py:524
  16.3 105.4 %copy-start.21 = (s32[3,256]{1,0:T(4,128)S(1)}, s32[3,256]{1,0:T(4,128)}, u32[]{:S(2)}) copy-start(s32[3,256]{1,0:T(4,128)} %param.16) | copy-start | bytes 9220
  16.3 105.4 %copy-start.25 = (bf16[256]{0:T(256)(128)(2,1)S(1)}, bf16[256]{0:T(256)(128)(2,1)}, u32[]{:S(2)}) copy-start(bf16[256]{0:T(256)(128)(2,1)} %param.19) | copy-start | bytes 1540
  16.4 105.4 %copy-start.26 = (bf16[256]{0:T(256)(128)(2,1)S(1)}, bf16[256]{0:T(256)(128)(2,1)}, u32[]{:S(2)}) copy-start(bf16[256]{0:T(256)(128)(2,1)} %param.24) | copy-start | bytes 1540
  16.4 105.4 %copy-start = (bf16[3,256,2048]{2,1,0:T(8,128)(2,1)S(1)}, bf16[3,256,2048]{2,1,0:T(8,128)(2,1)}, u32[]{:S(2)}) copy-start(bf16[3,256,2048]{2,1,0:T(8,128)(2,1)} %param.14) | copy-start | bytes 9437188
  121.7 335.5 %all-gather.9.cloned.1.call-start = ((), (), s32[]{:S(2)}) async-start(), calls=%async_computation.15 | async-start | bytes 25952256 | tf_op jit(solution)/shard_map/all_gather | solution.py:524
  137.2 62.4 %copy-start.18 = (s32[3,1024]{1,0:T(4,128)S(1)}, s32[3,1024]{1,0:T(4,128)}, u32[]{:S(2)}) copy-start(s32[3,1024]{1,0:T(4,128)} %param.17) | copy-start | bytes 36868
  137.2 63.7 %copy-start.27 = (s32[3]{0:T(128)S(1)}, s32[3]{0:T(128)}, u32[]{:S(2)}) copy-start(s32[3]{0:T(128)} %param.18) | copy-start | bytes 40
  155.5 37.9 %collective-permute-start = (bf16[768,1024]{1,0:T(8,128)(2,1)}, bf16[768,1024]{1,0:T(8,128)(2,1)S(1)}, u32[]{:S(2)}, u32[]{:S(2)}) collective-permute-start(bf16[768,1024]{1,0:T(8,128)(2,1)} %get-tuple-element.73.refs_0_.refs_4_), channel_id=1, source_target_pairs={{0,1},{1,2},{2,3},{4,5},{5,6},{6,7},{8,9},{9,10},{10,11},{12,13},{... | collective-permute-start | bytes 4718600 | tf_op jit(solution)/shard_map/ppermute | solution.py:581
  194.5 3.2 collective-permute-start.1
  196.3 41.1 %collective-permute-start.3 = (bf16[768,1024]{1,0:T(8,128)(2,1)}, bf16[768,1024]{1,0:T(8,128)(2,1)S(1)}, u32[]{:S(2)}, u32[]{:S(2)}) collective-permute-start(bf16[768,1024]{1,0:T(8,128)(2,1)} %get-tuple-element.73.refs_0_.refs_4_), channel_id=1, source_target_pairs={{1,0},{2,1},{3,2},{5,4},{6,5},{7,6},{9,8},{10,9},{11,10},{13,12},{... | collective-permute-start | bytes 4718600 | tf_op jit(solution)/shard_map/ppermute | solution.py:585
  197.6 39.8 %collective-permute-start.2 = (bf16[768,1024]{1,0:T(8,128)(2,1)}, bf16[768,1024]{1,0:T(8,128)(2,1)}, u32[]{:S(2)}, u32[]{:S(2)}) collective-permute-start(bf16[768,1024]{1,0:T(8,128)(2,1)} %collective-permute-done.1.refs_2_.refs_6_), channel_id=1, source_target_pairs={{2,3},{6,7},{10,11},{14,15},{18,19},{22,23},{26,27},{30,31}} | collective-permute-start | bytes 4718600 | tf_op jit(solution)/shard_map/ppermute | solution.py:581
  338.8 223.1 %reduce-scatter.6.cloned.1.call-start = ((), (), s32[]{:S(2)}) async-start(), calls=%async_computation.7 | async-start | bytes 14417920 | tf_op jit(solution)/shard_map/reduce_scatter | solution.py:530
  363.3 27.9 %copy-start.1 = (bf16[3,256,2048]{2,1,0:T(8,128)(2,1)S(1)}, bf16[3,256,2048]{2,1,0:T(8,128)(2,1)}, u32[]{:S(2)}) copy-start(bf16[3,256,2048]{2,1,0:T(8,128)(2,1)} %param.15) | copy-start | bytes 9437188
  390.9 27.2 %collective-permute-start.6 = (bf16[768,5632]{1,0:T(8,128)(2,1)}, bf16[768,5632]{1,0:T(8,128)(2,1)}, u32[]{:S(2)}, u32[]{:S(2)}) collective-permute-start(bf16[768,5632]{1,0:T(8,128)(2,1)} %get-tuple-element.101.bo_ref.h_ref), channel_id=1, source_target_pairs={{0,4},{4,0},{8,12},{12,8},{16,20},{20,16},{24,28},{28,24},{1,5},{5... | collective-permute-start | bytes 25952264 | tf_op jit(solution)/shard_map/ppermute | solution.py:527
  393.9 14.9 %collective-permute-start.5 = (bf16[768,2048]{1,0:T(8,128)(2,1)}, bf16[768,2048]{1,0:T(8,128)(2,1)S(1)}, u32[]{:S(2)}, u32[]{:S(2)}) collective-permute-start(bf16[768,2048]{1,0:T(8,128)(2,1)} %multiply_convert_fusion.ao_ref.m_ref), channel_id=1, source_target_pairs={{0,4},{4,0},{8,12},{12,8},{16,20},{20,16},{24,28},{28,24},{1,5},{5... | collective-permute-start | bytes 9437192 | tf_op jit(solution)/shard_map/ppermute | solution.py:527
  408.8 9.2 copy-start.23
  443.3 118.9 %all-reduce.5.cloned.1.call-start = ((), (), s32[]{:S(2)}) async-start(), calls=%async_computation.10 | async-start | bytes 524288 | tf_op jit(solution)/shard_map/psum | solution.py:535
  457.2 31.8 %copy-start.22 = (bf16[768,2048]{1,0:T(8,128)(2,1)S(1)}, bf16[768,2048]{1,0:T(8,128)(2,1)}, u32[]{:S(2)}) copy-start(bf16[768,2048]{1,0:T(8,128)(2,1)} %get-tuple-element.75.x_ref.ao_ref) | copy-start | bytes 9437188
  488.6 46.9 %collective-permute-start.7 = (bf16[768,5632]{1,0:T(8,128)(2,1)}, bf16[768,5632]{1,0:T(8,128)(2,1)}, u32[]{:S(2)}, u32[]{:S(2)}) collective-permute-start(bf16[768,5632]{1,0:T(8,128)(2,1)} %get-tuple-element.84.a_ref.bo_ref), channel_id=1, source_target_pairs={{0,4},{4,0},{8,12},{12,8},{16,20},{20,16},{24,28},{28,24},{1,5},{5... | collective-permute-start | bytes 25952264 | tf_op jit(solution)/shard_map/ppermute | solution.py:527
  488.9 177.8 %reduce-scatter.8.cloned.1.call-start = ((), (), s32[]{:S(2)}) async-start(), calls=%async_computation.8 | async-start | bytes 14417920 | tf_op jit(solution)/shard_map/reduce_scatter | solution.py:530
  489.0 46.5 %collective-permute-start.4 = (bf16[768,2048]{1,0:T(8,128)(2,1)S(1)}, bf16[768,2048]{1,0:T(8,128)(2,1)}, u32[]{:S(2)}, u32[]{:S(2)}) collective-permute-start(bf16[768,2048]{1,0:T(8,128)(2,1)S(1)} %copy-done.22), channel_id=1, source_target_pairs={{0,4},{4,0},{8,12},{12,8},{16,20},{20,16},{24,28},{28,24},{1,5},{5... | collective-permute-start | bytes 9437192 | tf_op jit(solution)/shard_map/ppermute | solution.py:527
  562.0 115.3 %all-reduce.7.cloned.1.call-start = ((), (), s32[]{:S(2)}) async-start(), calls=%async_computation.11 | async-start | bytes 5767168 | tf_op jit(solution)/shard_map/psum | solution.py:535
  562.1 68.0 %collective-permute-start.8 = (bf16[768,5632]{1,0:T(8,128)(2,1)}, bf16[768,5632]{1,0:T(8,128)(2,1)}, u32[]{:S(2)}, u32[]{:S(2)}) collective-permute-start(bf16[768,5632]{1,0:T(8,128)(2,1)} %get-tuple-element.89.b_ref.bo_ref), channel_id=1, source_target_pairs={{0,4},{4,0},{8,12},{12,8},{16,20},{20,16},{24,28},{28,24},{1,5},{5... | collective-permute-start | bytes 25952264 | tf_op jit(solution)/shard_map/ppermute | solution.py:527
  562.6 208.9 %reduce-scatter.10.cloned.1.call-start = ((), (), s32[]{:S(2)}) async-start(), calls=%async_computation.9 | async-start | bytes 14417920 | tf_op jit(solution)/shard_map/reduce_scatter | solution.py:530
  666.7 177.0 %all-reduce.9.cloned.1.call-start = ((), (), s32[]{:S(2)}) async-start(), calls=%async_computation.12 | async-start | bytes 5767168 | tf_op jit(solution)/shard_map/psum | solution.py:535
  666.8 14.8 %collective-permute-start.12 = (bf16[768,2048]{1,0:T(8,128)(2,1)}, bf16[768,2048]{1,0:T(8,128)(2,1)}, u32[]{:S(2)}, u32[]{:S(2)}) collective-permute-start(bf16[768,2048]{1,0:T(8,128)(2,1)} %get-tuple-element.74.a_ref.ao_ref), channel_id=1, source_target_pairs={{0,4},{4,0},{8,12},{12,8},{16,20},{20,16},{24,28},{28,24},{1,5},{5... | collective-permute-start | bytes 9437192 | tf_op jit(solution)/shard_map/ppermute | solution.py:527
  666.9 15.0 %collective-permute-start.13 = (bf16[768,2048]{1,0:T(8,128)(2,1)}, bf16[768,2048]{1,0:T(8,128)(2,1)}, u32[]{:S(2)}, u32[]{:S(2)}) collective-permute-start(bf16[768,2048]{1,0:T(8,128)(2,1)} %get-tuple-element.97.bo_ref), channel_id=1, source_target_pairs={{0,4},{4,0},{8,12},{12,8},{16,20},{20,16},{24,28},{28,24},{1,5},{5... | collective-permute-start | bytes 9437192 | tf_op jit(solution)/shard_map/ppermute | solution.py:527
  667.4 27.2 %collective-permute-start.9 = (bf16[768,2048]{1,0:T(8,128)(2,1)}, bf16[768,2048]{1,0:T(8,128)(2,1)}, u32[]{:S(2)}, u32[]{:S(2)}) collective-permute-start(bf16[768,2048]{1,0:T(8,128)(2,1)} %multiply_convert_fusion.1.x_ref.ao_ref), channel_id=1, source_target_pairs={{0,4},{4,0},{8,12},{12,8},{16,20},{20,16},{24,28},{28,24},{1,5},{5... | collective-permute-start | bytes 9437192 | tf_op jit(solution)/shard_map/ppermute | solution.py:527
  668.6 25.9 %collective-permute-start.11 = (bf16[768,2048]{1,0:T(8,128)(2,1)S(1)}, bf16[768,2048]{1,0:T(8,128)(2,1)}, u32[]{:S(2)}, u32[]{:S(2)}) collective-permute-start(bf16[768,2048]{1,0:T(8,128)(2,1)S(1)} %copy-done.2), channel_id=1, source_target_pairs={{0,4},{4,0},{8,12},{12,8},{16,20},{20,16},{24,28},{28,24},{1,5},{5... | collective-permute-start | bytes 9437192 | tf_op jit(solution)/shard_map/ppermute | solution.py:527
  668.6 9.3 collective-permute-start.10
  677.4 280.4 %reduce-scatter.12.cloned.1.call-start = ((), (), s32[]{:S(2)}) async-start(), calls=%async_computation.13 | async-start | bytes 10485760 | tf_op jit(solution)/shard_map/reduce_scatter | solution.py:530
  707.1 64.4 %copy-start.12 = (bf16[768,1024]{1,0:T(8,128)(2,1)S(1)}, bf16[768,1024]{1,0:T(8,128)(2,1)}, u32[]{:S(2)}) copy-start(bf16[768,1024]{1,0:T(8,128)(2,1)} %add_convert_fusion.1) | copy-start | bytes 4718596
  707.1 70.3 %copy-start.11 = (bf16[768,1024]{1,0:T(8,128)(2,1)S(1)}, bf16[768,1024]{1,0:T(8,128)(2,1)}, u32[]{:S(2)}) copy-start(bf16[768,1024]{1,0:T(8,128)(2,1)} %get-tuple-element.98) | copy-start | bytes 4718596
  771.5 295.3 %reduce-scatter.14.cloned.1.call-start = ((), (), s32[]{:S(2)}) async-start(), calls=%async_computation.14 | async-start | bytes 2949120 | tf_op jit(solution)/shard_map/reduce_scatter | solution.py:530
  771.5 5.9 collective-permute-start.14
  773.4 125.1 %collective-permute-start.15 = (bf16[768,1024]{1,0:T(8,128)(2,1)}, bf16[768,1024]{1,0:T(8,128)(2,1)}, u32[]{:S(2)}, u32[]{:S(2)}) collective-permute-start(bf16[768,1024]{1,0:T(8,128)(2,1)} %get-tuple-element.94), channel_id=1, source_target_pairs={{0,1},{1,2},{2,3},{4,5},{5,6},{6,7},{8,9},{9,10},{10,11},{12,13},{... | collective-permute-start | bytes 4718600 | tf_op jit(solution)/shard_map/ppermute | solution.py:592
  843.7 40.6 %collective-permute-start.17 = (bf16[128,5632]{1,0:T(8,128)(2,1)S(1)}, bf16[128,5632]{1,0:T(8,128)(2,1)}, u32[]{:S(2)}, u32[]{:S(2)}) collective-permute-start(bf16[128,5632]{1,0:T(8,128)(2,1)S(1)} %get-tuple-element.100), channel_id=1, source_target_pairs={{0,1},{3,2},{4,5},{7,6},{8,9},{11,10},{12,13},{15,14},{16,17},{19,... | collective-permute-start | bytes 4325384 | tf_op jit(solution)/shard_map/ppermute | solution.py:564
  854.4 44.1 %collective-permute-start.16 = (bf16[768,1024]{1,0:T(8,128)(2,1)S(1)}, bf16[768,1024]{1,0:T(8,128)(2,1)}, u32[]{:S(2)}, u32[]{:S(2)}) collective-permute-start(bf16[768,1024]{1,0:T(8,128)(2,1)S(1)} %add_convert_fusion), channel_id=1, source_target_pairs={{1,0},{2,1},{3,2},{5,4},{6,5},{7,6},{9,8},{10,9},{11,10},{13,12},{... | collective-permute-start | bytes 4718600 | tf_op jit(solution)/shard_map/ppermute | solution.py:597
  880.6 14.7 %copy-start.8 = (bf16[256,5632]{1,0:T(8,128)(2,1)S(1)}, bf16[256,5632]{1,0:T(8,128)(2,1)}, u32[]{:S(2)}) copy-start(bf16[256,5632]{1,0:T(8,128)(2,1)} %all-reduce.7.cloned.1.call-done) | copy-start | bytes 8650756
  887.1 11.4 copy-start.14
  887.1 39.2 %collective-permute-start.19 = (bf16[128,5632]{1,0:T(8,128)(2,1)}, bf16[128,5632]{1,0:T(8,128)(2,1)}, u32[]{:S(2)}, u32[]{:S(2)}) collective-permute-start(bf16[128,5632]{1,0:T(8,128)(2,1)} %add_convert_fusion.5), channel_id=1, source_target_pairs={{1,2},{2,1},{5,6},{6,5},{9,10},{10,9},{13,14},{14,13},{17,18},{18,... | collective-permute-start | bytes 4325384 | tf_op jit(solution)/shard_map/ppermute | solution.py:564
  889.1 35.1 %collective-permute-start.20 = (bf16[128,5632]{1,0:T(8,128)(2,1)}, bf16[128,5632]{1,0:T(8,128)(2,1)}, u32[]{:S(2)}, u32[]{:S(2)}) collective-permute-start(bf16[128,5632]{1,0:T(8,128)(2,1)} %get-tuple-element.111), channel_id=1, source_target_pairs={{0,1},{3,2},{4,5},{7,6},{8,9},{11,10},{12,13},{15,14},{16,17},{19,... | collective-permute-start | bytes 4325384 | tf_op jit(solution)/shard_map/ppermute | solution.py:564
  911.9 16.6 %copy-start.3 = (bf16[768,1024]{1,0:T(8,128)(2,1)}, bf16[768,1024]{1,0:T(8,128)(2,1)S(1)}, u32[]{:S(2)}) copy-start(bf16[768,1024]{1,0:T(8,128)(2,1)S(1)} %pad_maximum_fusion.3.bo_ref.kv_ref) | copy-start | bytes 4718596
  911.9 16.6 %collective-permute-start.18 = (bf16[768,1024]{1,0:T(8,128)(2,1)S(1)}, bf16[768,1024]{1,0:T(8,128)(2,1)}, u32[]{:S(2)}, u32[]{:S(2)}) collective-permute-start(bf16[768,1024]{1,0:T(8,128)(2,1)S(1)} %pad_maximum_fusion.3.bo_ref.kv_ref), channel_id=1, source_target_pairs={{0,4},{4,0},{8,12},{12,8},{16,20},{20,16},{24,28},{28,24},{1,5},{5... | collective-permute-start | bytes 4718600 | tf_op jit(solution)/shard_map/ppermute | solution.py:527
  937.3 19.6 %copy-start.19 = (f32[1,2048]{1,0:T(1,128)S(1)}, f32[1,2048]{1,0:T(1,128)}, u32[]{:S(2)}) copy-start(f32[1,2048]{1,0:T(1,128)} %get-tuple-element.121) | copy-start | bytes 24580
  956.9 9.6 copy-start.20
  957.7 8.8 collective-permute-start.27
  960.9 27.9 %collective-permute-start.23 = (bf16[128,4096]{1,0:T(8,128)(2,1)}, bf16[128,4096]{1,0:T(8,128)(2,1)}, u32[]{:S(2)}, u32[]{:S(2)}) collective-permute-start(bf16[128,4096]{1,0:T(8,128)(2,1)} %get-tuple-element.115), channel_id=1, source_target_pairs={{0,1},{3,2},{4,5},{7,6},{8,9},{11,10},{12,13},{15,14},{16,17},{19,... | collective-permute-start | bytes 3145736 | tf_op jit(solution)/shard_map/ppermute | solution.py:564
  966.6 24.1 %collective-permute-start.22 = (bf16[128,5632]{1,0:T(8,128)(2,1)S(1)}, bf16[128,5632]{1,0:T(8,128)(2,1)}, u32[]{:S(2)}, u32[]{:S(2)}) collective-permute-start(bf16[128,5632]{1,0:T(8,128)(2,1)S(1)} %add_convert_fusion.3), channel_id=1, source_target_pairs={{1,2},{2,1},{5,6},{6,5},{9,10},{10,9},{13,14},{14,13},{17,18},{18,... | collective-permute-start | bytes 4325384 | tf_op jit(solution)/shard_map/ppermute | solution.py:564
  971.8 55.9 %collective-permute-start.21 = (bf16[128,5632]{1,0:T(8,128)(2,1)S(1)}, bf16[128,5632]{1,0:T(8,128)(2,1)S(1)}, u32[]{:S(2)}, u32[]{:S(2)}) collective-permute-start(bf16[128,5632]{1,0:T(8,128)(2,1)S(1)} %add_convert_fusion.4), channel_id=1, source_target_pairs={{1,0},{2,3},{5,4},{6,7},{9,8},{10,11},{13,12},{14,15},{17,16},{18,... | collective-permute-start | bytes 4325384 | tf_op jit(solution)/shard_map/ppermute | solution.py:564
  992.3 35.6 %copy-start.6 = (bf16[128,4096]{1,0:T(8,128)(2,1)S(1)}, bf16[128,4096]{1,0:T(8,128)(2,1)}, u32[]{:S(2)}) copy-start(bf16[128,4096]{1,0:T(8,128)(2,1)} %get-tuple-element.119) | copy-start | bytes 3145732
  1027.9 23.8 %collective-permute-start.26 = (bf16[128,4096]{1,0:T(8,128)(2,1)S(1)}, bf16[128,4096]{1,0:T(8,128)(2,1)S(1)}, u32[]{:S(2)}, u32[]{:S(2)}) collective-permute-start(bf16[128,4096]{1,0:T(8,128)(2,1)S(1)} %copy-done.6), channel_id=1, source_target_pairs={{0,1},{3,2},{4,5},{7,6},{8,9},{11,10},{12,13},{15,14},{16,17},{19,... | collective-permute-start | bytes 3145736 | tf_op jit(solution)/shard_map/ppermute | solution.py:564
  1029.5 23.5 %collective-permute-start.25 = (bf16[128,4096]{1,0:T(8,128)(2,1)S(1)}, bf16[128,4096]{1,0:T(8,128)(2,1)S(1)}, u32[]{:S(2)}, u32[]{:S(2)}) collective-permute-start(bf16[128,4096]{1,0:T(8,128)(2,1)S(1)} %add_convert_fusion.9), channel_id=1, source_target_pairs={{1,2},{2,1},{5,6},{6,5},{9,10},{10,9},{13,14},{14,13},{17,18},{18,... | collective-permute-start | bytes 3145736 | tf_op jit(solution)/shard_map/ppermute | solution.py:564
  1030.2 36.4 %collective-permute-start.24 = (bf16[128,5632]{1,0:T(8,128)(2,1)S(1)}, bf16[128,5632]{1,0:T(8,128)(2,1)S(1)}, u32[]{:S(2)}, u32[]{:S(2)}) collective-permute-start(bf16[128,5632]{1,0:T(8,128)(2,1)S(1)} %add_convert_fusion.2), channel_id=1, source_target_pairs={{1,0},{2,3},{5,4},{6,7},{9,8},{10,11},{13,12},{14,15},{17,16},{18,... | collective-permute-start | bytes 4325384 | tf_op jit(solution)/shard_map/ppermute | solution.py:564
  1066.8 13.5 %collective-permute-start.30 = (bf16[256,1152]{1,0:T(8,128)(2,1)}, bf16[256,1152]{1,0:T(8,128)(2,1)}, u32[]{:S(2)}, u32[]{:S(2)}) collective-permute-start(bf16[256,1152]{1,0:T(8,128)(2,1)} %reduce-scatter.14.cloned.1.call-done), channel_id=1, source_target_pairs={{0,1},{3,2},{4,5},{7,6},{8,9},{11,10},{12,13},{15,14},{16,17},{19,... | collective-permute-start | bytes 1769480 | tf_op jit(solution)/shard_map/ppermute | solution.py:564
  1069.1 12.4 %collective-permute-start.29 = (bf16[128,4096]{1,0:T(8,128)(2,1)}, bf16[128,4096]{1,0:T(8,128)(2,1)}, u32[]{:S(2)}, u32[]{:S(2)}) collective-permute-start(bf16[128,4096]{1,0:T(8,128)(2,1)} %add_convert_fusion.7), channel_id=1, source_target_pairs={{1,2},{2,1},{5,6},{6,5},{9,10},{10,9},{13,14},{14,13},{17,18},{18,... | collective-permute-start | bytes 3145736 | tf_op jit(solution)/shard_map/ppermute | solution.py:564
  1072.6 7.7 copy-start.16
  1078.9 25.6 %copy-start.5 = (bf16[128,4096]{1,0:T(8,128)(2,1)S(1)}, bf16[128,4096]{1,0:T(8,128)(2,1)}, u32[]{:S(2)}) copy-start(bf16[128,4096]{1,0:T(8,128)(2,1)} %add_convert_fusion.8) | copy-start | bytes 3145732
  1078.9 25.6 %collective-permute-start.28 = (bf16[128,4096]{1,0:T(8,128)(2,1)}, bf16[128,4096]{1,0:T(8,128)(2,1)S(1)}, u32[]{:S(2)}, u32[]{:S(2)}) collective-permute-start(bf16[128,4096]{1,0:T(8,128)(2,1)} %add_convert_fusion.8), channel_id=1, source_target_pairs={{1,0},{2,3},{5,4},{6,7},{9,8},{10,11},{13,12},{14,15},{17,16},{18,... | collective-permute-start | bytes 3145736 | tf_op jit(solution)/shard_map/ppermute | solution.py:564
  1104.6 5.3 collective-permute-start.32
  1105.3 24.3 %collective-permute-start.31 = (bf16[128,4096]{1,0:T(8,128)(2,1)S(1)}, bf16[128,4096]{1,0:T(8,128)(2,1)S(1)}, u32[]{:S(2)}, u32[]{:S(2)}) collective-permute-start(bf16[128,4096]{1,0:T(8,128)(2,1)S(1)} %add_convert_fusion.6), channel_id=1, source_target_pairs={{1,0},{2,3},{5,4},{6,7},{9,8},{10,11},{13,12},{14,15},{17,16},{18,... | collective-permute-start | bytes 3145736 | tf_op jit(solution)/shard_map/ppermute | solution.py:564
  1129.7 13.5 %collective-permute-start.33 = (bf16[256,1152]{1,0:T(8,128)(2,1)S(1)}, bf16[256,1152]{1,0:T(8,128)(2,1)S(1)}, u32[]{:S(2)}, u32[]{:S(2)}) collective-permute-start(bf16[256,1152]{1,0:T(8,128)(2,1)S(1)} %add_convert_fusion.10), channel_id=1, source_target_pairs={{1,0},{2,3},{5,4},{6,7},{9,8},{10,11},{13,12},{14,15},{17,16},{18,... | collective-permute-start | bytes 1769480 | tf_op jit(solution)/shard_map/ppermute | solution.py:564
  (9 other events, 19.8 us)
Sparse Core Ops, SparseCore 0:
  11.3 110.2 all-gather.4
  124.1 214.6 all-gather.6
  340.7 116.4 all-gather.8
  459.4 102.5 reduce-scatter.5
  564.2 102.4 reduce-scatter.7
  668.9 102.5 reduce-scatter.9
  773.8 76.9 reduce-scatter.11
  972.0 50.7 reduce-scatter.13
Sparse Core Ops, SparseCore 1:
  489.0 35.8 all-reduce.4
  565.0 112.3 all-reduce.6
  679.7 164.0 all-reduce.8

commit v3 on v2

--- a/solution.py
+++ b/solution.py
@@ -674,8 +674,11 @@
     grad_kv = collecting.send(after(kv_held, token))
     output = down_matmul(after(hidden, token), down_full, middle, keep)
     token = tick(fresh[1:], output)
+    out_down = after(down_all, token).astype(F32).T
+    att_all, fresh = chunks(att_sum, 2)
+    token = tick(fresh[:1])
+    token = tick(fresh[1:])
     grad_kv = after(grad_kv, token)
-    out_down = after(down_all, token).astype(F32).T
     grad_key = grad_kv[:, :pair_width].reshape(rows, KVH, HD)
     turned = grad_key * sine[:, None, :]
     turned = jnp.concatenate([turned[..., half:], turned[..., :half]], -1)
@@ -692,10 +695,7 @@
     gain_grads = jnp.stack([gain_grads[:, chip] for chip in ring], 1).reshape(2, width // 2)
     gain_part = jnp.pad(gain_grads.T, ((0, 0), (0, HD - 2))).astype(BF16)
     kv_sum = scatter(after(jnp.concatenate([kv_part, gain_part], 1), att_sum))
-    att_all, fresh = chunks(att_sum, 2)
-    token = tick(fresh[:1], grad_input)
     out_gate = after(gate_all, token).astype(F32)
-    token = tick(fresh[1:], out_gate)
     kv_sums, fresh = chunks(kv_sum, 1)
     token = tick(fresh)
     while under_way:

time: 1160 us -> 1200 us (1.034)
  starting transfers between devices: 60.7 us -> 102 us
    ppermute x15, starting transfers between devices: 39.7 us -> 84.9 us  [tick(): chunk['came'] = lax.ppermute(v, 'ulysses', hops[chunk['hop']][0])]
  transfers between devices with their start and end apart: 45 -> 45, of which waited for: 22 -> 23; matrix products, arithmetic and copies ran while one was open for 7% -> 6% of each run, Pallas kernels for 37% -> 33%
where the time goes in v3:
time: 1200 us; the launch traced here: 1190 us
  waiting for transfers between devices  542 us (45%)
  Pallas kernels  422 us (35%)
  starting transfers between devices  102 us (8%)
  other arithmetic  67.4 us (6%)
  local copies, waits for them, and re-layouts  29.4 us (2%)
  between operations  17.4 us (1%)
    all_gather x3, waiting for transfers between devices, gather(): return lax.all_gather(v, 'fsdp', axis=0, tiled=tiled)  166 us
    ppermute x15, waiting for transfers between devices, tick(): chunk['came'] = lax.ppermute(v, 'ulysses', hops[chunk['hop']][0])  146 us
    pallas_call x6, Pallas kernels, weight_grad(): pl.pallas_call(body, grid_spec=pltpu.PrefetchScalarGridSpec(num_scalar_pr...  110 us
    ppermute x15, starting transfers between devices, tick(): chunk['came'] = lax.ppermute(v, 'ulysses', hops[chunk['hop']][0])  84.9 us
    reduce_scatter x5, waiting for transfers between devices, scatter(): lax.psum_scatter(v, 'fsdp', scatter_dimension=0, tiled=True, axis_index_g...  77.1 us
    psum x3, waiting for transfers between devices, finish(): return lax.psum(v, 'ulysses')  59.1 us
    pallas_call x1, Pallas kernels, attend_back(): pl.pallas_call(body, grid=(seqs, KVH), in_specs=[pl.BlockSpec((local, GRO...  48.7 us
    pallas_call x1, Pallas kernels, mlp_back(): pl.pallas_call(body, grid=(width // tile,), in_specs=[pl.BlockSpec((rows,...  46.2 us
  transfers between devices with their start and end apart: 45, of which 23 were waited for; matrix products, arithmetic and copies ran while one was open for 6% of the time, Pallas kernels for 33%

profile of v3, /device:TPU:0, one launch (start us, length us, event | category | flops | bytes accessed | tf_op | source)
XLA Modules:
  0.0 1189.3 jit_solution(16547358497964823033)
XLA Ops:
  8.1 3.1 pad_maximum_fusion.1
  11.2 5.1 pad_maximum_fusion
  16.4 105.3 %all-gather.5.cloned.1.call-done.w_ref.wq_ref.wkv_ref = bf16[2048,5120]{1,0:T(8,128)(2,1)} async-done(((bf16[256,5120]{1,0:T(8,128)(2,1)}), bf16[2048,5120]{1,0:T(8,128)(2,1)}) %all-gather.5.cloned.1.call-update) | async-done | bytes 20971536 | tf_op jit(solution)/shard_map/all_gather | solution.py:524
  122.5 8.8 all_gather.15
  134.6 2.6 multiply_convert_fusion.1.x_ref.ao_ref
  137.2 18.2 %project.1 = (bf16[768,2048]{1,0:T(8,128)(2,1)}, bf16[768,1024]{1,0:T(8,128)(2,1)}) custom-call(bf16[768,2048]{1,0:T(8,128)(2,1)} %multiply_convert_fusion.1.x_ref.ao_ref, bf16[2048,5120]{1,0:T(8,128)(2,1)} %all-gather.5.cloned.1.call-done.w_ref.wq_ref.wkv_ref, f32[768,128]{1,0:T(8,128)} %get-tuple-element.174.c_ref.refs_12_, ...), custom_call_target="tpu_custom_call" | custom-call | flops 9663676416 | bytes 18874368 | tf_op jit(solution)/shard_map/project/pallas_call | solution.py:71
  155.5 3.5 collective-permute-start
  158.9 34.4 %collective-permute-done.refs_1_.refs_5_ = bf16[768,1024]{1,0:T(8,128)(2,1)S(1)} collective-permute-done((bf16[768,1024]{1,0:T(8,128)(2,1)}, bf16[768,1024]{1,0:T(8,128)(2,1)S(1)}, u32[]{:S(2)}, u32[]{:S(2)}) %collective-permute-start) | collective-permute-done | bytes 1572896 | tf_op jit(solution)/shard_map/ppermute | solution.py:581
  194.5 1.9 collective-permute-start.1
  197.6 2.3 collective-permute-start.2
  204.2 33.3 %collective-permute-done.3 = bf16[768,1024]{1,0:T(8,128)(2,1)S(1)} collective-permute-done((bf16[768,1024]{1,0:T(8,128)(2,1)}, bf16[768,1024]{1,0:T(8,128)(2,1)S(1)}, u32[]{:S(2)}, u32[]{:S(2)}) %collective-permute-start.3) | collective-permute-done | bytes 1572896 | tf_op jit(solution)/shard_map/ppermute | solution.py:585
  238.8 39.0 %attend.1 = (bf16[768,2048]{1,0:T(8,128)(2,1)}, f32[3,4,4,256]{3,2,1,0:T(4,128)}) custom-call(bf16[768,2048]{1,0:T(8,128)(2,1)} %get-tuple-element.72.q_ref, bf16[768,1024]{1,0:T(8,128)(2,1)} %get-tuple-element.73.refs_0_.refs_4_, bf16[768,1024]{1,0:T(8,128)(2,1)} %copy-done.27, bf16[768,1024]{1,0:T(8,128)(2,1)} %collective-permute-done.1.refs_2_.refs_6_, ...), custom_call_target="tpu_custom_call" | custom-call | flops 12884901888 | bytes 6291456 | tf_op jit(solution)/shard_map/attend/pallas_call | solution.py:121
  277.8 13.6 %out_project.1 = (f32[768,2048]{1,0:T(8,128)}, bf16[768,2048]{1,0:T(8,128)(2,1)}) custom-call(bf16[768,2048]{1,0:T(8,128)(2,1)} %get-tuple-element.74.a_ref.ao_ref, bf16[2048,5120]{1,0:T(8,128)(2,1)} %all-gather.5.cloned.1.call-done.w_ref.wq_ref.wkv_ref, bf16[768,2048]{1,0:T(8,128)(2,1)} %bitcast.41, f32[768,1]{1,0:T(8,128)} %bitcast.46, ...), custom_call_target="tpu_custom_call" | custom-call | flops 6442450944 | bytes 24117248 | tf_op jit(solution)/shard_map/out_project/pallas_call | solution.py:219
  291.4 47.4 %all-gather.7.cloned.1.call-done.w_ref.wa_ref.wb_ref = bf16[2048,11264]{1,0:T(8,128)(2,1)} async-done(((bf16[256,11264]{1,0:T(8,128)(2,1)}), bf16[2048,11264]{1,0:T(8,128)(2,1)}) %all-gather.7.cloned.1.call-update) | async-done | bytes 46137360 | tf_op jit(solution)/shard_map/all_gather | solution.py:524
  338.9 24.4 %gate_matmul.1.g_ref = bf16[768,5632]{1,0:T(8,128)(2,1)} custom-call(bf16[768,2048]{1,0:T(8,128)(2,1)} %get-tuple-element.75.x_ref.ao_ref, bf16[2048,11264]{1,0:T(8,128)(2,1)} %all-gather.7.cloned.1.call-done.w_ref.wa_ref.wb_ref), custom_call_target="tpu_custom_call" | custom-call | flops 17716740096 | bytes 31719424 | tf_op jit(solution)/shard_map/gate_matmul/pallas_call | solution.py:242
  363.3 27.5 %up_matmul.1 = (bf16[768,5632]{1,0:T(8,128)(2,1)}, bf16[768,5632]{1,0:T(8,128)(2,1)}) custom-call(bf16[768,2048]{1,0:T(8,128)(2,1)} %get-tuple-element.75.x_ref.ao_ref, bf16[2048,11264]{1,0:T(8,128)(2,1)} %all-gather.7.cloned.1.call-done.w_ref.wa_ref.wb_ref, bf16[768,5632]{1,0:T(8,128)(2,1)} %gate_matmul.1.g_ref), custom_call_target="tpu_custom_call" | custom-call | flops 17716740096 | bytes 49020928 | tf_op jit(solution)/shard_map/up_matmul/pallas_call | solution.py:263
  391.2 2.7 multiply_convert_fusion.ao_ref.m_ref
  394.1 14.6 %collective-permute-done.5.ap_ref = bf16[768,2048]{1,0:T(8,128)(2,1)S(1)} collective-permute-done((bf16[768,2048]{1,0:T(8,128)(2,1)}, bf16[768,2048]{1,0:T(8,128)(2,1)S(1)}, u32[]{:S(2)}, u32[]{:S(2)}) %collective-permute-start.5) | collective-permute-done | bytes 3145760 | tf_op jit(solution)/shard_map/ppermute | solution.py:527
  408.7 9.3 collective-permute-done.6.bp_ref
  418.0 25.2 %weight_grad.6 = bf16[1024,5632]{1,0:T(8,128)(2,1)} custom-call(s32[1]{0:T(128)} %bitcast.6.side_ref, bf16[768,2048]{1,0:T(8,128)(2,1)} %multiply_convert_fusion.ao_ref.m_ref, bf16[768,2048]{1,0:T(8,128)(2,1)} %copy-done.26, bf16[768,5632]{1,0:T(8,128)(2,1)} %get-tuple-element.101.bo_ref.h_ref, bf16[768,5632]{1,0:T(8,128)(2,1)} %collective-permute-done.6.bp_ref), custom_call_target="tpu_custom_call" | custom-call | flops 17716740096 | bytes 35127296 | tf_op jit(solution)/shard_map/weight_grad/pallas_call | solution.py:467
  443.5 13.7 %all-gather.9.cloned.1.call-done = bf16[45056,256]{1,0:T(8,128)(2,1)} async-done(((bf16[5632,256]{1,0:T(8,128)(2,1)}), bf16[45056,256]{1,0:T(8,128)(2,1)}) %all-gather.9.cloned.1.call-update) | async-done | bytes 23068688 | tf_op jit(solution)/shard_map/all_gather | solution.py:524
  457.2 31.2 %hidden_back.1 = (bf16[768,5632]{1,0:T(8,128)(2,1)}, bf16[768,5632]{1,0:T(8,128)(2,1)}) custom-call(bf16[768,2048]{1,0:T(8,128)(2,1)} %multiply_convert_fusion.ao_ref.m_ref, bf16[8,5632,256]{2,1,0:T(8,128)(2,1)} %bitcast.56, bf16[768,5632]{1,0:T(8,128)(2,1)} %gate_matmul.1.g_ref, bf16[768,5632]{1,0:T(8,128)(2,1)} %get-tuple-element.80.u_ref), custom_call_target="tpu_custom_call" | custom-call | flops 17716740096 | bytes 57671680 | tf_op jit(solution)/shard_map/hidden_back/pallas_call | solution.py:315
  489.1 46.2 %mlp_back.1.n_ref = f32[768,2048]{1,0:T(8,128)} custom-call(bf16[768,5632]{1,0:T(8,128)(2,1)} %get-tuple-element.84.a_ref.bo_ref, bf16[768,5632]{1,0:T(8,128)(2,1)} %get-tuple-element.89.b_ref.bo_ref, bf16[2048,11264]{1,0:T(8,128)(2,1)} %all-gather.7.cloned.1.call-done.w_ref.wa_ref.wb_ref, bf16[2048,11264]{1,0:T(8,128)(2,1)} %all-gather.7.cloned.1.call-done.w_ref.wa_ref.wb_ref), custom_call_target="tpu_custom_call" | custom-call | flops 35433480192 | bytes 63438848 | tf_op jit(solution)/shard_map/mlp_back/pallas_call | solution.py:339
  535.4 25.2 %weight_grad.7 = bf16[1024,5632]{1,0:T(8,128)(2,1)} custom-call(s32[1]{0:T(128)} %bitcast.6.side_ref, bf16[768,2048]{1,0:T(8,128)(2,1)} %get-tuple-element.75.x_ref.ao_ref, bf16[768,2048]{1,0:T(8,128)(2,1)} %collective-permute-done.4.ap_ref, bf16[768,5632]{1,0:T(8,128)(2,1)} %get-tuple-element.84.a_ref.bo_ref, bf16[768,5632]{1,0:T(8,128)(2,1)} %collective-permute-done.7.bp_ref), custom_call_target="tpu_custom_call" | custom-call | flops 17716740096 | bytes 35127296 | tf_op jit(solution)/shard_map/weight_grad/pallas_call | solution.py:467
  562.9 18.5 %middle_back.1 = (f32[768,2048]{1,0:T(8,128)}, bf16[768,2048]{1,0:T(8,128)(2,1)}, bf16[768,2048]{1,0:T(8,128)(2,1)}, f32[1,2048]{1,0:T(1,128)}) custom-call(f32[768,2048]{1,0:T(8,128)} %mlp_back.1.n_ref, f32[768,2048]{1,0:T(8,128)} %get-tuple-element.86.m_ref, bf16[768,2048]{1,0:T(8,128)(2,1)} %bitcast.43, f32[768,1]{1,0:T(8,128)} %bitcast.47, ...), custom_call_target="tpu_custom_call" | custom-call | flops 6442450944 | bytes 36700160 | tf_op jit(solution)/shard_map/middle_back/pallas_call | solution.py:381
  581.3 48.7 %attend_back.1 = (bf16[768,2048]{1,0:T(8,128)(2,1)}, bf16[768,1024]{1,0:T(8,128)(2,1)}, bf16[768,1024]{1,0:T(8,128)(2,1)}, bf16[768,1024]{1,0:T(8,128)(2,1)}, bf16[768,1024]{1,0:T(8,128)(2,1)}) custom-call(bf16[768,2048]{1,0:T(8,128)(2,1)} %get-tuple-element.72.q_ref, bf16[768,1024]{1,0:T(8,128)(2,1)} %get-tuple-element.73.refs_0_.refs_4_, ...), custom_call_target="tpu_custom_call" | custom-call | flops 32212254720 | bytes 12582912 | tf_op jit(solution)/shard_map/attend_back/pallas_call | solution.py:186
  630.1 25.3 %weight_grad.8 = bf16[1024,5632]{1,0:T(8,128)(2,1)} custom-call(s32[1]{0:T(128)} %bitcast.6.side_ref, bf16[768,2048]{1,0:T(8,128)(2,1)} %get-tuple-element.75.x_ref.ao_ref, bf16[768,2048]{1,0:T(8,128)(2,1)} %collective-permute-done.4.ap_ref, bf16[768,5632]{1,0:T(8,128)(2,1)} %get-tuple-element.89.b_ref.bo_ref, bf16[768,5632]{1,0:T(8,128)(2,1)} %collective-permute-done.8.bp_ref), custom_call_target="tpu_custom_call" | custom-call | flops 17716740096 | bytes 35127296 | tf_op jit(solution)/shard_map/weight_grad/pallas_call | solution.py:467
  655.4 11.4 reduce-scatter.8.cloned.1.call-done
  668.6 1.8 collective-permute-start.10
  670.4 6.9 all-reduce.7.cloned.1.call-done
  677.8 3.7 add_convert_fusion.1
  681.9 12.7 %weight_grad.9.refs_0_ = bf16[1024,4096]{1,0:T(8,128)(2,1)} custom-call(s32[1]{0:T(128)} %bitcast.6.side_ref, bf16[768,2048]{1,0:T(8,128)(2,1)} %get-tuple-element.74.a_ref.ao_ref, bf16[768,2048]{1,0:T(8,128)(2,1)} %collective-permute-done.12.ap_ref, bf16[768,2048]{1,0:T(8,128)(2,1)} %get-tuple-element.97.bo_ref, ...), custom_call_target="tpu_custom_call" | custom-call | flops 6442450944 | bytes 16777216 | tf_op jit(solution)/shard_map/weight_grad/pallas_call | solution.py:467
  694.5 12.6 %weight_grad.10 = bf16[1024,4096]{1,0:T(8,128)(2,1)} custom-call(s32[1]{0:T(128)} %bitcast.6.side_ref, bf16[768,2048]{1,0:T(8,128)(2,1)} %multiply_convert_fusion.1.x_ref.ao_ref, bf16[768,2048]{1,0:T(8,128)(2,1)} %collective-permute-done.9.ap_ref, bf16[768,2048]{1,0:T(8,128)(2,1)} %get-tuple-element.95.bo_ref.q_ref, ...), custom_call_target="tpu_custom_call", output_to_operand_aliasing={{}: (5, {})} | custom-call | flops 6442450944 | bytes 16777216 | tf_op jit(solution)/shard_map/weight_grad/pallas_call | solution.py:467
  707.1 64.3 %reduce-scatter.10.cloned.1.call-done = bf16[256,5632]{1,0:T(8,128)(2,1)} async-done(((bf16[1024,5632]{1,0:T(8,128)(2,1)}), bf16[256,5632]{1,0:T(8,128)(2,1)}) %reduce-scatter.10.cloned.1.call-update) | async-done | bytes 2883600 | tf_op jit(solution)/shard_map/reduce_scatter | solution.py:530
  772.4 1.8 add_convert_fusion
  774.8 52.1 %all-reduce.9.cloned.1.call-done = bf16[256,5632]{1,0:T(8,128)(2,1)} async-done(((bf16[256,5632]{1,0:T(8,128)(2,1)}), bf16[256,5632]{1,0:T(8,128)(2,1)}) %all-reduce.9.cloned.1.call-update) | async-done | bytes 2883600 | tf_op jit(solution)/shard_map/psum | solution.py:535
  826.9 26.2 %collective-permute-start.17 = (bf16[128,5632]{1,0:T(8,128)(2,1)S(1)}, bf16[128,5632]{1,0:T(8,128)(2,1)}, u32[]{:S(2)}, u32[]{:S(2)}) collective-permute-start(bf16[128,5632]{1,0:T(8,128)(2,1)S(1)} %get-tuple-element.100), channel_id=1, source_target_pairs={{0,1},{3,2},{4,5},{7,6},{8,9},{11,10},{12,13},{15,14},{16,17},{19,... | collective-permute-start | bytes 4325384 | tf_op jit(solution)/shard_map/ppermute | solution.py:564
  853.1 24.8 %down_matmul.1 = bf16[768,2048]{1,0:T(8,128)(2,1)} custom-call(bf16[768,5632]{1,0:T(8,128)(2,1)} %get-tuple-element.101.bo_ref.h_ref, bf16[8,5632,256]{2,1,0:T(8,128)(2,1)} %bitcast.57, f32[768,2048]{1,0:T(8,128)} %get-tuple-element.86.m_ref, f32[768,1]{1,0:T(8,128)} %bitcast.48), custom_call_target="tpu_custom_call" | custom-call | flops 17716740096 | bytes 31719424 | tf_op jit(solution)/shard_map/down_matmul/pallas_call | solution.py:285
  878.0 5.2 collective-permute-done.17
  884.9 4.6 collective-permute-start.19
  892.9 28.5 %collective-permute-done.19 = bf16[128,5632]{1,0:T(8,128)(2,1)S(1)} collective-permute-done((bf16[128,5632]{1,0:T(8,128)(2,1)S(1)}, bf16[128,5632]{1,0:T(8,128)(2,1)S(1)}, u32[]{:S(2)}, u32[]{:S(2)}) %collective-permute-start.19) | collective-permute-done | bytes 1441824 | tf_op jit(solution)/shard_map/ppermute | solution.py:564
  924.4 3.1 fusion.10
  927.5 39.3 %collective-permute-start.22 = (bf16[128,4096]{1,0:T(8,128)(2,1)}, bf16[128,4096]{1,0:T(8,128)(2,1)}, u32[]{:S(2)}, u32[]{:S(2)}) collective-permute-start(bf16[128,4096]{1,0:T(8,128)(2,1)} %get-tuple-element.109), channel_id=1, source_target_pairs={{0,1},{3,2},{4,5},{7,6},{8,9},{11,10},{12,13},{15,14},{16,17},{19,... | collective-permute-start | bytes 3145736 | tf_op jit(solution)/shard_map/ppermute | solution.py:564
  969.7 3.4 convert_add_fusion
  974.6 12.3 %collective-permute-done.22 = bf16[128,4096]{1,0:T(8,128)(2,1)} collective-permute-done((bf16[128,4096]{1,0:T(8,128)(2,1)}, bf16[128,4096]{1,0:T(8,128)(2,1)}, u32[]{:S(2)}, u32[]{:S(2)}) %collective-permute-start.22) | collective-permute-done | bytes 1048608 | tf_op jit(solution)/shard_map/ppermute | solution.py:564
  986.9 2.8 add_convert_fusion.9
  989.7 3.2 add_convert_fusion.2
  992.9 13.6 %collective-permute-done.20 = bf16[128,5632]{1,0:T(8,128)(2,1)S(1)} collective-permute-done((bf16[128,5632]{1,0:T(8,128)(2,1)S(1)}, bf16[128,5632]{1,0:T(8,128)(2,1)S(1)}, u32[]{:S(2)}, u32[]{:S(2)}) %collective-permute-start.20) | collective-permute-done | bytes 1441824 | tf_op jit(solution)/shard_map/ppermute | solution.py:564
  1010.1 2.7 reshape.170
  1012.8 1.8 broadcast_multiply_fusion
  1018.2 2.1 copy-done.12
  1020.3 3.2 convert_bitcast_fusion
  1024.7 8.8 weight_grad.11
  1033.4 19.8 %input_back.1 = (bf16[768,2048]{1,0:T(8,128)(2,1)}, f32[1,2048]{1,0:T(1,128)}) custom-call(bf16[768,2048]{1,0:T(8,128)(2,1)} %get-tuple-element.95.bo_ref.q_ref, bf16[768,1024]{1,0:T(8,128)(2,1)} %copy-done.3, bf16[2048,5120]{1,0:T(8,128)(2,1)} %all-gather.5.cloned.1.call-done.w_ref.wq_ref.wkv_ref, ...), custom_call_target="tpu_custom_call" | custom-call | flops 9663676416 | bytes 28311552 | tf_op jit(solution)/shard_map/input_back/pallas_call | solution.py:426
  1056.2 3.4 fusion.1
  1063.5 20.5 %collective-permute-done.26 = bf16[128,4096]{1,0:T(8,128)(2,1)S(1)} collective-permute-done((bf16[128,4096]{1,0:T(8,128)(2,1)S(1)}, bf16[128,4096]{1,0:T(8,128)(2,1)S(1)}, u32[]{:S(2)}, u32[]{:S(2)}) %collective-permute-start.26) | collective-permute-done | bytes 1048608 | tf_op jit(solution)/shard_map/ppermute | solution.py:564
  1086.5 10.9 collective-permute-done.24
  1101.7 6.2 copy.36
  1107.9 5.1 convert_element_type.233
  1114.9 24.2 %collective-permute-done.28 = bf16[128,4096]{1,0:T(8,128)(2,1)S(1)} collective-permute-done((bf16[128,4096]{1,0:T(8,128)(2,1)S(1)}, bf16[128,4096]{1,0:T(8,128)(2,1)S(1)}, u32[]{:S(2)}, u32[]{:S(2)}) %collective-permute-start.28) | collective-permute-done | bytes 1048608 | tf_op jit(solution)/shard_map/ppermute | solution.py:564
  1141.3 3.2 maximum_convert_fusion
  1144.8 20.3 %collective-permute-done.31 = bf16[128,4096]{1,0:T(8,128)(2,1)S(1)} collective-permute-done((bf16[128,4096]{1,0:T(8,128)(2,1)S(1)}, bf16[128,4096]{1,0:T(8,128)(2,1)S(1)}, u32[]{:S(2)}, u32[]{:S(2)}) %collective-permute-start.31) | collective-permute-done | bytes 1048608 | tf_op jit(solution)/shard_map/ppermute | solution.py:564
  1166.5 2.5 slice_convert_fusion.1
  1169.1 10.4 collective-permute-done.33
  (202 shorter events, 61.2 us)
Async XLA Ops:
  8.0 113.6 %all-gather.5.cloned.1.call-start = ((), (), s32[]{:S(2)}) async-start(), calls=%async_computation.5 | async-start | bytes 23592960 | tf_op jit(solution)/shard_map/all_gather | solution.py:524
  11.2 327.6 %all-gather.7.cloned.1.call-start = ((), (), s32[]{:S(2)}) async-start(), calls=%async_computation.6 | async-start | bytes 51904512 | tf_op jit(solution)/shard_map/all_gather | solution.py:524
  16.3 105.4 %copy-start.24 = (s32[3,256]{1,0:T(4,128)S(1)}, s32[3,256]{1,0:T(4,128)}, u32[]{:S(2)}) copy-start(s32[3,256]{1,0:T(4,128)} %param.16) | copy-start | bytes 9220
  16.3 105.4 %copy-start.29 = (bf16[256]{0:T(256)(128)(2,1)S(1)}, bf16[256]{0:T(256)(128)(2,1)}, u32[]{:S(2)}) copy-start(bf16[256]{0:T(256)(128)(2,1)} %param.19) | copy-start | bytes 1540
  16.4 105.4 %copy-start.30 = (bf16[256]{0:T(256)(128)(2,1)S(1)}, bf16[256]{0:T(256)(128)(2,1)}, u32[]{:S(2)}) copy-start(bf16[256]{0:T(256)(128)(2,1)} %param.24) | copy-start | bytes 1540
  16.4 105.4 %copy-start = (bf16[3,256,2048]{2,1,0:T(8,128)(2,1)S(1)}, bf16[3,256,2048]{2,1,0:T(8,128)(2,1)}, u32[]{:S(2)}) copy-start(bf16[3,256,2048]{2,1,0:T(8,128)(2,1)} %param.14) | copy-start | bytes 9437188
  121.7 335.6 %all-gather.9.cloned.1.call-start = ((), (), s32[]{:S(2)}) async-start(), calls=%async_computation.15 | async-start | bytes 25952256 | tf_op jit(solution)/shard_map/all_gather | solution.py:524
  137.2 62.7 %copy-start.22 = (s32[3,1024]{1,0:T(4,128)S(1)}, s32[3,1024]{1,0:T(4,128)}, u32[]{:S(2)}) copy-start(s32[3,1024]{1,0:T(4,128)} %param.17) | copy-start | bytes 36868
  137.2 64.0 %copy-start.31 = (s32[3]{0:T(128)S(1)}, s32[3]{0:T(128)}, u32[]{:S(2)}) copy-start(s32[3]{0:T(128)} %param.18) | copy-start | bytes 40
  155.5 37.9 %collective-permute-start = (bf16[768,1024]{1,0:T(8,128)(2,1)}, bf16[768,1024]{1,0:T(8,128)(2,1)S(1)}, u32[]{:S(2)}, u32[]{:S(2)}) collective-permute-start(bf16[768,1024]{1,0:T(8,128)(2,1)} %get-tuple-element.73.refs_0_.refs_4_), channel_id=1, source_target_pairs={{0,1},{1,2},{2,3},{4,5},{5,6},{6,7},{8,9},{9,10},{10,11},{12,13},{... | collective-permute-start | bytes 4718600 | tf_op jit(solution)/shard_map/ppermute | solution.py:581
  194.5 3.2 collective-permute-start.1
  196.3 41.1 %collective-permute-start.3 = (bf16[768,1024]{1,0:T(8,128)(2,1)}, bf16[768,1024]{1,0:T(8,128)(2,1)S(1)}, u32[]{:S(2)}, u32[]{:S(2)}) collective-permute-start(bf16[768,1024]{1,0:T(8,128)(2,1)} %get-tuple-element.73.refs_0_.refs_4_), channel_id=1, source_target_pairs={{1,0},{2,1},{3,2},{5,4},{6,5},{7,6},{9,8},{10,9},{11,10},{13,12},{... | collective-permute-start | bytes 4718600 | tf_op jit(solution)/shard_map/ppermute | solution.py:585
  197.6 39.8 %collective-permute-start.2 = (bf16[768,1024]{1,0:T(8,128)(2,1)}, bf16[768,1024]{1,0:T(8,128)(2,1)}, u32[]{:S(2)}, u32[]{:S(2)}) collective-permute-start(bf16[768,1024]{1,0:T(8,128)(2,1)} %collective-permute-done.1.refs_2_.refs_6_), channel_id=1, source_target_pairs={{2,3},{6,7},{10,11},{14,15},{18,19},{22,23},{26,27},{30,31}} | collective-permute-start | bytes 4718600 | tf_op jit(solution)/shard_map/ppermute | solution.py:581
  338.8 223.2 %reduce-scatter.6.cloned.1.call-start = ((), (), s32[]{:S(2)}) async-start(), calls=%async_computation.7 | async-start | bytes 14417920 | tf_op jit(solution)/shard_map/reduce_scatter | solution.py:530
  363.3 27.9 %copy-start.1 = (bf16[3,256,2048]{2,1,0:T(8,128)(2,1)S(1)}, bf16[3,256,2048]{2,1,0:T(8,128)(2,1)}, u32[]{:S(2)}) copy-start(bf16[3,256,2048]{2,1,0:T(8,128)(2,1)} %param.15) | copy-start | bytes 9437188
  390.8 27.2 %collective-permute-start.6 = (bf16[768,5632]{1,0:T(8,128)(2,1)}, bf16[768,5632]{1,0:T(8,128)(2,1)}, u32[]{:S(2)}, u32[]{:S(2)}) collective-permute-start(bf16[768,5632]{1,0:T(8,128)(2,1)} %get-tuple-element.101.bo_ref.h_ref), channel_id=1, source_target_pairs={{0,4},{4,0},{8,12},{12,8},{16,20},{20,16},{24,28},{28,24},{1,5},{5... | collective-permute-start | bytes 25952264 | tf_op jit(solution)/shard_map/ppermute | solution.py:527
  393.9 14.9 %collective-permute-start.5 = (bf16[768,2048]{1,0:T(8,128)(2,1)}, bf16[768,2048]{1,0:T(8,128)(2,1)S(1)}, u32[]{:S(2)}, u32[]{:S(2)}) collective-permute-start(bf16[768,2048]{1,0:T(8,128)(2,1)} %multiply_convert_fusion.ao_ref.m_ref), channel_id=1, source_target_pairs={{0,4},{4,0},{8,12},{12,8},{16,20},{20,16},{24,28},{28,24},{1,5},{5... | collective-permute-start | bytes 9437192 | tf_op jit(solution)/shard_map/ppermute | solution.py:527
  408.7 9.3 copy-start.26
  443.2 118.9 %all-reduce.5.cloned.1.call-start = ((), (), s32[]{:S(2)}) async-start(), calls=%async_computation.10 | async-start | bytes 524288 | tf_op jit(solution)/shard_map/psum | solution.py:535
  457.2 31.6 %copy-start.25 = (bf16[768,2048]{1,0:T(8,128)(2,1)S(1)}, bf16[768,2048]{1,0:T(8,128)(2,1)}, u32[]{:S(2)}) copy-start(bf16[768,2048]{1,0:T(8,128)(2,1)} %get-tuple-element.75.x_ref.ao_ref) | copy-start | bytes 9437188
  488.5 46.9 %collective-permute-start.7 = (bf16[768,5632]{1,0:T(8,128)(2,1)}, bf16[768,5632]{1,0:T(8,128)(2,1)}, u32[]{:S(2)}, u32[]{:S(2)}) collective-permute-start(bf16[768,5632]{1,0:T(8,128)(2,1)} %get-tuple-element.84.a_ref.bo_ref), channel_id=1, source_target_pairs={{0,4},{4,0},{8,12},{12,8},{16,20},{20,16},{24,28},{28,24},{1,5},{5... | collective-permute-start | bytes 25952264 | tf_op jit(solution)/shard_map/ppermute | solution.py:527
  488.8 177.9 %reduce-scatter.8.cloned.1.call-start = ((), (), s32[]{:S(2)}) async-start(), calls=%async_computation.8 | async-start | bytes 14417920 | tf_op jit(solution)/shard_map/reduce_scatter | solution.py:530
  488.8 46.5 %collective-permute-start.4 = (bf16[768,2048]{1,0:T(8,128)(2,1)S(1)}, bf16[768,2048]{1,0:T(8,128)(2,1)}, u32[]{:S(2)}, u32[]{:S(2)}) collective-permute-start(bf16[768,2048]{1,0:T(8,128)(2,1)S(1)} %copy-done.25), channel_id=1, source_target_pairs={{0,4},{4,0},{8,12},{12,8},{16,20},{20,16},{24,28},{28,24},{1,5},{5... | collective-permute-start | bytes 9437192 | tf_op jit(solution)/shard_map/ppermute | solution.py:527
  562.0 115.3 %all-reduce.7.cloned.1.call-start = ((), (), s32[]{:S(2)}) async-start(), calls=%async_computation.11 | async-start | bytes 5767168 | tf_op jit(solution)/shard_map/psum | solution.py:535
  562.1 68.0 %collective-permute-start.8 = (bf16[768,5632]{1,0:T(8,128)(2,1)}, bf16[768,5632]{1,0:T(8,128)(2,1)}, u32[]{:S(2)}, u32[]{:S(2)}) collective-permute-start(bf16[768,5632]{1,0:T(8,128)(2,1)} %get-tuple-element.89.b_ref.bo_ref), channel_id=1, source_target_pairs={{0,4},{4,0},{8,12},{12,8},{16,20},{20,16},{24,28},{28,24},{1,5},{5... | collective-permute-start | bytes 25952264 | tf_op jit(solution)/shard_map/ppermute | solution.py:527
  562.6 208.9 %reduce-scatter.10.cloned.1.call-start = ((), (), s32[]{:S(2)}) async-start(), calls=%async_computation.9 | async-start | bytes 14417920 | tf_op jit(solution)/shard_map/reduce_scatter | solution.py:530
  666.7 160.2 %all-reduce.9.cloned.1.call-start = ((), (), s32[]{:S(2)}) async-start(), calls=%async_computation.12 | async-start | bytes 5767168 | tf_op jit(solution)/shard_map/psum | solution.py:535
  666.8 14.8 %collective-permute-start.12 = (bf16[768,2048]{1,0:T(8,128)(2,1)}, bf16[768,2048]{1,0:T(8,128)(2,1)}, u32[]{:S(2)}, u32[]{:S(2)}) collective-permute-start(bf16[768,2048]{1,0:T(8,128)(2,1)} %get-tuple-element.74.a_ref.ao_ref), channel_id=1, source_target_pairs={{0,4},{4,0},{8,12},{12,8},{16,20},{20,16},{24,28},{28,24},{1,5},{5... | collective-permute-start | bytes 9437192 | tf_op jit(solution)/shard_map/ppermute | solution.py:527
  666.9 15.0 %collective-permute-start.13 = (bf16[768,2048]{1,0:T(8,128)(2,1)}, bf16[768,2048]{1,0:T(8,128)(2,1)}, u32[]{:S(2)}, u32[]{:S(2)}) collective-permute-start(bf16[768,2048]{1,0:T(8,128)(2,1)} %get-tuple-element.97.bo_ref), channel_id=1, source_target_pairs={{0,4},{4,0},{8,12},{12,8},{16,20},{20,16},{24,28},{28,24},{1,5},{5... | collective-permute-start | bytes 9437192 | tf_op jit(solution)/shard_map/ppermute | solution.py:527
  667.4 27.2 %collective-permute-start.9 = (bf16[768,2048]{1,0:T(8,128)(2,1)}, bf16[768,2048]{1,0:T(8,128)(2,1)}, u32[]{:S(2)}, u32[]{:S(2)}) collective-permute-start(bf16[768,2048]{1,0:T(8,128)(2,1)} %multiply_convert_fusion.1.x_ref.ao_ref), channel_id=1, source_target_pairs={{0,4},{4,0},{8,12},{12,8},{16,20},{20,16},{24,28},{28,24},{1,5},{5... | collective-permute-start | bytes 9437192 | tf_op jit(solution)/shard_map/ppermute | solution.py:527
  668.6 25.9 %collective-permute-start.11 = (bf16[768,2048]{1,0:T(8,128)(2,1)S(1)}, bf16[768,2048]{1,0:T(8,128)(2,1)}, u32[]{:S(2)}, u32[]{:S(2)}) collective-permute-start(bf16[768,2048]{1,0:T(8,128)(2,1)S(1)} %copy-done.2), channel_id=1, source_target_pairs={{0,4},{4,0},{8,12},{12,8},{16,20},{20,16},{24,28},{28,24},{1,5},{5... | collective-permute-start | bytes 9437192 | tf_op jit(solution)/shard_map/ppermute | solution.py:527
  668.6 9.2 collective-permute-start.10
  677.4 247.0 %reduce-scatter.12.cloned.1.call-start = ((), (), s32[]{:S(2)}) async-start(), calls=%async_computation.13 | async-start | bytes 10485760 | tf_op jit(solution)/shard_map/reduce_scatter | solution.py:530
  707.1 64.4 %copy-start.16 = (bf16[768,1024]{1,0:T(8,128)(2,1)S(1)}, bf16[768,1024]{1,0:T(8,128)(2,1)}, u32[]{:S(2)}) copy-start(bf16[768,1024]{1,0:T(8,128)(2,1)} %add_convert_fusion.1) | copy-start | bytes 4718596
  707.1 65.2 %copy-start.15 = (bf16[768,1024]{1,0:T(8,128)(2,1)S(1)}, bf16[768,1024]{1,0:T(8,128)(2,1)}, u32[]{:S(2)}) copy-start(bf16[768,1024]{1,0:T(8,128)(2,1)} %get-tuple-element.98) | copy-start | bytes 4718596
  771.5 326.1 %reduce-scatter.14.cloned.1.call-start = ((), (), s32[]{:S(2)}) async-start(), calls=%async_computation.14 | async-start | bytes 2949120 | tf_op jit(solution)/shard_map/reduce_scatter | solution.py:530
  771.6 0.8 collective-permute-start.14
  826.9 56.3 %collective-permute-start.17 = (bf16[128,5632]{1,0:T(8,128)(2,1)S(1)}, bf16[128,5632]{1,0:T(8,128)(2,1)}, u32[]{:S(2)}, u32[]{:S(2)}) collective-permute-start(bf16[128,5632]{1,0:T(8,128)(2,1)S(1)} %get-tuple-element.100), channel_id=1, source_target_pairs={{0,1},{3,2},{4,5},{7,6},{8,9},{11,10},{12,13},{15,14},{16,17},{19,... | collective-permute-start | bytes 4325384 | tf_op jit(solution)/shard_map/ppermute | solution.py:564
  884.9 36.5 %collective-permute-start.19 = (bf16[128,5632]{1,0:T(8,128)(2,1)S(1)}, bf16[128,5632]{1,0:T(8,128)(2,1)S(1)}, u32[]{:S(2)}, u32[]{:S(2)}) collective-permute-start(bf16[128,5632]{1,0:T(8,128)(2,1)S(1)} %get-tuple-element.105), channel_id=1, source_target_pairs={{0,1},{3,2},{4,5},{7,6},{8,9},{11,10},{12,13},{15,14},{16,17},{19,... | collective-permute-start | bytes 4325384 | tf_op jit(solution)/shard_map/ppermute | solution.py:564
  889.5 79.0 %collective-permute-start.15 = (bf16[768,1024]{1,0:T(8,128)(2,1)}, bf16[768,1024]{1,0:T(8,128)(2,1)S(1)}, u32[]{:S(2)}, u32[]{:S(2)}) collective-permute-start(bf16[768,1024]{1,0:T(8,128)(2,1)} %get-tuple-element.94), channel_id=1, source_target_pairs={{0,1},{1,2},{2,3},{4,5},{5,6},{6,7},{8,9},{9,10},{10,11},{12,13},{... | collective-permute-start | bytes 4718600 | tf_op jit(solution)/shard_map/ppermute | solution.py:592
  890.9 77.6 %collective-permute-start.16 = (bf16[768,1024]{1,0:T(8,128)(2,1)}, bf16[768,1024]{1,0:T(8,128)(2,1)}, u32[]{:S(2)}, u32[]{:S(2)}) collective-permute-start(bf16[768,1024]{1,0:T(8,128)(2,1)} %add_convert_fusion), channel_id=1, source_target_pairs={{1,0},{2,1},{3,2},{5,4},{6,5},{7,6},{9,8},{10,9},{11,10},{13,12},{... | collective-permute-start | bytes 4718600 | tf_op jit(solution)/shard_map/ppermute | solution.py:597
  892.2 30.8 %collective-permute-start.18 = (bf16[128,5632]{1,0:T(8,128)(2,1)S(1)}, bf16[128,5632]{1,0:T(8,128)(2,1)S(1)}, u32[]{:S(2)}, u32[]{:S(2)}) collective-permute-start(bf16[128,5632]{1,0:T(8,128)(2,1)S(1)} %add_convert_fusion.5), channel_id=1, source_target_pairs={{1,2},{2,1},{5,6},{6,5},{9,10},{10,9},{13,14},{14,13},{17,18},{18,... | collective-permute-start | bytes 4325384 | tf_op jit(solution)/shard_map/ppermute | solution.py:564
  927.5 59.5 %collective-permute-start.22 = (bf16[128,4096]{1,0:T(8,128)(2,1)}, bf16[128,4096]{1,0:T(8,128)(2,1)}, u32[]{:S(2)}, u32[]{:S(2)}) collective-permute-start(bf16[128,4096]{1,0:T(8,128)(2,1)} %get-tuple-element.109), channel_id=1, source_target_pairs={{0,1},{3,2},{4,5},{7,6},{8,9},{11,10},{12,13},{15,14},{16,17},{19,... | collective-permute-start | bytes 3145736 | tf_op jit(solution)/shard_map/ppermute | solution.py:564
  966.8 22.9 %collective-permute-start.21 = (bf16[128,5632]{1,0:T(8,128)(2,1)}, bf16[128,5632]{1,0:T(8,128)(2,1)}, u32[]{:S(2)}, u32[]{:S(2)}) collective-permute-start(bf16[128,5632]{1,0:T(8,128)(2,1)} %add_convert_fusion.3), channel_id=1, source_target_pairs={{1,2},{2,1},{5,6},{6,5},{9,10},{10,9},{13,14},{14,13},{17,18},{18,... | collective-permute-start | bytes 4325384 | tf_op jit(solution)/shard_map/ppermute | solution.py:564
  969.7 3.5 copy-start.5
  973.1 33.4 %collective-permute-start.20 = (bf16[128,5632]{1,0:T(8,128)(2,1)S(1)}, bf16[128,5632]{1,0:T(8,128)(2,1)S(1)}, u32[]{:S(2)}, u32[]{:S(2)}) collective-permute-start(bf16[128,5632]{1,0:T(8,128)(2,1)S(1)} %copy-done.5), channel_id=1, source_target_pairs={{1,0},{2,3},{5,4},{6,7},{9,8},{10,11},{13,12},{14,15},{17,16},{18,... | collective-permute-start | bytes 4325384 | tf_op jit(solution)/shard_map/ppermute | solution.py:564
  1009.1 3.7 copy-start.17
  1018.1 5.4 copy-start.3
  1018.2 5.4 collective-permute-start.23
  1033.4 19.8 %copy-start.23 = (f32[1,2048]{1,0:T(1,128)S(1)}, f32[1,2048]{1,0:T(1,128)}, u32[]{:S(2)}) copy-start(f32[1,2048]{1,0:T(1,128)} %get-tuple-element.121) | copy-start | bytes 24580
  1053.9 1.2 collective-permute-start.27
  1056.2 5.0 copy-start.7
  1059.6 24.4 %collective-permute-start.26 = (bf16[128,4096]{1,0:T(8,128)(2,1)S(1)}, bf16[128,4096]{1,0:T(8,128)(2,1)S(1)}, u32[]{:S(2)}, u32[]{:S(2)}) collective-permute-start(bf16[128,4096]{1,0:T(8,128)(2,1)S(1)} %copy-done.10), channel_id=1, source_target_pairs={{0,1},{3,2},{4,5},{7,6},{8,9},{11,10},{12,13},{15,14},{16,17},{19,... | collective-permute-start | bytes 3145736 | tf_op jit(solution)/shard_map/ppermute | solution.py:564
  1061.3 24.0 %collective-permute-start.25 = (bf16[128,4096]{1,0:T(8,128)(2,1)S(1)}, bf16[128,4096]{1,0:T(8,128)(2,1)S(1)}, u32[]{:S(2)}, u32[]{:S(2)}) collective-permute-start(bf16[128,4096]{1,0:T(8,128)(2,1)S(1)} %copy-done.7), channel_id=1, source_target_pairs={{1,2},{2,1},{5,6},{6,5},{9,10},{10,9},{13,14},{14,13},{17,18},{18,... | collective-permute-start | bytes 3145736 | tf_op jit(solution)/shard_map/ppermute | solution.py:564
  1062.0 35.4 %collective-permute-start.24 = (bf16[128,5632]{1,0:T(8,128)(2,1)S(1)}, bf16[128,5632]{1,0:T(8,128)(2,1)S(1)}, u32[]{:S(2)}, u32[]{:S(2)}) collective-permute-start(bf16[128,5632]{1,0:T(8,128)(2,1)S(1)} %copy-done.4), channel_id=1, source_target_pairs={{1,0},{2,3},{5,4},{6,7},{9,8},{10,11},{13,12},{14,15},{17,16},{18,... | collective-permute-start | bytes 4325384 | tf_op jit(solution)/shard_map/ppermute | solution.py:564
  1097.6 16.9 %collective-permute-start.30 = (bf16[256,1152]{1,0:T(8,128)(2,1)}, bf16[256,1152]{1,0:T(8,128)(2,1)S(1)}, u32[]{:S(2)}, u32[]{:S(2)}) collective-permute-start(bf16[256,1152]{1,0:T(8,128)(2,1)} %reduce-scatter.14.cloned.1.call-done), channel_id=1, source_target_pairs={{0,1},{3,2},{4,5},{7,6},{8,9},{11,10},{12,13},{15,14},{16,17},{19,... | collective-permute-start | bytes 1769480 | tf_op jit(solution)/shard_map/ppermute | solution.py:564
  1099.1 15.5 %collective-permute-start.29 = (bf16[128,4096]{1,0:T(8,128)(2,1)}, bf16[128,4096]{1,0:T(8,128)(2,1)S(1)}, u32[]{:S(2)}, u32[]{:S(2)}) collective-permute-start(bf16[128,4096]{1,0:T(8,128)(2,1)} %add_convert_fusion.7), channel_id=1, source_target_pairs={{1,2},{2,1},{5,6},{6,5},{9,10},{10,9},{13,14},{14,13},{17,18},{18,... | collective-permute-start | bytes 3145736 | tf_op jit(solution)/shard_map/ppermute | solution.py:564
  1107.9 5.1 copy-start.9
  1107.9 6.6 copy-start.20
  1113.1 26.1 %collective-permute-start.28 = (bf16[128,4096]{1,0:T(8,128)(2,1)S(1)}, bf16[128,4096]{1,0:T(8,128)(2,1)S(1)}, u32[]{:S(2)}, u32[]{:S(2)}) collective-permute-start(bf16[128,4096]{1,0:T(8,128)(2,1)S(1)} %copy-done.9), channel_id=1, source_target_pairs={{1,0},{2,3},{5,4},{6,7},{9,8},{10,11},{13,12},{14,15},{17,16},{18,... | collective-permute-start | bytes 3145736 | tf_op jit(solution)/shard_map/ppermute | solution.py:564
  1114.9 26.4 %copy-start.6 = (bf16[128,5632]{1,0:T(8,128)(2,1)S(1)}, bf16[128,5632]{1,0:T(8,128)(2,1)}, u32[]{:S(2)}) copy-start(bf16[128,5632]{1,0:T(8,128)(2,1)} %broadcast_select_fusion.2) | copy-start | bytes 4325380
  1139.3 5.3 collective-permute-start.32
  1140.0 25.1 %collective-permute-start.31 = (bf16[128,4096]{1,0:T(8,128)(2,1)S(1)}, bf16[128,4096]{1,0:T(8,128)(2,1)S(1)}, u32[]{:S(2)}, u32[]{:S(2)}) collective-permute-start(bf16[128,4096]{1,0:T(8,128)(2,1)S(1)} %add_convert_fusion.6), channel_id=1, source_target_pairs={{1,0},{2,3},{5,4},{6,7},{9,8},{10,11},{13,12},{14,15},{17,16},{18,... | collective-permute-start | bytes 3145736 | tf_op jit(solution)/shard_map/ppermute | solution.py:564
  1165.2 14.3 %collective-permute-start.33 = (bf16[256,1152]{1,0:T(8,128)(2,1)S(1)}, bf16[256,1152]{1,0:T(8,128)(2,1)S(1)}, u32[]{:S(2)}, u32[]{:S(2)}) collective-permute-start(bf16[256,1152]{1,0:T(8,128)(2,1)S(1)} %add_convert_fusion.10), channel_id=1, source_target_pairs={{1,0},{2,3},{5,4},{6,7},{9,8},{10,11},{13,12},{14,15},{17,16},{18,... | collective-permute-start | bytes 1769480 | tf_op jit(solution)/shard_map/ppermute | solution.py:564
  (13 other events, 25.3 us)
Sparse Core Ops, SparseCore 0:
  11.3 110.2 all-gather.4
  124.1 214.6 all-gather.6
  340.7 116.4 all-gather.8
  459.4 102.5 reduce-scatter.5
  564.2 102.4 reduce-scatter.7
  668.9 102.5 reduce-scatter.9
  773.8 76.9 reduce-scatter.11
  1059.7 26.4 reduce-scatter.13
Sparse Core Ops, SparseCore 1:
  488.9 35.8 all-reduce.4
  565.0 112.3 all-reduce.6
  679.7 147.1 all-reduce.8
